TPU v7x, 32 devices: a whole 2x2x4 slice. The times are simulated.
32 devices in a mesh: sub: 16 (over z, y, x), coarse: 2 (over core).
Axes of the slice: x: 2, y: 2, z: 4, core: 2. Of those that a mesh axis runs over, the one named last changes fastest.
Arguments:
- right_side: float32 [2, 256, 96], P('coarse', 'sub'), may hold values from -6 to 6
- blocks: float32 [2, 256, 6, 96, 96], P('coarse', 'sub')
- pattern: int32 [2, 256, 6], P('coarse', 'sub'), may hold values from 0 to 31, as said below
- send_rows: int32 [2, 64, 4], P('coarse', 'sub'), may hold values from 0 to 15, as said below
- inverse_blocks: float32 [2, 256, 96, 96], P('coarse', 'sub')
- margin_blocks: float32 [2, 256, 96, 96], P('coarse', 'sub')
- near_null: float32 [2, 256, 6, 96], P('coarse', 'sub'), may hold values from -0.625 to 0.625
- aggregate: int32 [2, 256], P('coarse', 'sub'), may hold values from 0 to 7
- coarse_inverse: float32 [16, 48, 48], P('sub')
Outputs:
- solution: float32 [2, 256, 96], P('coarse', 'sub')
- residual: float32 [2, 256, 96], P('coarse', 'sub')
Inputs may be any that keep to these rules, and one draw needn't show every extreme that they name: `pattern`: slot 0 of every block row names the row itself; in every other slot the rows of one subdomain name distinct extended rows. `send_rows`: the 4 rows one subdomain sends in one round are distinct.
All inputs are finite; a program needn't handle non-finite values.
Results may differ from a plain program's by a relative error of at most 0.0003.
Values sent between devices are 32-bit elements; how exact they have to be, the bound alone decides.
No kernel may reach another device: no remote copies, remote signals or barrier semaphores. Data moves between devices by JAX's collectives and lax.ppermute only.
A program may use at most 64 MiB of HBM per device.

v0:
```python
import jax
import jax.numpy as jnp
from jax import lax
from jax.sharding import PartitionSpec as P

ITERS = 3


highest = lax.Precision.HIGHEST


def partner(array, axis, bit):
    return lax.ppermute(array, axis, [(i, i ^ 1 << bit) for i in range(lax.axis_size(axis))])


def on_device(
    right_side,
    blocks,
    pattern,
    send_rows,
    inverse_blocks,
    margin_blocks,
    near_null,
    aggregate,
    coarse_inverse,
):
    source = right_side[0]
    matrix = blocks[0]
    columns = pattern[0]
    senders = send_rows[0]
    inverse = inverse_blocks[0]
    margin = margin_blocks[0]
    null_modes = near_null[0]
    groups_of = aggregate[0]
    coarse_inv = coarse_inverse[0]
    row_count = source.shape[0]
    width = source.shape[1]
    turns = senders.shape[0]
    ghost_count = senders.shape[1]
    extent = row_count + turns * ghost_count
    mode_count = null_modes.shape[1]
    group_count = coarse_inv.shape[0] // mode_count
    levels = lax.axis_size("sub").bit_length() - 1
    bit_list = [turn * levels // turns for turn in range(turns)]
    flat_senders = senders.reshape(-1)
    column_table = (
        columns.reshape(-1)[None, :] == jnp.arange(extent, dtype=jnp.int32)[:, None]
    ).astype(jnp.float32)
    sender_table = (
        jnp.arange(row_count, dtype=jnp.int32)[:, None] == flat_senders[None, :]
    ).astype(jnp.float32)
    group_table = (jnp.arange(group_count, dtype=jnp.int32)[:, None] == groups_of[None, :]).astype(
        jnp.float32
    )

    def coarse_term(residual):
        local = jnp.einsum("rmb,rb->rm", null_modes, residual, precision=highest)
        partial_sum = jnp.dot(group_table, local, precision=highest)
        total = lax.psum(partial_sum, "coarse")
        solved = jnp.dot(coarse_inv, total.reshape(-1), precision=highest).reshape(
            group_count, mode_count
        )
        per_row = jnp.dot(group_table.T, solved, precision=highest)
        return jnp.einsum("rmb,rm->rb", null_modes, per_row, precision=highest)

    def precondition(residual):
        result = jnp.einsum("rab,rb->ra", inverse, residual, precision=highest)
        backs = []
        for turn in range(turns):
            arrived = partner(residual[senders[turn]], "sub", bit_list[turn])
            local_term = jnp.einsum(
                "gab,gb->ga",
                margin[turn * ghost_count : (turn + 1) * ghost_count],
                arrived,
                precision=highest,
            )
            backs.append(partner(local_term, "sub", bit_list[turn]))
        terms = jnp.concatenate(backs, axis=0)
        return result + jnp.dot(sender_table, terms, precision=highest) + coarse_term(residual)

    def residual_dot(residual, precond):
        return lax.psum(jnp.sum(residual * precond), ("sub", "coarse"))

    solution = jnp.zeros_like(source)
    residual = source
    precond = precondition(residual)
    direction = precond
    product_now = residual_dot(residual, precond)
    for step in range(ITERS):
        transposed = jnp.einsum("rkab,ra->rkb", matrix, direction, precision=highest)
        spread = jnp.dot(column_table, transposed.reshape(-1, width), precision=highest)
        rims = []
        returned = []
        for operate_turn in range(turns):
            start = row_count + operate_turn * ghost_count
            packet = jnp.concatenate(
                [direction[senders[operate_turn]], spread[start : start + ghost_count]], axis=0
            )
            operate_arrived = partner(packet, "sub", bit_list[operate_turn])
            rims.append(operate_arrived[:ghost_count])
            returned.append(operate_arrived[ghost_count:])
        extended = jnp.concatenate([direction] + rims, axis=0)
        forward = jnp.einsum("rkab,rkb->ra", matrix, extended[columns], precision=highest)
        back_recv = jnp.dot(sender_table, jnp.concatenate(returned, axis=0), precision=highest)
        image = 0.5 * (forward + (spread[:row_count] + back_recv))
        alpha = product_now / lax.psum(jnp.sum(direction * image), ("sub", "coarse"))
        solution = solution + alpha * direction
        residual = residual - alpha * image
        if step + 1 < ITERS:
            precond = precondition(residual)
            product_next = residual_dot(residual, precond)
            direction = precond + product_next / product_now * direction
            product_now = product_next
    return (solution[None], residual[None])


def solution(mesh):
    in_specs = (
        P("coarse", "sub", None),
        P("coarse", "sub", None, None, None),
        P("coarse", "sub", None),
        P("coarse", "sub", None),
        P("coarse", "sub", None, None),
        P("coarse", "sub", None, None),
        P("coarse", "sub", None, None),
        P("coarse", "sub"),
        P("sub", None, None),
    )
    out_specs = (P("coarse", "sub", None), P("coarse", "sub", None))
    return jax.shard_map(
        on_device, mesh=mesh, in_specs=in_specs, out_specs=out_specs, check_vma=False
    )
```

profile of v0, /device:TPU:0, one launch (start us, length us, event | category | flops | bytes accessed | tf_op | source)
XLA Modules:
  0.0 355.7 jit_solution(15735029921158721290)
XLA Ops:
  1.5 1.3 gather_fusion
  2.7 3.0 collective-permute-start
  7.0 1.6 collective-permute-start.2
  9.9 1.6 collective-permute-start.4
  12.8 2.7 collective-permute-start.6
  17.3 2.5 psum.63
  23.0 2.0 fusion.22
  25.9 1.3 fusion.46
  27.8 1.3 fusion.40
  29.6 1.3 fusion.34
  31.4 1.3 fusion.28
  34.6 2.7 collective-permute-done.7
  39.7 4.7 %fusion.10 = f32[16,1,6,96]{3,1,2,0:T(1,128)S(1)} fusion(f32[16,96,1,1]{1,2,3,0:T(1,128)S(1)} %bitcast.263, f32[1,16,6,96,96]{4,3,2,1,0:T(8,128)} %param.10), kind=kOutput, calls=%fused_computation.37 | convolution fusion | flops 10616832 | bytes 3581952 | tf_op jit(solution)/shard_map/rkab,ra->rkb/dot_general | solution.py:90
  44.8 1.8 collective-permute-start.10
  46.6 1.5 collective-permute-start.9
  48.2 1.5 collective-permute-start.8
  50.2 1.5 collective-permute-done.8
  52.4 6.1 %fusion.8 = f32[16,1,96,1]{2,1,3,0:T(1,128)S(1)} fusion(f32[16,6,96,1]{2,3,1,0:T(1,128)S(1)} %bitcast.277, f32[1,16,6,96,96]{4,3,2,1,0:T(8,128)} %param.10), kind=kOutput, calls=%fused_computation.35 | convolution fusion | flops 10616832 | bytes 3581952 | tf_op jit(solution)/shard_map/rkab,rkb->ra/dot_general | solution.py:103
  59.3 39.7 %all-reduce = (f32[]{:T(128)}, f32[]{:T(128)}) all-reduce(f32[]{:T(128)} %get-tuple-element.3, f32[]{:T(128)} %get-tuple-element.2), channel_id=1, replica_groups=mesh['sub'=16,'coarse'=2] {'sub','coarse'}, use_global_device_ids=true, to_apply=%region_2.0 | all-reduce | flops 2 | bytes 16 | tf_op jit(solution)/shard_map/psum | solution.py:82
  101.2 1.3 fusion.20
  102.7 2.6 psum.66
  105.9 2.3 collective-permute-start.12
  110.1 1.7 collective-permute-start.14
  112.3 2.4 collective-permute-start.18
  117.4 2.2 collective-permute-start.19
  120.2 1.8 collective-permute-done.19
  122.7 40.9 %psum.67 = f32[]{:T(128)} all-reduce(f32[]{:T(128)} %get-tuple-element.47), channel_id=1, replica_groups=mesh['sub'=16,'coarse'=2] {'sub','coarse'}, use_global_device_ids=true, to_apply=%region_7.0 | all-reduce | flops 1 | bytes 8 | tf_op jit(solution)/shard_map/psum | solution.py:82
  167.2 4.7 %fusion.6 = f32[16,1,6,96]{3,1,2,0:T(1,128)S(1)} fusion(f32[16,96,1,1]{1,2,3,0:T(1,128)S(1)} %bitcast.264, f32[1,16,6,96,96]{4,3,2,1,0:T(8,128)} %param.10), kind=kOutput, calls=%fused_computation.33 | convolution fusion | flops 10616832 | bytes 3581952 | tf_op jit(solution)/shard_map/rkab,ra->rkb/dot_general | solution.py:90
  172.6 1.6 collective-permute-start.22
  174.2 2.5 collective-permute-start.21
  178.3 2.0 collective-permute-done.20
  181.0 6.1 %fusion.4 = f32[16,1,96,1]{2,1,3,0:T(1,128)S(1)} fusion(f32[16,6,96,1]{2,3,1,0:T(1,128)S(1)} %bitcast.278, f32[1,16,6,96,96]{4,3,2,1,0:T(8,128)} %param.10), kind=kOutput, calls=%fused_computation.31 | convolution fusion | flops 10616832 | bytes 3581952 | tf_op jit(solution)/shard_map/rkab,rkb->ra/dot_general | solution.py:103
  187.8 38.3 %psum.68 = f32[]{:T(128)} all-reduce(f32[]{:T(128)} %get-tuple-element.49), channel_id=1, replica_groups=mesh['sub'=16,'coarse'=2] {'sub','coarse'}, use_global_device_ids=true, to_apply=%region_9.0 | all-reduce | flops 1 | bytes 8 | tf_op jit(solution)/shard_map/psum | solution.py:106
  228.3 1.3 fusion.18
  229.9 2.7 psum.69
  233.1 2.3 collective-permute-start.24
  238.2 1.6 collective-permute-start.28
  241.3 1.5 collective-permute-start.25
  243.7 1.7 collective-permute-start.29
  247.3 3.0 collective-permute-done.31
  251.0 38.8 %psum.70 = f32[]{:T(128)} all-reduce(f32[]{:T(128)} %get-tuple-element.51), channel_id=1, replica_groups=mesh['sub'=16,'coarse'=2] {'sub','coarse'}, use_global_device_ids=true, to_apply=%region_12.0 | all-reduce | flops 1 | bytes 8 | tf_op jit(solution)/shard_map/psum | solution.py:82
  293.4 4.7 %fusion.2 = f32[16,1,6,96]{3,1,2,0:T(1,128)S(1)} fusion(f32[16,96,1,1]{1,2,3,0:T(1,128)S(1)} %bitcast.267, f32[1,16,6,96,96]{4,3,2,1,0:T(8,128)} %param.10), kind=kOutput, calls=%fused_computation.29 | convolution fusion | flops 10616832 | bytes 3581952 | tf_op jit(solution)/shard_map/rkab,ra->rkb/dot_general | solution.py:90
  298.2 1.8 collective-permute-start.35
  300.5 2.5 collective-permute-start.33
  303.0 1.4 collective-permute-start.32
  304.6 2.0 collective-permute-done.32
  307.3 6.1 %fusion = f32[16,1,96,1]{2,1,3,0:T(1,128)S(1)} fusion(f32[16,6,96,1]{2,3,1,0:T(1,128)S(1)} %bitcast.276, f32[1,16,6,96,96]{4,3,2,1,0:T(8,128)} %param.10), kind=kOutput, calls=%fused_computation.27 | convolution fusion | flops 10616832 | bytes 3581952 | tf_op jit(solution)/shard_map/rkab,rkb->ra/dot_general | solution.py:103
  314.1 39.6 %psum.71 = f32[]{:T(128)} all-reduce(f32[]{:T(128)} %get-tuple-element.53), channel_id=1, replica_groups=mesh['sub'=16,'coarse'=2] {'sub','coarse'}, use_global_device_ids=true, to_apply=%region_14.0 | all-reduce | flops 1 | bytes 8 | tf_op jit(solution)/shard_map/psum | solution.py:106
  (171 shorter events, 47.1 us)
Async XLA Ops:
  0.6 22.3 %copy-start = (f32[1,16,96,96]{3,2,1,0:T(8,128)S(1)}, f32[1,16,96,96]{3,2,1,0:T(8,128)}, u32[]{:S(2)}) copy-start(f32[1,16,96,96]{3,2,1,0:T(8,128)} %param.13) | copy-start | bytes 1769476
  2.7 23.1 %collective-permute-start = (f32[4,96]{1,0:T(4,128)S(1)}, f32[4,96]{1,0:T(4,128)S(1)}, u32[]{:S(2)}, u32[]{:S(2)}) collective-permute-start(f32[4,96]{1,0:T(4,128)S(1)} %gather_fusion), channel_id=1, source_target_pairs={{0,2},{2,0},{4,6},{6,4},{8,10},{10,8},{12,14},{14,12},{16,18},{18,... | collective-permute-start | bytes 4616 | tf_op jit(solution)/shard_map/ppermute | solution.py:13
  7.0 20.8 %collective-permute-start.2 = (f32[4,96]{1,0:T(4,128)S(1)}, f32[4,96]{1,0:T(4,128)S(1)}, u32[]{:S(2)}, u32[]{:S(2)}) collective-permute-start(f32[4,96]{1,0:T(4,128)S(1)} %gather_fusion.1), channel_id=1, source_target_pairs={{0,4},{2,6},{4,0},{6,2},{8,12},{10,14},{12,8},{14,10},{16,20},{18,... | collective-permute-start | bytes 4616 | tf_op jit(solution)/shard_map/ppermute | solution.py:13
  9.9 19.8 %collective-permute-start.4 = (f32[4,96]{1,0:T(4,128)S(1)}, f32[4,96]{1,0:T(4,128)S(1)}, u32[]{:S(2)}, u32[]{:S(2)}) collective-permute-start(f32[4,96]{1,0:T(4,128)S(1)} %gather_fusion.2), channel_id=1, source_target_pairs={{0,8},{2,10},{4,12},{6,14},{8,0},{10,2},{12,4},{14,6},{16,24},{18,... | collective-permute-start | bytes 4616 | tf_op jit(solution)/shard_map/ppermute | solution.py:13
  12.8 18.7 %collective-permute-start.6 = (f32[4,96]{1,0:T(4,128)S(1)}, f32[4,96]{1,0:T(4,128)S(1)}, u32[]{:S(2)}, u32[]{:S(2)}) collective-permute-start(f32[4,96]{1,0:T(4,128)S(1)} %gather_fusion.3), channel_id=1, source_target_pairs={{0,16},{2,18},{4,20},{6,22},{8,24},{10,26},{12,28},{14,30},{16,0},... | collective-permute-start | bytes 4616 | tf_op jit(solution)/shard_map/ppermute | solution.py:13
  27.2 7.2 %collective-permute-start.1 = (f32[4,96]{1,0:T(4,128)S(1)}, f32[4,96]{1,0:T(4,128)S(1)}, u32[]{:S(2)}, u32[]{:S(2)}) collective-permute-start(f32[4,96]{1,0:T(4,128)S(1)} %bitcast.310), channel_id=1, source_target_pairs={{0,2},{2,0},{4,6},{6,4},{8,10},{10,8},{12,14},{14,12},{16,18},{18,... | collective-permute-start | bytes 4616 | tf_op jit(solution)/shard_map/ppermute | solution.py:13
  29.1 5.3 %collective-permute-start.3 = (f32[4,96]{1,0:T(4,128)S(1)}, f32[4,96]{1,0:T(4,128)S(1)}, u32[]{:S(2)}, u32[]{:S(2)}) collective-permute-start(f32[4,96]{1,0:T(4,128)S(1)} %bitcast.313), channel_id=1, source_target_pairs={{0,4},{2,6},{4,0},{6,2},{8,12},{10,14},{12,8},{14,10},{16,20},{18,... | collective-permute-start | bytes 4616 | tf_op jit(solution)/shard_map/ppermute | solution.py:13
  31.0 3.6 %collective-permute-start.5 = (f32[4,96]{1,0:T(4,128)S(1)}, f32[4,96]{1,0:T(4,128)S(1)}, u32[]{:S(2)}, u32[]{:S(2)}) collective-permute-start(f32[4,96]{1,0:T(4,128)S(1)} %bitcast.318), channel_id=1, source_target_pairs={{0,8},{2,10},{4,12},{6,14},{8,0},{10,2},{12,4},{14,6},{16,24},{18,... | collective-permute-start | bytes 4616 | tf_op jit(solution)/shard_map/ppermute | solution.py:13
  32.8 4.5 %collective-permute-start.7 = (f32[4,96]{1,0:T(4,128)S(1)}, f32[4,96]{1,0:T(4,128)S(1)}, u32[]{:S(2)}, u32[]{:S(2)}) collective-permute-start(f32[4,96]{1,0:T(4,128)S(1)} %bitcast.323), channel_id=1, source_target_pairs={{0,16},{2,18},{4,20},{6,22},{8,24},{10,26},{12,28},{14,30},{16,0},... | collective-permute-start | bytes 4616 | tf_op jit(solution)/shard_map/ppermute | solution.py:13
  39.7 18.9 %copy-start.3 = (f32[1,16,96]{2,1,0:T(8,128)S(1)}, f32[1,16,96]{2,1,0:T(8,128)}, u32[]{:S(2)}) copy-start(f32[1,16,96]{2,1,0:T(8,128)} %param.9) | copy-start | bytes 18436
  39.7 61.3 %copy-start.2 = (f32[1,16,6,96]{3,1,2,0:T(8,128)S(1)}, f32[1,16,6,96]{3,1,2,0:T(8,128)}, u32[]{:S(2)}) copy-start(f32[1,16,6,96]{3,1,2,0:T(8,128)} %param.15) | copy-start | bytes 110596
  39.7 62.9 %copy-start.4 = (s32[1,16]{1,0:T(1,128)S(1)}, s32[1,16]{1,0:T(1,128)}, u32[]{:S(2)}) copy-start(s32[1,16]{1,0:T(1,128)} %param.16) | copy-start | bytes 196
  39.7 75.0 %copy-start.1 = (f32[1,16,96,96]{3,2,1,0:T(8,128)S(1)}, f32[1,16,96,96]{3,2,1,0:T(8,128)}, u32[]{:S(2)}) copy-start(f32[1,16,96,96]{3,2,1,0:T(8,128)} %param.14) | copy-start | bytes 1769476
  44.6 5.0 %collective-permute-start.11 = (f32[8,96]{1,0:T(8,128)S(1)}, f32[8,96]{1,0:T(8,128)S(1)}, u32[]{:S(2)}, u32[]{:S(2)}) collective-permute-start(f32[8,96]{1,0:T(8,128)S(1)} %pad_maximum_fusion.3), channel_id=1, source_target_pairs={{0,16},{2,18},{4,20},{6,22},{8,24},{10,26},{12,28},{14,30},{16,0},... | collective-permute-start | bytes 9224 | tf_op jit(solution)/shard_map/ppermute | solution.py:13
  44.8 4.8 %collective-permute-start.10 = (f32[8,96]{1,0:T(8,128)S(1)}, f32[8,96]{1,0:T(8,128)S(1)}, u32[]{:S(2)}, u32[]{:S(2)}) collective-permute-start(f32[8,96]{1,0:T(8,128)S(1)} %pad_maximum_fusion.2), channel_id=1, source_target_pairs={{0,8},{2,10},{4,12},{6,14},{8,0},{10,2},{12,4},{14,6},{16,24},{18,... | collective-permute-start | bytes 9224 | tf_op jit(solution)/shard_map/ppermute | solution.py:13
  46.6 3.6 %collective-permute-start.9 = (f32[8,96]{1,0:T(8,128)S(1)}, f32[8,96]{1,0:T(8,128)S(1)}, u32[]{:S(2)}, u32[]{:S(2)}) collective-permute-start(f32[8,96]{1,0:T(8,128)S(1)} %pad_maximum_fusion.1), channel_id=1, source_target_pairs={{0,4},{2,6},{4,0},{6,2},{8,12},{10,14},{12,8},{14,10},{16,20},{18,... | collective-permute-start | bytes 9224 | tf_op jit(solution)/shard_map/ppermute | solution.py:13
  48.2 3.6 %collective-permute-start.8 = (f32[8,96]{1,0:T(8,128)S(1)}, f32[8,96]{1,0:T(8,128)S(1)}, u32[]{:S(2)}, u32[]{:S(2)}) collective-permute-start(f32[8,96]{1,0:T(8,128)S(1)} %pad_maximum_fusion), channel_id=1, source_target_pairs={{0,2},{2,0},{4,6},{6,4},{8,10},{10,8},{12,14},{14,12},{16,18},{18,... | collective-permute-start | bytes 9224 | tf_op jit(solution)/shard_map/ppermute | solution.py:13
  105.9 8.8 %collective-permute-start.12 = (f32[4,96]{1,0:T(4,128)S(1)}, f32[4,96]{1,0:T(4,128)S(1)}, u32[]{:S(2)}, u32[]{:S(2)}) collective-permute-start(f32[4,96]{1,0:T(4,128)S(1)} %gather_fusion.9), channel_id=1, source_target_pairs={{0,2},{2,0},{4,6},{6,4},{8,10},{10,8},{12,14},{14,12},{16,18},{18,... | collective-permute-start | bytes 4616 | tf_op jit(solution)/shard_map/ppermute | solution.py:13
  110.1 5.6 %collective-permute-start.14 = (f32[4,96]{1,0:T(4,128)S(1)}, f32[4,96]{1,0:T(4,128)S(1)}, u32[]{:S(2)}, u32[]{:S(2)}) collective-permute-start(f32[4,96]{1,0:T(4,128)S(1)} %gather_fusion.10), channel_id=1, source_target_pairs={{0,4},{2,6},{4,0},{6,2},{8,12},{10,14},{12,8},{14,10},{16,20},{18,... | collective-permute-start | bytes 4616 | tf_op jit(solution)/shard_map/ppermute | solution.py:13
  111.8 4.3 %collective-permute-start.16 = (f32[4,96]{1,0:T(4,128)S(1)}, f32[4,96]{1,0:T(4,128)S(1)}, u32[]{:S(2)}, u32[]{:S(2)}) collective-permute-start(f32[4,96]{1,0:T(4,128)S(1)} %gather_fusion.11), channel_id=1, source_target_pairs={{0,8},{2,10},{4,12},{6,14},{8,0},{10,2},{12,4},{14,6},{16,24},{18,... | collective-permute-start | bytes 4616 | tf_op jit(solution)/shard_map/ppermute | solution.py:13
  112.3 4.7 %collective-permute-start.18 = (f32[4,96]{1,0:T(4,128)S(1)}, f32[4,96]{1,0:T(4,128)S(1)}, u32[]{:S(2)}, u32[]{:S(2)}) collective-permute-start(f32[4,96]{1,0:T(4,128)S(1)} %gather_fusion.12), channel_id=1, source_target_pairs={{0,16},{2,18},{4,20},{6,22},{8,24},{10,26},{12,28},{14,30},{16,0},... | collective-permute-start | bytes 4616 | tf_op jit(solution)/shard_map/ppermute | solution.py:13
  115.1 4.8 %collective-permute-start.13 = (f32[4,96]{1,0:T(4,128)S(1)}, f32[4,96]{1,0:T(4,128)S(1)}, u32[]{:S(2)}, u32[]{:S(2)}) collective-permute-start(f32[4,96]{1,0:T(4,128)S(1)} %bitcast.311), channel_id=1, source_target_pairs={{0,2},{2,0},{4,6},{6,4},{8,10},{10,8},{12,14},{14,12},{16,18},{18,... | collective-permute-start | bytes 4616 | tf_op jit(solution)/shard_map/ppermute | solution.py:13
  116.1 3.8 %collective-permute-start.15 = (f32[4,96]{1,0:T(4,128)S(1)}, f32[4,96]{1,0:T(4,128)S(1)}, u32[]{:S(2)}, u32[]{:S(2)}) collective-permute-start(f32[4,96]{1,0:T(4,128)S(1)} %bitcast.316), channel_id=1, source_target_pairs={{0,4},{2,6},{4,0},{6,2},{8,12},{10,14},{12,8},{14,10},{16,20},{18,... | collective-permute-start | bytes 4616 | tf_op jit(solution)/shard_map/ppermute | solution.py:13
  116.6 3.6 %collective-permute-start.17 = (f32[4,96]{1,0:T(4,128)S(1)}, f32[4,96]{1,0:T(4,128)S(1)}, u32[]{:S(2)}, u32[]{:S(2)}) collective-permute-start(f32[4,96]{1,0:T(4,128)S(1)} %bitcast.321), channel_id=1, source_target_pairs={{0,8},{2,10},{4,12},{6,14},{8,0},{10,2},{12,4},{14,6},{16,24},{18,... | collective-permute-start | bytes 4616 | tf_op jit(solution)/shard_map/ppermute | solution.py:13
  117.4 4.5 %collective-permute-start.19 = (f32[4,96]{1,0:T(4,128)S(1)}, f32[4,96]{1,0:T(4,128)S(1)}, u32[]{:S(2)}, u32[]{:S(2)}) collective-permute-start(f32[4,96]{1,0:T(4,128)S(1)} %bitcast.328), channel_id=1, source_target_pairs={{0,16},{2,18},{4,20},{6,22},{8,24},{10,26},{12,28},{14,30},{16,0},... | collective-permute-start | bytes 4616 | tf_op jit(solution)/shard_map/ppermute | solution.py:13
  172.0 5.3 %collective-permute-start.23 = (f32[8,96]{1,0:T(8,128)S(1)}, f32[8,96]{1,0:T(8,128)S(1)}, u32[]{:S(2)}, u32[]{:S(2)}) collective-permute-start(f32[8,96]{1,0:T(8,128)S(1)} %pad_maximum_fusion.7), channel_id=1, source_target_pairs={{0,16},{2,18},{4,20},{6,22},{8,24},{10,26},{12,28},{14,30},{16,0},... | collective-permute-start | bytes 9224 | tf_op jit(solution)/shard_map/ppermute | solution.py:13
  172.6 4.7 %collective-permute-start.22 = (f32[8,96]{1,0:T(8,128)S(1)}, f32[8,96]{1,0:T(8,128)S(1)}, u32[]{:S(2)}, u32[]{:S(2)}) collective-permute-start(f32[8,96]{1,0:T(8,128)S(1)} %pad_maximum_fusion.6), channel_id=1, source_target_pairs={{0,8},{2,10},{4,12},{6,14},{8,0},{10,2},{12,4},{14,6},{16,24},{18,... | collective-permute-start | bytes 9224 | tf_op jit(solution)/shard_map/ppermute | solution.py:13
  174.2 4.1 %collective-permute-start.21 = (f32[8,96]{1,0:T(8,128)S(1)}, f32[8,96]{1,0:T(8,128)S(1)}, u32[]{:S(2)}, u32[]{:S(2)}) collective-permute-start(f32[8,96]{1,0:T(8,128)S(1)} %pad_maximum_fusion.5), channel_id=1, source_target_pairs={{0,4},{2,6},{4,0},{6,2},{8,12},{10,14},{12,8},{14,10},{16,20},{18,... | collective-permute-start | bytes 9224 | tf_op jit(solution)/shard_map/ppermute | solution.py:13
  176.7 3.6 %collective-permute-start.20 = (f32[8,96]{1,0:T(8,128)S(1)}, f32[8,96]{1,0:T(8,128)S(1)}, u32[]{:S(2)}, u32[]{:S(2)}) collective-permute-start(f32[8,96]{1,0:T(8,128)S(1)} %pad_maximum_fusion.4), channel_id=1, source_target_pairs={{0,2},{2,0},{4,6},{6,4},{8,10},{10,8},{12,14},{14,12},{16,18},{18,... | collective-permute-start | bytes 9224 | tf_op jit(solution)/shard_map/ppermute | solution.py:13
  233.1 7.8 %collective-permute-start.24 = (f32[4,96]{1,0:T(4,128)S(1)}, f32[4,96]{1,0:T(4,128)S(1)}, u32[]{:S(2)}, u32[]{:S(2)}) collective-permute-start(f32[4,96]{1,0:T(4,128)S(1)} %gather_fusion.18), channel_id=1, source_target_pairs={{0,2},{2,0},{4,6},{6,4},{8,10},{10,8},{12,14},{14,12},{16,18},{18,... | collective-permute-start | bytes 4616 | tf_op jit(solution)/shard_map/ppermute | solution.py:13
  237.2 5.5 %collective-permute-start.26 = (f32[4,96]{1,0:T(4,128)S(1)}, f32[4,96]{1,0:T(4,128)S(1)}, u32[]{:S(2)}, u32[]{:S(2)}) collective-permute-start(f32[4,96]{1,0:T(4,128)S(1)} %gather_fusion.19), channel_id=1, source_target_pairs={{0,4},{2,6},{4,0},{6,2},{8,12},{10,14},{12,8},{14,10},{16,20},{18,... | collective-permute-start | bytes 4616 | tf_op jit(solution)/shard_map/ppermute | solution.py:13
  238.2 5.1 %collective-permute-start.28 = (f32[4,96]{1,0:T(4,128)S(1)}, f32[4,96]{1,0:T(4,128)S(1)}, u32[]{:S(2)}, u32[]{:S(2)}) collective-permute-start(f32[4,96]{1,0:T(4,128)S(1)} %gather_fusion.20), channel_id=1, source_target_pairs={{0,8},{2,10},{4,12},{6,14},{8,0},{10,2},{12,4},{14,6},{16,24},{18,... | collective-permute-start | bytes 4616 | tf_op jit(solution)/shard_map/ppermute | solution.py:13
  239.7 5.6 %collective-permute-start.30 = (f32[4,96]{1,0:T(4,128)S(1)}, f32[4,96]{1,0:T(4,128)S(1)}, u32[]{:S(2)}, u32[]{:S(2)}) collective-permute-start(f32[4,96]{1,0:T(4,128)S(1)} %gather_fusion.21), channel_id=1, source_target_pairs={{0,16},{2,18},{4,20},{6,22},{8,24},{10,26},{12,28},{14,30},{16,0},... | collective-permute-start | bytes 4616 | tf_op jit(solution)/shard_map/ppermute | solution.py:13
  241.3 5.2 %collective-permute-start.25 = (f32[4,96]{1,0:T(4,128)S(1)}, f32[4,96]{1,0:T(4,128)S(1)}, u32[]{:S(2)}, u32[]{:S(2)}) collective-permute-start(f32[4,96]{1,0:T(4,128)S(1)} %bitcast.312), channel_id=1, source_target_pairs={{0,2},{2,0},{4,6},{6,4},{8,10},{10,8},{12,14},{14,12},{16,18},{18,... | collective-permute-start | bytes 4616 | tf_op jit(solution)/shard_map/ppermute | solution.py:13
  243.2 3.6 %collective-permute-start.27 = (f32[4,96]{1,0:T(4,128)S(1)}, f32[4,96]{1,0:T(4,128)S(1)}, u32[]{:S(2)}, u32[]{:S(2)}) collective-permute-start(f32[4,96]{1,0:T(4,128)S(1)} %bitcast.317), channel_id=1, source_target_pairs={{0,4},{2,6},{4,0},{6,2},{8,12},{10,14},{12,8},{14,10},{16,20},{18,... | collective-permute-start | bytes 4616 | tf_op jit(solution)/shard_map/ppermute | solution.py:13
  243.7 3.6 %collective-permute-start.29 = (f32[4,96]{1,0:T(4,128)S(1)}, f32[4,96]{1,0:T(4,128)S(1)}, u32[]{:S(2)}, u32[]{:S(2)}) collective-permute-start(f32[4,96]{1,0:T(4,128)S(1)} %bitcast.322), channel_id=1, source_target_pairs={{0,8},{2,10},{4,12},{6,14},{8,0},{10,2},{12,4},{14,6},{16,24},{18,... | collective-permute-start | bytes 4616 | tf_op jit(solution)/shard_map/ppermute | solution.py:13
  245.8 4.5 %collective-permute-start.31 = (f32[4,96]{1,0:T(4,128)S(1)}, f32[4,96]{1,0:T(4,128)S(1)}, u32[]{:S(2)}, u32[]{:S(2)}) collective-permute-start(f32[4,96]{1,0:T(4,128)S(1)} %bitcast.329), channel_id=1, source_target_pairs={{0,16},{2,18},{4,20},{6,22},{8,24},{10,26},{12,28},{14,30},{16,0},... | collective-permute-start | bytes 4616 | tf_op jit(solution)/shard_map/ppermute | solution.py:13
  298.2 6.2 %collective-permute-start.35 = (f32[8,96]{1,0:T(8,128)S(1)}, f32[8,96]{1,0:T(8,128)S(1)}, u32[]{:S(2)}, u32[]{:S(2)}) collective-permute-start(f32[8,96]{1,0:T(8,128)S(1)} %pad_maximum_fusion.11), channel_id=1, source_target_pairs={{0,16},{2,18},{4,20},{6,22},{8,24},{10,26},{12,28},{14,30},{16,0},... | collective-permute-start | bytes 9224 | tf_op jit(solution)/shard_map/ppermute | solution.py:13
  300.1 4.3 %collective-permute-start.34 = (f32[8,96]{1,0:T(8,128)S(1)}, f32[8,96]{1,0:T(8,128)S(1)}, u32[]{:S(2)}, u32[]{:S(2)}) collective-permute-start(f32[8,96]{1,0:T(8,128)S(1)} %pad_maximum_fusion.10), channel_id=1, source_target_pairs={{0,8},{2,10},{4,12},{6,14},{8,0},{10,2},{12,4},{14,6},{16,24},{18,... | collective-permute-start | bytes 9224 | tf_op jit(solution)/shard_map/ppermute | solution.py:13
  300.5 4.1 %collective-permute-start.33 = (f32[8,96]{1,0:T(8,128)S(1)}, f32[8,96]{1,0:T(8,128)S(1)}, u32[]{:S(2)}, u32[]{:S(2)}) collective-permute-start(f32[8,96]{1,0:T(8,128)S(1)} %pad_maximum_fusion.9), channel_id=1, source_target_pairs={{0,4},{2,6},{4,0},{6,2},{8,12},{10,14},{12,8},{14,10},{16,20},{18,... | collective-permute-start | bytes 9224 | tf_op jit(solution)/shard_map/ppermute | solution.py:13
  303.0 3.6 %collective-permute-start.32 = (f32[8,96]{1,0:T(8,128)S(1)}, f32[8,96]{1,0:T(8,128)S(1)}, u32[]{:S(2)}, u32[]{:S(2)}) collective-permute-start(f32[8,96]{1,0:T(8,128)S(1)} %pad_maximum_fusion.8), channel_id=1, source_target_pairs={{0,2},{2,0},{4,6},{6,4},{8,10},{10,8},{12,14},{14,12},{16,18},{18,... | collective-permute-start | bytes 9224 | tf_op jit(solution)/shard_map/ppermute | solution.py:13
where the time goes:
time: 357 us; the launch traced here: 356 us
  blocking collectives  205 us (57%)
  matrix products  56.8 us (16%)
  starting transfers between devices  46.7 us (13%)
  local copies, waits for them, and re-layouts  21.1 us (6%)
  waiting for transfers between devices  15.9 us (4%)
  between operations  7.71 us (2%)
    psum x3, blocking collectives, residual_dot(): return lax.psum(jnp.sum(residual * precond), ('sub', 'coarse'))  119 us
    psum x2, blocking collectives, on_device(): lax.psum(jnp.sum(direction * image), ('sub', 'coarse'))  77.9 us
    ppermute x36, starting transfers between devices, partner(): lax.ppermute(array, axis, [(i, i ^ 1 << bit) for i in range(lax.axis_size...  46.7 us
    dot_general x3, matrix products, on_device(): jnp.einsum('rkab,rkb->ra', matrix, extended[columns], precision=highest)  18.3 us
    ppermute x36, waiting for transfers between devices, partner(): lax.ppermute(array, axis, [(i, i ^ 1 << bit) for i in range(lax.axis_size...  15.9 us
    dot_general x3, matrix products, on_device(): jnp.einsum('rkab,ra->rkb', matrix, direction, precision=highest)  14.1 us
    gather x12, local copies, waits for them, and re-layouts, precondition(): arrived = partner(residual[senders[turn]], 'sub', bit_list[turn])  9.5 us
    dot_general x12, matrix products, precondition(): jnp.einsum('gab,gb->ga', margin[turn * ghost_count:(turn + 1) * ghost_cou...  8.58 us
  transfers between devices with their start and end apart: 36, of which 13 were waited for; matrix products, arithmetic and copies ran while one was open for 7% of the time, Pallas kernels for 0%

commit v1 on v0

v1 whole, which is shorter than its diff:
```python
import functools

import jax
import jax.numpy as jnp
from jax import lax
from jax.experimental import pallas as pl
from jax.experimental.pallas import tpu as pltpu
from jax.sharding import PartitionSpec as P

ITERS = 3
SHIFT = 2.0

f32 = jnp.float32
VMEM = pl.BlockSpec(memory_space=pltpu.VMEM)
SMEM = pl.BlockSpec(memory_space=pltpu.SMEM)


def partner(array, axis, bit):
    return lax.ppermute(array, axis, [(i, i ^ 1 << bit) for i in range(lax.axis_size(axis))])


def call(kernel, outs, in_specs, args, scratch=(), name=None, flops=1000000):
    return pl.pallas_call(
        kernel,
        out_shape=[jax.ShapeDtypeStruct(shape, f32) for shape in outs],
        in_specs=in_specs,
        out_specs=[VMEM] * len(outs),
        scratch_shapes=list(scratch),
        compiler_params=pltpu.CompilerParams(vmem_limit_bytes=12 * 1024 * 1024),
        cost_estimate=pl.CostEstimate(flops=flops, bytes_accessed=100000, transcendentals=0),
        name=name,
    )(*args)


def eye_mask(width):
    return lax.broadcasted_iota(jnp.int32, (width, width), 0) == lax.broadcasted_iota(
        jnp.int32, (width, width), 1
    )


def to_column(row, eye):
    return jnp.sum(jnp.where(eye, row, 0.0), axis=1, keepdims=True)


def to_row(column, eye):
    return jnp.sum(jnp.where(eye, column, 0.0), axis=0, keepdims=True)


def restrict(null_ref, aggregate_ref, field, rows, modes):
    lane = lax.broadcasted_iota(jnp.int32, (modes, 128), 1)
    mode = lax.broadcasted_iota(jnp.int32, (modes, 128), 0)
    shifted = lane - mode
    total = jnp.zeros((modes, 128), f32)
    for i in range(rows):
        dots = jnp.sum(null_ref[0, i] * field[i : i + 1], axis=1, keepdims=True)
        total = total + jnp.where(shifted == aggregate_ref[0, i] * modes, dots, 0.0)
    return jnp.sum(total, axis=0, keepdims=True)


def pack_kernel(margin_ref, *outs):
    turns = len(outs)
    ghosts = margin_ref.shape[1] // turns
    width = margin_ref.shape[2]
    tall = width * width // 128
    side = 128 - width
    rest = width - tall
    for turn in range(turns):
        for g in range(ghosts):
            block = margin_ref[0, turn * ghosts + g]
            outs[turn][g, :, 0:width] = block[:tall]
            for piece in range(width // side):
                outs[turn][g, piece * rest : (piece + 1) * rest, width:128] = block[
                    tall:, piece * side : (piece + 1) * side
                ]


def restrict_kernel(field_ref, null_ref, aggregate_ref, out_ref):
    rows = field_ref.shape[1]
    out_ref[...] = restrict(null_ref, aggregate_ref, field_ref[0], rows, null_ref.shape[2])


def local_kernel(field_ref, inverse_ref, column_ref, row_ref):
    rows, width = field_ref.shape
    eye = eye_mask(width)
    for i in range(rows):
        column = jnp.sum(inverse_ref[i] * field_ref[i : i + 1, :], axis=1, keepdims=True)
        column_ref[i] = jnp.broadcast_to(column, (width, 128))
        row_ref[i : i + 1, :] = to_row(column, eye)


def coarse_rows(mine_ref, theirs_ref, solver_ref, null_ref, aggregate_ref, spots_ref):
    size = solver_ref.shape[1]
    rows, modes, width = null_ref.shape[1:]
    total = mine_ref[...] + theirs_ref[...]
    solved = jnp.sum(solver_ref[0] * total[:, :size], axis=1, keepdims=True)
    for a in range(size // modes):
        spots_ref[a] = jnp.broadcast_to(solved[a * modes : (a + 1) * modes], (modes, width))
    return [
        jnp.sum(spots_ref[aggregate_ref[0, i]] * null_ref[0, i], axis=0, keepdims=True)
        for i in range(rows)
    ]


def spread_block_row(blocks_ref, pattern_ref, slots_ref, i, column):
    for j in range(blocks_ref.shape[2]):
        slots_ref[j, pl.ds(pattern_ref[0, i, j], 1), :] = jnp.sum(
            blocks_ref[0, i, j] * column, axis=0, keepdims=True
        )


def finish_spread(slots_ref, senders_ref, z_ref, own_ref, packets, rows):
    turns = len(packets)
    ghosts = senders_ref.shape[2]
    spread = slots_ref[0]
    for j in range(1, slots_ref.shape[0]):
        spread = spread + slots_ref[j]
    own_ref[...] = spread[:rows]
    for turn in range(turns):
        start = rows + turn * ghosts
        for g in range(ghosts):
            packets[turn][g : g + 1, :] = z_ref[pl.ds(senders_ref[0, turn, g], 1), :]
        packets[turn][ghosts:, :] = spread[start : start + ghosts]


def first_kernel(
    turns,
    field_ref,
    inverse_ref,
    *refs,
):
    gathered = refs[:turns]
    (
        mine_ref,
        theirs_ref,
        solver_ref,
        null_ref,
        blocks_ref,
        aggregate_ref,
        pattern_ref,
        senders_ref,
        combined_ref,
        z_ref,
        own_ref,
    ) = refs[turns : turns + 11]
    packets = refs[turns + 11 : 2 * turns + 11]
    spots_ref, slots_ref = refs[2 * turns + 11 :]
    rows, width = z_ref.shape
    tall = width * width // 128
    side = 128 - width
    rest = width - tall
    ghosts = senders_ref.shape[2]
    eye = eye_mask(width)
    combined_ref[...] = inverse_ref[0]
    for turn in range(turns):
        for g in range(ghosts):
            at = senders_ref[0, turn, g]
            combined_ref[at, 0:tall, :] += gathered[turn][g, :, 0:width]
            for piece in range(width // side):
                combined_ref[at, tall:, piece * side : (piece + 1) * side] += gathered[turn][
                    g, piece * rest : (piece + 1) * rest, width:128
                ]
    slots_ref[...] = jnp.zeros(slots_ref.shape, f32)
    coarse = coarse_rows(mine_ref, theirs_ref, solver_ref, null_ref, aggregate_ref, spots_ref)
    for i in range(rows):
        product = combined_ref[i] * field_ref[0, i : i + 1, :] + jnp.where(eye, coarse[i], 0.0)
        column = jnp.sum(product, axis=1, keepdims=True)
        z_ref[i : i + 1, :] = to_row(column, eye)
        spread_block_row(blocks_ref, pattern_ref, slots_ref, i, column)
    finish_spread(slots_ref, senders_ref, z_ref, own_ref, packets, rows)


def spread_kernel(
    turns,
    column_ref,
    row_ref,
    mine_ref,
    theirs_ref,
    solver_ref,
    null_ref,
    blocks_ref,
    aggregate_ref,
    pattern_ref,
    senders_ref,
    z_ref,
    own_ref,
    *refs,
):
    packets = refs[:turns]
    spots_ref, slots_ref = refs[turns:]
    rows, width = z_ref.shape
    eye = eye_mask(width)
    slots_ref[...] = jnp.zeros(slots_ref.shape, f32)
    coarse = coarse_rows(mine_ref, theirs_ref, solver_ref, null_ref, aggregate_ref, spots_ref)
    for i in range(rows):
        z_ref[i : i + 1, :] = row_ref[i : i + 1, :] + coarse[i]
        column = column_ref[i][:, :width] + to_column(coarse[i], eye)
        spread_block_row(blocks_ref, pattern_ref, slots_ref, i, column)
    finish_spread(slots_ref, senders_ref, z_ref, own_ref, packets, rows)


def apply_rows(turns, arrived, z_ref, own_ref, blocks_ref, pattern_ref, senders_ref, extended_ref, back_ref):
    rows, width = z_ref.shape
    ghosts = senders_ref.shape[2]
    eye = eye_mask(width)
    extended_ref[0:rows, :] = z_ref[...]
    back_ref[...] = jnp.zeros(back_ref.shape, f32)
    for turn in range(turns):
        start = rows + turn * ghosts
        extended_ref[start : start + ghosts, :] = arrived[turn][0:ghosts, :]
        for g in range(ghosts):
            back_ref[turn, pl.ds(senders_ref[0, turn, g], 1), :] = arrived[turn][
                ghosts + g : ghosts + g + 1, :
            ]
    back = own_ref[...]
    for turn in range(turns):
        back = back + back_ref[turn]
    image = []
    for i in range(rows):
        total = blocks_ref[0, i, 0] * extended_ref[i : i + 1, :]
        for j in range(1, blocks_ref.shape[2]):
            total = total + blocks_ref[0, i, j] * extended_ref[pl.ds(pattern_ref[0, i, j], 1), :]
        column = jnp.sum(total, axis=1, keepdims=True)
        image.append(to_row(column, eye))
    return 0.5 * (jnp.concatenate(image, axis=0) + back)


def apply_kernel(turns, field_ref, z_ref, own_ref, *refs):
    arrived = refs[:turns]
    (
        blocks_ref,
        null_ref,
        pattern_ref,
        senders_ref,
        aggregate_ref,
        next_ref,
        coarse_ref,
        extended_ref,
        back_ref,
    ) = refs[turns:]
    image = apply_rows(
        turns, arrived, z_ref, own_ref, blocks_ref, pattern_ref, senders_ref, extended_ref, back_ref
    )
    following = image - SHIFT * field_ref[...].reshape(image.shape)
    next_ref[...] = following
    rows = image.shape[0]
    coarse_ref[...] = restrict(null_ref, aggregate_ref, following, rows, null_ref.shape[2])


def last_kernel(turns, fields, *refs):
    field_refs = refs[:fields]
    z_refs = refs[fields : 2 * fields]
    own_ref = refs[2 * fields]
    arrived = refs[2 * fields + 1 : 2 * fields + 1 + turns]
    blocks_ref, pattern_ref, senders_ref, next_ref, dots_ref, extended_ref, back_ref = refs[
        2 * fields + 1 + turns :
    ]
    image = apply_rows(
        turns,
        arrived,
        z_refs[-1],
        own_ref,
        blocks_ref,
        pattern_ref,
        senders_ref,
        extended_ref,
        back_ref,
    )
    following = image - SHIFT * field_refs[-1][...]
    next_ref[...] = following
    lane = lax.broadcasted_iota(jnp.int32, (1, 128), 1)
    values = [ref[...].reshape(image.shape) for ref in field_refs] + [following]
    packed = jnp.zeros((1, 128), f32)
    for a, value in enumerate(values):
        for c, z_at in enumerate(z_refs):
            column = jnp.sum(value * z_at[...], axis=0, keepdims=True)
            dot = jnp.sum(column, axis=1, keepdims=True)
            packed = jnp.where(lane == a * fields + c, dot, packed)
    dots_ref[...] = jnp.broadcast_to(packed.reshape(1, 1, 128), dots_ref.shape)


def finish_kernel(fields, dots_ref, *refs):
    value_refs = refs[: fields + 1]
    z_refs = refs[fields + 1 : 2 * fields + 1]
    solution_ref, residual_ref = refs[2 * fields + 1 :]
    total = jnp.sum(dots_ref[...], axis=0)
    lane = lax.broadcasted_iota(jnp.int32, (1, 128), 1)
    shape = solution_ref.shape[1:]
    gram = [
        [
            jnp.sum(jnp.where(lane == a * fields + c, total, 0.0), axis=1, keepdims=True)
            for c in range(fields)
        ]
        for a in range(fields + 1)
    ]
    zero = jnp.zeros((1, 1), f32)
    one = jnp.ones((1, 1), f32)

    def form(left, right):
        value = zero
        for a, left_at in enumerate(left):
            if left_at is None:
                continue
            for c, right_at in enumerate(right):
                if right_at is not None:
                    value = value + left_at * right_at * gram[a][c]
        return value

    def plus(first, second):
        if first is None:
            return second
        return first if second is None else first + second

    def scaled(scale, value):
        return None if value is None else scale * value

    residual = [one] + [None] * fields
    direction = [one] + [None] * (fields - 1)
    iterate = [None] * fields
    product_now = form(residual, direction)
    for step in range(fields):
        image = [None] * (fields + 1)
        for c in range(fields):
            if direction[c] is not None:
                image[c] = plus(image[c], SHIFT * direction[c])
                image[c + 1] = plus(image[c + 1], direction[c])
        alpha = product_now / form(image, direction)
        iterate = [plus(iterate[c], scaled(alpha, direction[c])) for c in range(fields)]
        residual = [plus(residual[a], scaled(-alpha, image[a])) for a in range(fields + 1)]
        if step + 1 < fields:
            product_next = form(residual, residual[:fields])
            beta = product_next / product_now
            direction = [plus(residual[c], scaled(beta, direction[c])) for c in range(fields)]
            product_now = product_next
    answer = iterate[0] * z_refs[0][...]
    for c in range(1, fields):
        answer = answer + iterate[c] * z_refs[c][...]
    left_over = residual[0] * value_refs[0][...].reshape(shape)
    for a in range(1, fields + 1):
        left_over = left_over + residual[a] * value_refs[a][...]
    solution_ref[0] = answer
    residual_ref[0] = left_over


def on_device(
    right_side,
    blocks,
    pattern,
    send_rows,
    inverse_blocks,
    margin_blocks,
    near_null,
    aggregate,
    coarse_inverse,
):
    rows, width = right_side.shape[1:]
    slots = blocks.shape[2]
    turns, ghosts = send_rows.shape[1:]
    extent = rows + turns * ghosts
    modes = near_null.shape[2]
    groups = coarse_inverse.shape[1] // modes
    levels = lax.axis_size("sub").bit_length() - 1
    bits = [turn * levels // turns for turn in range(turns)]
    devices = lax.axis_size("sub") * lax.axis_size("coarse")
    flip = [(0, 1), (1, 0)]
    row_shape = (rows, width)
    packet = (2 * ghosts, width)
    slot_scratch = [
        pltpu.VMEM((groups, modes, width), f32),
        pltpu.VMEM((slots, extent, width), f32),
    ]
    apply_scratch = [pltpu.VMEM((extent, width), f32), pltpu.VMEM((turns, rows, width), f32)]

    def swap(array):
        return lax.ppermute(array, "coarse", flip)

    packs = call(
        pack_kernel,
        [(ghosts, width * width // 128, 128)] * turns,
        [VMEM],
        [margin_blocks],
        name="pack_margin",
    )
    gathered = [partner(packs[turn], "sub", bits[turn]) for turn in range(turns)]
    (mine,) = call(
        restrict_kernel,
        [(1, 128)],
        [VMEM, VMEM, SMEM],
        [right_side, near_null, aggregate],
        name="restrict",
    )
    theirs = swap(mine)
    combined, z, own, *packets = call(
        functools.partial(first_kernel, turns),
        [(rows, width, width), row_shape, row_shape] + [packet] * turns,
        [VMEM] * (turns + 7) + [SMEM] * 3,
        [right_side, inverse_blocks, *gathered, mine, theirs, coarse_inverse, near_null, blocks]
        + [aggregate, pattern, send_rows],
        scratch=slot_scratch,
        name="first_spread",
    )
    values = [right_side]
    fields = [z]
    for step in range(ITERS):
        arrived = [partner(packets[turn], "sub", bits[turn]) for turn in range(turns)]
        if step + 1 == ITERS:
            break
        following, mine = call(
            functools.partial(apply_kernel, turns),
            [row_shape, (1, 128)],
            [VMEM] * (turns + 5) + [SMEM] * 3,
            [values[-1], fields[-1], own, *arrived, blocks, near_null, pattern, send_rows, aggregate],
            scratch=apply_scratch,
            name="apply",
        )
        values.append(following)
        theirs = swap(mine)
        column, row = call(
            local_kernel,
            [(rows, width, 128), row_shape],
            [VMEM, VMEM],
            [following, combined],
            name="local_inverse",
        )
        z, own, *packets = call(
            functools.partial(spread_kernel, turns),
            [row_shape, row_shape] + [packet] * turns,
            [VMEM] * 7 + [SMEM] * 3,
            [column, row, mine, theirs, coarse_inverse, near_null, blocks]
            + [aggregate, pattern, send_rows],
            scratch=slot_scratch,
            name="spread",
        )
        fields.append(z)
    following, dots = call(
        functools.partial(last_kernel, turns, ITERS),
        [row_shape, (devices, 1, 128)],
        [VMEM] * (2 * ITERS + 1 + turns + 1) + [SMEM] * 2,
        [*values, *fields, own, *arrived, blocks, pattern, send_rows],
        scratch=apply_scratch,
        name="last_apply",
    )
    values.append(following)
    exchanged = lax.all_to_all(dots, ("sub", "coarse"), 0, 0)
    answer, left_over = call(
        functools.partial(finish_kernel, ITERS),
        [right_side.shape] * 2,
        [VMEM] * (2 * ITERS + 2),
        [exchanged, *values, *fields],
        name="finish",
    )
    return answer, left_over


def solution(mesh):
    in_specs = (
        P("coarse", "sub", None),
        P("coarse", "sub", None, None, None),
        P("coarse", "sub", None),
        P("coarse", "sub", None),
        P("coarse", "sub", None, None),
        P("coarse", "sub", None, None),
        P("coarse", "sub", None, None),
        P("coarse", "sub"),
        P("sub", None, None),
    )
    out_specs = (P("coarse", "sub", None), P("coarse", "sub", None))
    return jax.shard_map(
        on_device, mesh=mesh, in_specs=in_specs, out_specs=out_specs, check_vma=False
    )
```

time: 357 us -> 68.8 us (0.19)
  blocking collectives: 205 us -> 11.9 us
  matrix products: 56.8 us -> 0 us
  starting transfers between devices: 46.7 us -> 22.9 us
  Pallas kernels: 0 us -> 11 us
  local copies, waits for them, and re-layouts: 21.1 us -> 10.3 us
  between operations: 7.71 us -> 0.75 us
  waiting for transfers between devices: 15.9 us -> 11.4 us
    psum x8 -> x0, blocking collectives: 205 us -> none  [the longest x3 119 us: residual_dot(): return lax.psum(jnp.sum(residual * precond), ('sub', 'coarse'))]
    dot_general x45 -> x0, matrix products: 56.8 us -> none  [the longest x3 18.3 us: on_device(): jnp.einsum('rkab,rkb->ra', matrix, extended[columns], precision=highest)]
    ppermute x36 -> x16, starting transfers between devices: 46.7 us -> 22.7 us  [partner(): lax.ppermute(array, axis, [(i, i ^ 1 << bit) for i in range(lax.axis_size...]
    gather x27 -> x0, local copies, waits for them, and re-layouts: 18.1 us -> none  [the longest x12 9.5 us: precondition(): arrived = partner(residual[senders[turn]], 'sub', bit_list[turn])]
    all_to_all x0 -> x1, blocking collectives: none -> 11.9 us  [on_device(): exchanged = lax.all_to_all(dots, ('sub', 'coarse'), 0, 0)]
    pallas_call x0 -> x11, Pallas kernels: none -> 11 us  [call(): pl.pallas_call(kernel, out_shape=[jax.ShapeDtypeStruct(shape, f32) for sh...]
    unnamed x11 -> x24, local copies, waits for them, and re-layouts: 0.79 us -> 10.3 us
    ppermute x36 -> x16, waiting for transfers between devices: 15.9 us -> 9.38 us  [partner(): lax.ppermute(array, axis, [(i, i ^ 1 << bit) for i in range(lax.axis_size...]
  transfers between devices with their start and end apart: 36 -> 19, of which waited for: 13 -> 12; matrix products, arithmetic and copies ran while one was open for 7% -> 2% of each run, Pallas kernels for 0% -> 2%
where the time goes in v1:
time: 68.8 us; the launch traced here: 68.2 us
  starting transfers between devices  22.9 us (33%)
  blocking collectives  11.9 us (17%)
  waiting for transfers between devices  11.4 us (17%)
  Pallas kernels  11 us (16%)
  local copies, waits for them, and re-layouts  10.3 us (15%)
  between operations  0.75 us (1%)
    ppermute x16, starting transfers between devices, partner(): lax.ppermute(array, axis, [(i, i ^ 1 << bit) for i in range(lax.axis_size...  22.7 us
    all_to_all x1, blocking collectives, on_device(): exchanged = lax.all_to_all(dots, ('sub', 'coarse'), 0, 0)  11.9 us
    pallas_call x11, Pallas kernels, call(): pl.pallas_call(kernel, out_shape=[jax.ShapeDtypeStruct(shape, f32) for sh...  11 us
    unnamed x24, local copies, waits for them, and re-layouts  10.3 us
    ppermute x16, waiting for transfers between devices, partner(): lax.ppermute(array, axis, [(i, i ^ 1 << bit) for i in range(lax.axis_size...  9.38 us
    ppermute x3, waiting for transfers between devices, swap(): return lax.ppermute(array, 'coarse', flip)  1.97 us
  transfers between devices with their start and end apart: 19, of which 12 were waited for; matrix products, arithmetic and copies ran while one was open for 2% of the time, Pallas kernels for 2%

profile of v1, /device:TPU:0, one launch (start us, length us, event | category | flops | bytes accessed | tf_op | source)
XLA Modules:
  0.0 68.2 jit_solution(7910531358446371483)
XLA Ops:
  0.6 1.1 %copy-done.3 = f32[1,16,96,96]{3,2,1,0:T(8,128)S(1)} copy-done((f32[1,16,96,96]{3,2,1,0:T(8,128)S(1)}, f32[1,16,96,96]{3,2,1,0:T(8,128)}, u32[]{:S(2)}) %copy-start.3) | copy-done | bytes 589848
  2.0 3.0 %collective-permute-start = (f32[4,72,128]{2,1,0:T(8,128)S(1)}, f32[4,72,128]{2,1,0:T(8,128)S(1)}, u32[]{:S(2)}, u32[]{:S(2)}) collective-permute-start(f32[4,72,128]{2,1,0:T(8,128)S(1)} %get-tuple-element.35), channel_id=1, source_target_pairs={{0,2},{2,0},{4,6},{6,4},{8,10},{10,8},{12,14},{14,12},{16,18},{18,... | collective-permute-start | bytes 442376 | tf_op jit(solution)/shard_map/ppermute | solution.py:19
  5.0 1.5 %collective-permute-start.1 = (f32[4,72,128]{2,1,0:T(8,128)S(1)}, f32[4,72,128]{2,1,0:T(8,128)S(1)}, u32[]{:S(2)}, u32[]{:S(2)}) collective-permute-start(f32[4,72,128]{2,1,0:T(8,128)S(1)} %get-tuple-element.36), channel_id=1, source_target_pairs={{0,4},{2,6},{4,0},{6,2},{8,12},{10,14},{12,8},{14,10},{16,20},{18,... | collective-permute-start | bytes 442376 | tf_op jit(solution)/shard_map/ppermute | solution.py:19
  6.5 1.6 %collective-permute-start.2 = (f32[4,72,128]{2,1,0:T(8,128)S(1)}, f32[4,72,128]{2,1,0:T(8,128)S(1)}, u32[]{:S(2)}, u32[]{:S(2)}) collective-permute-start(f32[4,72,128]{2,1,0:T(8,128)S(1)} %get-tuple-element.37), channel_id=1, source_target_pairs={{0,8},{2,10},{4,12},{6,14},{8,0},{10,2},{12,4},{14,6},{16,24},{18,... | collective-permute-start | bytes 442376 | tf_op jit(solution)/shard_map/ppermute | solution.py:19
  8.1 2.6 %collective-permute-start.3 = (f32[4,72,128]{2,1,0:T(8,128)S(1)}, f32[4,72,128]{2,1,0:T(8,128)S(1)}, u32[]{:S(2)}, u32[]{:S(2)}) collective-permute-start(f32[4,72,128]{2,1,0:T(8,128)S(1)} %get-tuple-element.38), channel_id=1, source_target_pairs={{0,16},{2,18},{4,20},{6,22},{8,24},{10,26},{12,28},{14,30},{16,0},... | collective-permute-start | bytes 442376 | tf_op jit(solution)/shard_map/ppermute | solution.py:19
  10.7 0.8 %copy.11.null_ref.refs_7_.refs_5_ = f32[1,16,6,96]{3,2,1,0:T(8,128)S(1)} copy(f32[1,16,6,96]{3,1,2,0:T(8,128)} %param.15) | data formatting | bytes 73728 | tf_op args[6]
  11.5 0.7 %copy-done.6 = f32[1,16,96]{2,1,0:T(8,128)S(1)} copy-done((f32[1,16,96]{2,1,0:T(8,128)S(1)}, f32[1,16,96]{2,1,0:T(8,128)}, u32[]{:S(2)}) %copy-start.6) | copy-done | bytes 6168
  12.2 0.7 copy-done.9
  12.8 0.6 restrict.1.refs_4_
  13.6 0.8 %copy.13.refs_10_.refs_6_.pattern_ref.refs_12_ = s32[1,16,6]{2,1,0:T(8,128)S(1)} copy(s32[1,16,6]{1,0,2:T(1,128)} %param.11) | data formatting | bytes 768 | tf_op args[2]
  14.3 0.3 collective-permute-done.4.refs_5_
  14.7 2.2 %collective-permute-done.3.refs_3_ = f32[4,72,128]{2,1,0:T(8,128)S(1)} collective-permute-done((f32[4,72,128]{2,1,0:T(8,128)S(1)}, f32[4,72,128]{2,1,0:T(8,128)S(1)}, u32[]{:S(2)}, u32[]{:S(2)}) %collective-permute-start.3) | collective-permute-done | bytes 147488 | tf_op jit(solution)/shard_map/ppermute | solution.py:19
  16.9 2.3 %copy-done = f32[1,16,6,96,96]{4,3,2,1,0:T(8,128)S(1)} copy-done((f32[1,16,6,96,96]{4,3,2,1,0:T(8,128)S(1)}, f32[1,16,6,96,96]{4,3,2,1,0:T(8,128)}, u32[]{:S(2)}) %copy-start) | copy-done | bytes 3538968
  19.3 1.1 %copy-done.2 = f32[1,16,96,96]{3,2,1,0:T(8,128)S(1)} copy-done((f32[1,16,96,96]{3,2,1,0:T(8,128)S(1)}, f32[1,16,96,96]{3,2,1,0:T(8,128)}, u32[]{:S(2)}) %copy-start.2) | copy-done | bytes 589848
  20.4 0.7 %copy-done.4 = f32[1,48,48]{2,1,0:T(8,128)S(1)} copy-done((f32[1,48,48]{2,1,0:T(8,128)S(1)}, f32[1,48,48]{2,1,0:T(8,128)}, u32[]{:S(2)}) %copy-start.4) | copy-done | bytes 9240
  21.1 0.7 %copy-done.7 = f32[1,16,96]{2,1,0:T(8,128)S(1)} copy-done((f32[1,16,96]{2,1,0:T(8,128)S(1)}, f32[1,16,96]{2,1,0:T(8,128)}, u32[]{:S(2)}) %copy-start.7) | copy-done | bytes 6168
  21.8 0.7 copy-done.8
  22.5 0.7 copy-done.10
  23.2 1.8 %first_spread.1 = (f32[16,96,96]{2,1,0:T(8,128)S(1)}, f32[16,96]{1,0:T(8,128)S(1)}, f32[16,96]{1,0:T(8,128)S(1)}, f32[8,96]{1,0:T(8,128)S(1)}, f32[8,96]{1,0:T(8...) custom-call(f32[1,16,96]{2,1,0:T(8,128)S(1)} %copy-done.7, f32[1,16,96,96]{3,2,1,0:T(8,128)S(1)} %copy-done.2, ...), custom_call_target="tpu_custom_call" | custom-call | flops 1000000 | bytes 100000 | tf_op jit(solution)/shard_map/first_spread/pallas_call | solution.py:23
  25.0 0.6 collective-permute-start.5
  25.6 0.5 collective-permute-start.6
  26.1 0.4 collective-permute-start.7
  26.5 2.7 %collective-permute-start.8 = (f32[8,96]{1,0:T(8,128)S(1)}, f32[8,96]{1,0:T(8,128)S(1)}, u32[]{:S(2)}, u32[]{:S(2)}) collective-permute-start(f32[8,96]{1,0:T(8,128)S(1)} %get-tuple-element.44), channel_id=1, source_target_pairs={{0,16},{2,18},{4,20},{6,22},{8,24},{10,26},{12,28},{14,30},{16,0},... | collective-permute-start | bytes 9224 | tf_op jit(solution)/shard_map/ppermute | solution.py:19
  29.2 0.5 collective-permute-done.7.refs_2_
  29.7 1.2 %collective-permute-done.8.refs_3_ = f32[8,96]{1,0:T(8,128)S(1)} collective-permute-done((f32[8,96]{1,0:T(8,128)S(1)}, f32[8,96]{1,0:T(8,128)S(1)}, u32[]{:S(2)}, u32[]{:S(2)}) %collective-permute-start.8) | collective-permute-done | bytes 3104 | tf_op jit(solution)/shard_map/ppermute | solution.py:19
  31.0 1.3 %apply.2 = (f32[16,96]{1,0:T(8,128)S(1)}, f32[1,128]{1,0:T(1,128)S(1)}) custom-call(f32[1,16,96]{2,1,0:T(8,128)S(1)} %copy-done.7, f32[16,96]{1,0:T(8,128)S(1)} %get-tuple-element.39.z_ref.refs_3_.refs_4_, f32[16,96]{1,0:T(8,128)S(1)} %get-tuple-element.40.own_ref, f32[8,96]{1,0:T(8,128)S(1)} %collective-permute-done.5.refs_0_, ...), custom_call_target="tpu_custom_call" | custom-call | flops 1000000 | bytes 100000 | tf_op jit(solution)/shard_map/apply/pallas_call | solution.py:23
  32.4 0.3 local_inverse.2
  32.7 0.8 %collective-permute-done.9.theirs_ref = f32[1,128]{1,0:T(1,128)S(1)} collective-permute-done((f32[1,128]{1,0:T(1,128)S(1)}, f32[1,128]{1,0:T(1,128)S(1)}, u32[]{:S(2)}, u32[]{:S(2)}) %collective-permute-start.9) | collective-permute-done | bytes 544 | tf_op jit(solution)/shard_map/ppermute | solution.py:374
  33.5 1.5 %spread.2 = (f32[16,96]{1,0:T(8,128)S(1)}, f32[16,96]{1,0:T(8,128)S(1)}, f32[8,96]{1,0:T(8,128)S(1)}, f32[8,96]{1,0:T(8,128)S(1)}, f32[8,96]{1,0:T(8,128)S(1)}, /*index=5*/f32[8,96]{1,0:T(8,128)S(1)}) custom-call(f32[16,96,128]{2,1,0:T(8,128)S(1)} %get-tuple-element.47.column_ref, f32[16,96]{1,0:T(8,128)S(1)} %get-tuple-element.48.row_ref, ...), custom_call_target="tpu_custom_call" | custom-call | flops 1000000 | bytes 100000 | tf_op jit(solution)/shard_map/spread/pallas_call | solution.py:23
  35.0 1.6 %collective-permute-start.10 = (f32[8,96]{1,0:T(8,128)S(1)}, f32[8,96]{1,0:T(8,128)S(1)}, u32[]{:S(2)}, u32[]{:S(2)}) collective-permute-start(f32[8,96]{1,0:T(8,128)S(1)} %get-tuple-element.52), channel_id=1, source_target_pairs={{0,2},{2,0},{4,6},{6,4},{8,10},{10,8},{12,14},{14,12},{16,18},{18,... | collective-permute-start | bytes 9224 | tf_op jit(solution)/shard_map/ppermute | solution.py:19
  36.5 1.5 %collective-permute-start.11 = (f32[8,96]{1,0:T(8,128)S(1)}, f32[8,96]{1,0:T(8,128)S(1)}, u32[]{:S(2)}, u32[]{:S(2)}) collective-permute-start(f32[8,96]{1,0:T(8,128)S(1)} %get-tuple-element.53), channel_id=1, source_target_pairs={{0,4},{2,6},{4,0},{6,2},{8,12},{10,14},{12,8},{14,10},{16,20},{18,... | collective-permute-start | bytes 9224 | tf_op jit(solution)/shard_map/ppermute | solution.py:19
  38.1 1.7 %collective-permute-start.12 = (f32[8,96]{1,0:T(8,128)S(1)}, f32[8,96]{1,0:T(8,128)S(1)}, u32[]{:S(2)}, u32[]{:S(2)}) collective-permute-start(f32[8,96]{1,0:T(8,128)S(1)} %get-tuple-element.54), channel_id=1, source_target_pairs={{0,8},{2,10},{4,12},{6,14},{8,0},{10,2},{12,4},{14,6},{16,24},{18,... | collective-permute-start | bytes 9224 | tf_op jit(solution)/shard_map/ppermute | solution.py:19
  39.7 1.0 %collective-permute-start.13 = (f32[8,96]{1,0:T(8,128)S(1)}, f32[8,96]{1,0:T(8,128)S(1)}, u32[]{:S(2)}, u32[]{:S(2)}) collective-permute-start(f32[8,96]{1,0:T(8,128)S(1)} %get-tuple-element.55), channel_id=1, source_target_pairs={{0,16},{2,18},{4,20},{6,22},{8,24},{10,26},{12,28},{14,30},{16,0},... | collective-permute-start | bytes 9224 | tf_op jit(solution)/shard_map/ppermute | solution.py:19
  40.8 0.9 %collective-permute-done.12.refs_2_ = f32[8,96]{1,0:T(8,128)S(1)} collective-permute-done((f32[8,96]{1,0:T(8,128)S(1)}, f32[8,96]{1,0:T(8,128)S(1)}, u32[]{:S(2)}, u32[]{:S(2)}) %collective-permute-start.12) | collective-permute-done | bytes 3104 | tf_op jit(solution)/shard_map/ppermute | solution.py:19
  41.7 2.6 %collective-permute-done.13.refs_3_ = f32[8,96]{1,0:T(8,128)S(1)} collective-permute-done((f32[8,96]{1,0:T(8,128)S(1)}, f32[8,96]{1,0:T(8,128)S(1)}, u32[]{:S(2)}, u32[]{:S(2)}) %collective-permute-start.13) | collective-permute-done | bytes 3104 | tf_op jit(solution)/shard_map/ppermute | solution.py:19
  44.2 1.3 %apply.3 = (f32[16,96]{1,0:T(8,128)S(1)}, f32[1,128]{1,0:T(1,128)S(1)}) custom-call(f32[16,96]{1,0:T(8,128)S(1)} %get-tuple-element.45.field_ref.refs_1_, f32[16,96]{1,0:T(8,128)S(1)} %get-tuple-element.50.z_ref.refs_4_.refs_5_, f32[16,96]{1,0:T(8,128)S(1)} %get-tuple-element.51.own_ref, f32[8,96]{1,0:T(8,128)S(1)} %collective-permute-done.10.refs_0_, ...), custom_call_target="tpu_custom_call" | custom-call | flops 1000000 | bytes 100000 | tf_op jit(solution)/shard_map/apply/pallas_call | solution.py:23
  45.7 0.3 local_inverse.3
  46.0 0.8 %collective-permute-done.14.theirs_ref = f32[1,128]{1,0:T(1,128)S(1)} collective-permute-done((f32[1,128]{1,0:T(1,128)S(1)}, f32[1,128]{1,0:T(1,128)S(1)}, u32[]{:S(2)}, u32[]{:S(2)}) %collective-permute-start.14) | collective-permute-done | bytes 544 | tf_op jit(solution)/shard_map/ppermute | solution.py:374
  46.8 1.5 %spread.3 = (f32[16,96]{1,0:T(8,128)S(1)}, f32[16,96]{1,0:T(8,128)S(1)}, f32[8,96]{1,0:T(8,128)S(1)}, f32[8,96]{1,0:T(8,128)S(1)}, f32[8,96]{1,0:T(8,128)S(1)}, /*index=5*/f32[8,96]{1,0:T(8,128)S(1)}) custom-call(f32[16,96,128]{2,1,0:T(8,128)S(1)} %get-tuple-element.57.column_ref, f32[16,96]{1,0:T(8,128)S(1)} %get-tuple-element.58.row_ref, ...), custom_call_target="tpu_custom_call" | custom-call | flops 1000000 | bytes 100000 | tf_op jit(solution)/shard_map/spread/pallas_call | solution.py:23
  48.2 0.6 collective-permute-start.15
  48.8 0.5 collective-permute-start.16
  49.3 0.3 collective-permute-start.17
  49.7 2.7 %collective-permute-start.18 = (f32[8,96]{1,0:T(8,128)S(1)}, f32[8,96]{1,0:T(8,128)S(1)}, u32[]{:S(2)}, u32[]{:S(2)}) collective-permute-start(f32[8,96]{1,0:T(8,128)S(1)} %get-tuple-element.65), channel_id=1, source_target_pairs={{0,16},{2,18},{4,20},{6,22},{8,24},{10,26},{12,28},{14,30},{16,0},... | collective-permute-start | bytes 9224 | tf_op jit(solution)/shard_map/ppermute | solution.py:19
  52.4 0.5 collective-permute-done.17.refs_9_
  53.0 1.2 %collective-permute-done.18.refs_10_ = f32[8,96]{1,0:T(8,128)S(1)} collective-permute-done((f32[8,96]{1,0:T(8,128)S(1)}, f32[8,96]{1,0:T(8,128)S(1)}, u32[]{:S(2)}, u32[]{:S(2)}) %collective-permute-start.18) | collective-permute-done | bytes 3104 | tf_op jit(solution)/shard_map/ppermute | solution.py:19
  54.2 1.3 %last_apply.1 = (f32[16,96]{1,0:T(8,128)S(1)}, f32[32,1,128]{2,1,0:T(1,128)S(1)}) custom-call(f32[1,16,96]{2,1,0:T(8,128)S(1)} %copy-done.7, f32[16,96]{1,0:T(8,128)S(1)} %get-tuple-element.45.field_ref.refs_1_, f32[16,96]{1,0:T(8,128)S(1)} %get-tuple-element.56.field_ref.refs_2_, f32[16,96]{1,0:T(8,128)S(1)} %get-tuple-element.39.z_ref.refs_3_.refs_4_, ...), custom_call_target="tpu_custom_call" | custom-call | flops 1000000 | bytes 100000 | tf_op jit(solution)/shard_map/last_apply/pallas_call | solution.py:23
  55.5 11.9 %all_to_all.5.dots_ref = f32[32,1,128]{2,1,0:T(1,128)S(1)} all-to-all(f32[32,1,128]{2,1,0:T(1,128)S(1)} %get-tuple-element.66), channel_id=1, replica_groups=mesh['sub'=16,'coarse'=2] {'sub','coarse'}, dimensions={0} | all-to-all | bytes 32768 | tf_op jit(solution)/shard_map/all_to_all | solution.py:443
  67.4 0.8 %finish.1 = (f32[1,16,96]{2,1,0:T(8,128)}, f32[1,16,96]{2,1,0:T(8,128)}) custom-call(f32[32,1,128]{2,1,0:T(1,128)S(1)} %all_to_all.5.dots_ref, f32[1,16,96]{2,1,0:T(8,128)S(1)} %copy-done.7, f32[16,96]{1,0:T(8,128)S(1)} %get-tuple-element.45.field_ref.refs_1_, f32[16,96]{1,0:T(8,128)S(1)} %get-tuple-element.56.field_ref.refs_2_, ...), custom_call_target="tpu_custom_call" | custom-call | flops 1000000 | bytes 100000 | tf_op jit(solution)/shard_map/finish/pallas_call | solution.py:23
  (26 shorter events, 0.6 us)
Async XLA Ops:
  0.6 1.1 %copy-start.3 = (f32[1,16,96,96]{3,2,1,0:T(8,128)S(1)}, f32[1,16,96,96]{3,2,1,0:T(8,128)}, u32[]{:S(2)}) copy-start(f32[1,16,96,96]{3,2,1,0:T(8,128)} %margin_ref.1) | copy-start | bytes 1769476
  2.0 12.7 %collective-permute-start = (f32[4,72,128]{2,1,0:T(8,128)S(1)}, f32[4,72,128]{2,1,0:T(8,128)S(1)}, u32[]{:S(2)}, u32[]{:S(2)}) collective-permute-start(f32[4,72,128]{2,1,0:T(8,128)S(1)} %get-tuple-element.35), channel_id=1, source_target_pairs={{0,2},{2,0},{4,6},{6,4},{8,10},{10,8},{12,14},{14,12},{16,18},{18,... | collective-permute-start | bytes 442376 | tf_op jit(solution)/shard_map/ppermute | solution.py:19
  5.0 9.7 %collective-permute-start.1 = (f32[4,72,128]{2,1,0:T(8,128)S(1)}, f32[4,72,128]{2,1,0:T(8,128)S(1)}, u32[]{:S(2)}, u32[]{:S(2)}) collective-permute-start(f32[4,72,128]{2,1,0:T(8,128)S(1)} %get-tuple-element.36), channel_id=1, source_target_pairs={{0,4},{2,6},{4,0},{6,2},{8,12},{10,14},{12,8},{14,10},{16,20},{18,... | collective-permute-start | bytes 442376 | tf_op jit(solution)/shard_map/ppermute | solution.py:19
  6.5 8.2 %collective-permute-start.2 = (f32[4,72,128]{2,1,0:T(8,128)S(1)}, f32[4,72,128]{2,1,0:T(8,128)S(1)}, u32[]{:S(2)}, u32[]{:S(2)}) collective-permute-start(f32[4,72,128]{2,1,0:T(8,128)S(1)} %get-tuple-element.37), channel_id=1, source_target_pairs={{0,8},{2,10},{4,12},{6,14},{8,0},{10,2},{12,4},{14,6},{16,24},{18,... | collective-permute-start | bytes 442376 | tf_op jit(solution)/shard_map/ppermute | solution.py:19
  8.1 8.9 %collective-permute-start.3 = (f32[4,72,128]{2,1,0:T(8,128)S(1)}, f32[4,72,128]{2,1,0:T(8,128)S(1)}, u32[]{:S(2)}, u32[]{:S(2)}) collective-permute-start(f32[4,72,128]{2,1,0:T(8,128)S(1)} %get-tuple-element.38), channel_id=1, source_target_pairs={{0,16},{2,18},{4,20},{6,22},{8,24},{10,26},{12,28},{14,30},{16,0},... | collective-permute-start | bytes 442376 | tf_op jit(solution)/shard_map/ppermute | solution.py:19
  11.5 0.7 %copy-start.6 = (f32[1,16,96]{2,1,0:T(8,128)S(1)}, f32[1,16,96]{2,1,0:T(8,128)}, u32[]{:S(2)}) copy-start(f32[1,16,96]{2,1,0:T(8,128)} %refs_0_.3) | copy-start | bytes 18436
  12.2 0.7 copy-start.9
  12.8 20.7 %copy-start.5 = (f32[1,48,48]{2,1,0:T(8,128)S(1)}, f32[1,48,48]{2,1,0:T(8,128)}, u32[]{:S(2)}) copy-start(f32[1,48,48]{2,1,0:T(8,128)} %solver_ref.3) | copy-start | bytes 27652
  13.5 1.2 %collective-permute-start.4 = (f32[1,128]{1,0:T(1,128)S(1)}, f32[1,128]{1,0:T(1,128)S(1)}, u32[]{:S(2)}, u32[]{:S(2)}) collective-permute-start(f32[1,128]{1,0:T(1,128)S(1)} %restrict.1.refs_4_), channel_id=1, source_target_pairs={{0,1},{1,0},{2,3},{3,2},{4,5},{5,4},{6,7},{7,6},{8,9},{9,8},{10,11... | collective-permute-start | bytes 1544 | tf_op jit(solution)/shard_map/ppermute | solution.py:374
  16.9 2.3 %copy-start = (f32[1,16,6,96,96]{4,3,2,1,0:T(8,128)S(1)}, f32[1,16,6,96,96]{4,3,2,1,0:T(8,128)}, u32[]{:S(2)}) copy-start(f32[1,16,6,96,96]{4,3,2,1,0:T(8,128)} %refs_11_.3) | copy-start | bytes 10616836
  19.3 1.1 %copy-start.2 = (f32[1,16,96,96]{3,2,1,0:T(8,128)S(1)}, f32[1,16,96,96]{3,2,1,0:T(8,128)}, u32[]{:S(2)}) copy-start(f32[1,16,96,96]{3,2,1,0:T(8,128)} %inverse_ref.1) | copy-start | bytes 1769476
  20.4 0.7 %copy-start.4 = (f32[1,48,48]{2,1,0:T(8,128)S(1)}, f32[1,48,48]{2,1,0:T(8,128)}, u32[]{:S(2)}) copy-start(f32[1,48,48]{2,1,0:T(8,128)} %solver_ref.3) | copy-start | bytes 27652
  21.1 0.7 %copy-start.7 = (f32[1,16,96]{2,1,0:T(8,128)S(1)}, f32[1,16,96]{2,1,0:T(8,128)}, u32[]{:S(2)}) copy-start(f32[1,16,96]{2,1,0:T(8,128)} %refs_0_.3) | copy-start | bytes 18436
  21.8 0.7 copy-start.8
  22.5 0.7 copy-start.10
  23.2 7.8 %copy-start.1 = (f32[1,16,6,96,96]{4,3,2,1,0:T(8,128)S(1)}, f32[1,16,6,96,96]{4,3,2,1,0:T(8,128)}, u32[]{:S(2)}) copy-start(f32[1,16,6,96,96]{4,3,2,1,0:T(8,128)} %refs_11_.3) | copy-start | bytes 10616836
  25.0 4.1 %collective-permute-start.5 = (f32[8,96]{1,0:T(8,128)S(1)}, f32[8,96]{1,0:T(8,128)S(1)}, u32[]{:S(2)}, u32[]{:S(2)}) collective-permute-start(f32[8,96]{1,0:T(8,128)S(1)} %get-tuple-element.41), channel_id=1, source_target_pairs={{0,2},{2,0},{4,6},{6,4},{8,10},{10,8},{12,14},{14,12},{16,18},{18,... | collective-permute-start | bytes 9224 | tf_op jit(solution)/shard_map/ppermute | solution.py:19
  25.6 3.6 %collective-permute-start.6 = (f32[8,96]{1,0:T(8,128)S(1)}, f32[8,96]{1,0:T(8,128)S(1)}, u32[]{:S(2)}, u32[]{:S(2)}) collective-permute-start(f32[8,96]{1,0:T(8,128)S(1)} %get-tuple-element.42), channel_id=1, source_target_pairs={{0,4},{2,6},{4,0},{6,2},{8,12},{10,14},{12,8},{14,10},{16,20},{18,... | collective-permute-start | bytes 9224 | tf_op jit(solution)/shard_map/ppermute | solution.py:19
  26.1 3.6 %collective-permute-start.7 = (f32[8,96]{1,0:T(8,128)S(1)}, f32[8,96]{1,0:T(8,128)S(1)}, u32[]{:S(2)}, u32[]{:S(2)}) collective-permute-start(f32[8,96]{1,0:T(8,128)S(1)} %get-tuple-element.43), channel_id=1, source_target_pairs={{0,8},{2,10},{4,12},{6,14},{8,0},{10,2},{12,4},{14,6},{16,24},{18,... | collective-permute-start | bytes 9224 | tf_op jit(solution)/shard_map/ppermute | solution.py:19
  26.5 4.5 %collective-permute-start.8 = (f32[8,96]{1,0:T(8,128)S(1)}, f32[8,96]{1,0:T(8,128)S(1)}, u32[]{:S(2)}, u32[]{:S(2)}) collective-permute-start(f32[8,96]{1,0:T(8,128)S(1)} %get-tuple-element.44), channel_id=1, source_target_pairs={{0,16},{2,18},{4,20},{6,22},{8,24},{10,26},{12,28},{14,30},{16,0},... | collective-permute-start | bytes 9224 | tf_op jit(solution)/shard_map/ppermute | solution.py:19
  32.3 1.2 %collective-permute-start.9 = (f32[1,128]{1,0:T(1,128)S(1)}, f32[1,128]{1,0:T(1,128)S(1)}, u32[]{:S(2)}, u32[]{:S(2)}) collective-permute-start(f32[1,128]{1,0:T(1,128)S(1)} %get-tuple-element.49.mine_ref), channel_id=1, source_target_pairs={{0,1},{1,0},{2,3},{3,2},{4,5},{5,4},{6,7},{7,6},{8,9},{9,8},{10,11... | collective-permute-start | bytes 1544 | tf_op jit(solution)/shard_map/ppermute | solution.py:374
  35.0 5.8 %collective-permute-start.10 = (f32[8,96]{1,0:T(8,128)S(1)}, f32[8,96]{1,0:T(8,128)S(1)}, u32[]{:S(2)}, u32[]{:S(2)}) collective-permute-start(f32[8,96]{1,0:T(8,128)S(1)} %get-tuple-element.52), channel_id=1, source_target_pairs={{0,2},{2,0},{4,6},{6,4},{8,10},{10,8},{12,14},{14,12},{16,18},{18,... | collective-permute-start | bytes 9224 | tf_op jit(solution)/shard_map/ppermute | solution.py:19
  36.5 4.2 %collective-permute-start.11 = (f32[8,96]{1,0:T(8,128)S(1)}, f32[8,96]{1,0:T(8,128)S(1)}, u32[]{:S(2)}, u32[]{:S(2)}) collective-permute-start(f32[8,96]{1,0:T(8,128)S(1)} %get-tuple-element.53), channel_id=1, source_target_pairs={{0,4},{2,6},{4,0},{6,2},{8,12},{10,14},{12,8},{14,10},{16,20},{18,... | collective-permute-start | bytes 9224 | tf_op jit(solution)/shard_map/ppermute | solution.py:19
  38.1 3.6 %collective-permute-start.12 = (f32[8,96]{1,0:T(8,128)S(1)}, f32[8,96]{1,0:T(8,128)S(1)}, u32[]{:S(2)}, u32[]{:S(2)}) collective-permute-start(f32[8,96]{1,0:T(8,128)S(1)} %get-tuple-element.54), channel_id=1, source_target_pairs={{0,8},{2,10},{4,12},{6,14},{8,0},{10,2},{12,4},{14,6},{16,24},{18,... | collective-permute-start | bytes 9224 | tf_op jit(solution)/shard_map/ppermute | solution.py:19
  39.7 4.5 %collective-permute-start.13 = (f32[8,96]{1,0:T(8,128)S(1)}, f32[8,96]{1,0:T(8,128)S(1)}, u32[]{:S(2)}, u32[]{:S(2)}) collective-permute-start(f32[8,96]{1,0:T(8,128)S(1)} %get-tuple-element.55), channel_id=1, source_target_pairs={{0,16},{2,18},{4,20},{6,22},{8,24},{10,26},{12,28},{14,30},{16,0},... | collective-permute-start | bytes 9224 | tf_op jit(solution)/shard_map/ppermute | solution.py:19
  45.6 1.2 %collective-permute-start.14 = (f32[1,128]{1,0:T(1,128)S(1)}, f32[1,128]{1,0:T(1,128)S(1)}, u32[]{:S(2)}, u32[]{:S(2)}) collective-permute-start(f32[1,128]{1,0:T(1,128)S(1)} %get-tuple-element.59.mine_ref), channel_id=1, source_target_pairs={{0,1},{1,0},{2,3},{3,2},{4,5},{5,4},{6,7},{7,6},{8,9},{9,8},{10,11... | collective-permute-start | bytes 1544 | tf_op jit(solution)/shard_map/ppermute | solution.py:374
  48.2 4.1 %collective-permute-start.15 = (f32[8,96]{1,0:T(8,128)S(1)}, f32[8,96]{1,0:T(8,128)S(1)}, u32[]{:S(2)}, u32[]{:S(2)}) collective-permute-start(f32[8,96]{1,0:T(8,128)S(1)} %get-tuple-element.62), channel_id=1, source_target_pairs={{0,2},{2,0},{4,6},{6,4},{8,10},{10,8},{12,14},{14,12},{16,18},{18,... | collective-permute-start | bytes 9224 | tf_op jit(solution)/shard_map/ppermute | solution.py:19
  48.8 3.6 %collective-permute-start.16 = (f32[8,96]{1,0:T(8,128)S(1)}, f32[8,96]{1,0:T(8,128)S(1)}, u32[]{:S(2)}, u32[]{:S(2)}) collective-permute-start(f32[8,96]{1,0:T(8,128)S(1)} %get-tuple-element.63), channel_id=1, source_target_pairs={{0,4},{2,6},{4,0},{6,2},{8,12},{10,14},{12,8},{14,10},{16,20},{18,... | collective-permute-start | bytes 9224 | tf_op jit(solution)/shard_map/ppermute | solution.py:19
  49.3 3.6 %collective-permute-start.17 = (f32[8,96]{1,0:T(8,128)S(1)}, f32[8,96]{1,0:T(8,128)S(1)}, u32[]{:S(2)}, u32[]{:S(2)}) collective-permute-start(f32[8,96]{1,0:T(8,128)S(1)} %get-tuple-element.64), channel_id=1, source_target_pairs={{0,8},{2,10},{4,12},{6,14},{8,0},{10,2},{12,4},{14,6},{16,24},{18,... | collective-permute-start | bytes 9224 | tf_op jit(solution)/shard_map/ppermute | solution.py:19
  49.7 4.5 %collective-permute-start.18 = (f32[8,96]{1,0:T(8,128)S(1)}, f32[8,96]{1,0:T(8,128)S(1)}, u32[]{:S(2)}, u32[]{:S(2)}) collective-permute-start(f32[8,96]{1,0:T(8,128)S(1)} %get-tuple-element.65), channel_id=1, source_target_pairs={{0,16},{2,18},{4,20},{6,22},{8,24},{10,26},{12,28},{14,30},{16,0},... | collective-permute-start | bytes 9224 | tf_op jit(solution)/shard_map/ppermute | solution.py:19

commit v2 on v1

v2 whole, which is shorter than its diff:
```python
import functools

import jax
import jax.numpy as jnp
from jax import lax
from jax.experimental import pallas as pl
from jax.experimental.pallas import tpu as pltpu
from jax.sharding import PartitionSpec as P

ITERS = 3
SHIFT = 2.0
REPEATS = 16

f32 = jnp.float32
bf16 = jnp.bfloat16
VMEM = pl.BlockSpec(memory_space=pltpu.VMEM)
ANY = pl.BlockSpec(memory_space=pl.ANY)
SMEM = pl.BlockSpec(memory_space=pltpu.SMEM)


def partner(array, axis, bit):
    return lax.ppermute(array, axis, [(i, i ^ 1 << bit) for i in range(lax.axis_size(axis))])


def call(kernel, outs, in_specs, args, scratch=(), name=None, cost=100000):
    return pl.pallas_call(
        kernel,
        out_shape=[
            jax.ShapeDtypeStruct(*(out if isinstance(out[0], tuple) else (out, f32))) for out in outs
        ],
        in_specs=in_specs,
        out_specs=[VMEM] * len(outs),
        scratch_shapes=list(scratch),
        compiler_params=pltpu.CompilerParams(vmem_limit_bytes=12 * 1024 * 1024),
        cost_estimate=pl.CostEstimate(flops=0, bytes_accessed=cost, transcendentals=0),
        name=name,
    )(*args)


def eye_mask(width):
    return lax.broadcasted_iota(jnp.int32, (width, width), 0) == lax.broadcasted_iota(
        jnp.int32, (width, width), 1
    )


def to_column(row, eye):
    return jnp.sum(jnp.where(eye, row, 0.0), axis=1, keepdims=True)


def to_row(column, eye):
    return jnp.sum(jnp.where(eye, column, 0.0), axis=0, keepdims=True)


def restrict(null_ref, offset_ref, field):
    offset = offset_ref[...]
    total = jnp.zeros(offset.shape, f32)
    for mode in range(null_ref.shape[1]):
        dots = jnp.sum(null_ref[0, mode] * field, axis=1, keepdims=True)
        total = total + jnp.where(offset == mode, dots, 0.0)
    return jnp.sum(total, axis=0, keepdims=True)


def coarse_field(mine_ref, theirs_ref, solver_ref, null_ref, offset_ref):
    size = solver_ref.shape[1]
    total = mine_ref[...] + theirs_ref[...]
    solved = jnp.sum(solver_ref[0] * total[:, :size], axis=1, keepdims=True)
    flat = to_row(solved, eye_mask(size))
    offset = offset_ref[:, :size]
    field = None
    for mode in range(null_ref.shape[1]):
        weight = jnp.sum(jnp.where(offset == mode, flat, 0.0), axis=1, keepdims=True)
        term = null_ref[0, mode] * weight
        field = term if field is None else field + term
    return field


def thirds(value):
    high = value.astype(bf16)
    rest = value - high.astype(f32)
    middle = rest.astype(bf16)
    low = (rest - middle.astype(f32)).astype(bf16)
    return jnp.concatenate([high, middle, low], axis=0)


def select_rows(table_ref, value):
    return jnp.dot(table_ref[...], thirds(value), preferred_element_type=f32)


def triple(table):
    return jnp.concatenate([table.astype(bf16)] * 3, axis=1)


def pack_kernel(margin_ref, *refs):
    outs = refs[REPEATS:]
    turns = len(outs)
    ghosts = margin_ref.shape[1] // turns
    width = margin_ref.shape[2]
    tall = width * width // 128
    side = 128 - width
    rest = width - tall
    for turn in range(turns):
        for g in range(ghosts):
            block = margin_ref[0, turn * ghosts + g]
            outs[turn][g, :, 0:width] = block[:tall]
            for piece in range(width // side):
                outs[turn][g, piece * rest : (piece + 1) * rest, width:128] = block[
                    tall:, piece * side : (piece + 1) * side
                ]


def restrict_kernel(field_ref, null_ref, aggregate_ref, offset_ref, mine_ref):
    modes = null_ref.shape[1]
    lane = lax.broadcasted_iota(jnp.int32, (1, 128), 1)
    for i in range(offset_ref.shape[0]):
        offset_ref[i : i + 1, :] = lane - aggregate_ref[0, i] * modes
    mine_ref[...] = restrict(null_ref, offset_ref, field_ref[0])


def table_kernel(
    pattern_ref, senders_ref, pick_ref, spread_ref, send_ref, back_ref, table_ref, send_table_ref
):
    slots, _, rows = pattern_ref.shape
    turns, ghosts = senders_ref.shape[1:]
    extent = pick_ref.shape[1] // 3
    lane = lax.broadcasted_iota(jnp.int32, (1, 128), 1)
    for i in range(rows):
        for j in range(slots):
            at = i * slots + j
            table_ref[at : at + 1, :] = jnp.where(lane == pattern_ref[j, 0, i], 1.0, 0.0)
    for turn in range(turns):
        for g in range(ghosts):
            at = turn * ghosts + g
            send_table_ref[at : at + 1, :] = jnp.where(lane == senders_ref[0, turn, g], 1.0, 0.0)
    table = table_ref[...]
    pick_ref[...] = triple(table[:, :extent])
    spread_ref[...] = triple(table.T[:extent])
    send_table = send_table_ref[...]
    send_ref[...] = triple(send_table[:, :rows])
    back_ref[...] = triple(send_table.T[:rows])


def local_kernel(field_ref, inverse_ref, column_ref, row_ref):
    rows, width = field_ref.shape
    eye = eye_mask(width)
    for i in range(rows):
        column = jnp.sum(inverse_ref[i] * field_ref[i : i + 1, :], axis=1, keepdims=True)
        column_ref[i] = jnp.broadcast_to(column, (width, 128))
        row_ref[i : i + 1, :] = to_row(column, eye)


def spread_block_row(blocks_ref, parts_ref, i, column):
    slots = blocks_ref.shape[2]
    for j in range(slots):
        at = i * slots + j
        parts_ref[at : at + 1, :] = jnp.sum(blocks_ref[0, i, j] * column, axis=0, keepdims=True)


def finish_spread(parts_ref, spread_ref, send_ref, z, own_ref, packets):
    turns = len(packets)
    rows = z.shape[0]
    sent = select_rows(send_ref, z)
    spread = select_rows(spread_ref, parts_ref[...])
    own_ref[...] = spread[:rows]
    ghosts = sent.shape[0] // turns
    for turn in range(turns):
        start = turn * ghosts
        packets[turn][0:ghosts, :] = sent[start : start + ghosts]
        packets[turn][ghosts:, :] = spread[rows + start : rows + start + ghosts]


def first_kernel(turns, field_ref, inverse_ref, *refs):
    gathered = refs[:turns][::-1]
    (
        mine_ref,
        theirs_ref,
        solver_ref,
        null_ref,
        offset_ref,
        blocks_ref,
        spread_ref,
        send_ref,
        senders_ref,
        combined_ref,
        z_ref,
        own_ref,
    ) = refs[turns : turns + 12]
    packets = refs[turns + 12 : 2 * turns + 12]
    (parts_ref,) = refs[2 * turns + 12 :]
    rows, width = z_ref.shape
    tall = width * width // 128
    side = 128 - width
    rest = width - tall
    ghosts = senders_ref.shape[2]
    eye = eye_mask(width)
    combined_ref[...] = inverse_ref[0]
    for turn in range(turns):
        for g in range(ghosts):
            at = senders_ref[0, turn, g]
            combined_ref[at, 0:tall, :] += gathered[turn][g, :, 0:width]
            for piece in range(width // side):
                combined_ref[at, tall:, piece * side : (piece + 1) * side] += gathered[turn][
                    g, piece * rest : (piece + 1) * rest, width:128
                ]
    coarse = coarse_field(mine_ref, theirs_ref, solver_ref, null_ref, offset_ref)
    for i in range(rows):
        product = combined_ref[i] * field_ref[0, i : i + 1, :] + jnp.where(eye, coarse[i : i + 1], 0.0)
        column = jnp.sum(product, axis=1, keepdims=True)
        z_ref[i : i + 1, :] = to_row(column, eye)
        spread_block_row(blocks_ref, parts_ref, i, column)
    finish_spread(parts_ref, spread_ref, send_ref, z_ref[...], own_ref, packets)


def spread_kernel(
    turns,
    column_ref,
    row_ref,
    mine_ref,
    theirs_ref,
    solver_ref,
    null_ref,
    offset_ref,
    blocks_ref,
    spread_ref,
    send_ref,
    z_ref,
    own_ref,
    *refs,
):
    packets = refs[:turns]
    (parts_ref,) = refs[turns:]
    rows, width = z_ref.shape
    eye = eye_mask(width)
    coarse = coarse_field(mine_ref, theirs_ref, solver_ref, null_ref, offset_ref)
    z = row_ref[...] + coarse
    z_ref[...] = z
    for i in range(rows):
        column = column_ref[i][:, :width] + to_column(coarse[i : i + 1], eye)
        spread_block_row(blocks_ref, parts_ref, i, column)
    finish_spread(parts_ref, spread_ref, send_ref, z, own_ref, packets)


def apply_rows(arrived, z, own_ref, blocks_ref, pick_ref, back_ref, picked_ref):
    rows, width = z.shape
    slots = blocks_ref.shape[2]
    ghosts = arrived[0].shape[0] // 2
    eye = eye_mask(width)
    extended = jnp.concatenate([z] + [ref[0:ghosts, :] for ref in arrived], axis=0)
    picked_ref[...] = select_rows(pick_ref, extended)
    returned = jnp.concatenate([ref[ghosts:, :] for ref in arrived], axis=0)
    back = own_ref[...] + select_rows(back_ref, returned)
    image = []
    for i in range(rows):
        total = None
        for j in range(slots):
            at = i * slots + j
            term = blocks_ref[0, i, j] * picked_ref[at : at + 1, :]
            total = term if total is None else total + term
        column = jnp.sum(total, axis=1, keepdims=True)
        image.append(to_row(column, eye))
    return 0.5 * (jnp.concatenate(image, axis=0) + back)


def apply_kernel(turns, field_ref, z_ref, own_ref, *refs):
    arrived = refs[:turns]
    (
        blocks_ref,
        pick_ref,
        back_ref,
        null_ref,
        offset_ref,
        next_ref,
        coarse_ref,
        picked_ref,
    ) = refs[turns:]
    image = apply_rows(arrived, z_ref[...], own_ref, blocks_ref, pick_ref, back_ref, picked_ref)
    following = image - SHIFT * field_ref[...].reshape(image.shape)
    next_ref[...] = following
    coarse_ref[...] = restrict(null_ref, offset_ref, following)


def last_kernel(turns, fields, *refs):
    field_refs = refs[:fields]
    z_refs = refs[fields : 2 * fields]
    own_ref = refs[2 * fields]
    arrived = refs[2 * fields + 1 : 2 * fields + 1 + turns]
    blocks_ref, pick_ref, back_ref, next_ref, dots_ref, picked_ref = refs[2 * fields + 1 + turns :]
    image = apply_rows(
        arrived, z_refs[-1][...], own_ref, blocks_ref, pick_ref, back_ref, picked_ref
    )
    following = image - SHIFT * field_refs[-1][...]
    next_ref[...] = following
    lane = lax.broadcasted_iota(jnp.int32, (1, 128), 1)
    values = [ref[...].reshape(image.shape) for ref in field_refs] + [following]
    packed = jnp.zeros((1, 128), f32)
    for a, value in enumerate(values):
        for c, z_at in enumerate(z_refs):
            column = jnp.sum(value * z_at[...], axis=0, keepdims=True)
            dot = jnp.sum(column, axis=1, keepdims=True)
            packed = jnp.where(lane == a * fields + c, dot, packed)
    dots_ref[...] = jnp.broadcast_to(packed.reshape(1, 1, 128), dots_ref.shape)


def finish_kernel(fields, dots_ref, *refs):
    value_refs = refs[: fields + 1]
    z_refs = refs[fields + 1 : 2 * fields + 1]
    solution_ref, residual_ref = refs[2 * fields + 1 :]
    total = jnp.sum(dots_ref[...], axis=0)
    lane = lax.broadcasted_iota(jnp.int32, (1, 128), 1)
    shape = solution_ref.shape[1:]
    gram = [
        [
            jnp.sum(jnp.where(lane == a * fields + c, total, 0.0), axis=1, keepdims=True)
            for c in range(fields)
        ]
        for a in range(fields + 1)
    ]
    zero = jnp.zeros((1, 1), f32)
    one = jnp.ones((1, 1), f32)

    def form(left, right):
        value = zero
        for a, left_at in enumerate(left):
            if left_at is None:
                continue
            for c, right_at in enumerate(right):
                if right_at is not None:
                    value = value + left_at * right_at * gram[a][c]
        return value

    def plus(first, second):
        if first is None:
            return second
        return first if second is None else first + second

    def scaled(scale, value):
        return None if value is None else scale * value

    residual = [one] + [None] * fields
    direction = [one] + [None] * (fields - 1)
    iterate = [None] * fields
    product_now = form(residual, direction)
    for step in range(fields):
        image = [None] * (fields + 1)
        for c in range(fields):
            if direction[c] is not None:
                image[c] = plus(image[c], SHIFT * direction[c])
                image[c + 1] = plus(image[c + 1], direction[c])
        alpha = product_now / form(image, direction)
        iterate = [plus(iterate[c], scaled(alpha, direction[c])) for c in range(fields)]
        residual = [plus(residual[a], scaled(-alpha, image[a])) for a in range(fields + 1)]
        if step + 1 < fields:
            product_next = form(residual, residual[:fields])
            beta = product_next / product_now
            direction = [plus(residual[c], scaled(beta, direction[c])) for c in range(fields)]
            product_now = product_next
    answer = iterate[0] * z_refs[0][...]
    for c in range(1, fields):
        answer = answer + iterate[c] * z_refs[c][...]
    left_over = residual[0] * value_refs[0][...].reshape(shape)
    for a in range(1, fields + 1):
        left_over = left_over + residual[a] * value_refs[a][...]
    solution_ref[0] = answer
    residual_ref[0] = left_over


def on_device(
    right_side,
    blocks,
    pattern,
    send_rows,
    inverse_blocks,
    margin_blocks,
    near_null,
    aggregate,
    coarse_inverse,
):
    rows, width = right_side.shape[1:]
    slots = blocks.shape[2]
    turns, ghosts = send_rows.shape[1:]
    extent = rows + turns * ghosts
    modes = near_null.shape[2]
    levels = lax.axis_size("sub").bit_length() - 1
    bits = [turn * levels // turns for turn in range(turns)]
    devices = lax.axis_size("sub") * lax.axis_size("coarse")
    flip = [(0, 1), (1, 0)]
    row_shape = (rows, width)
    packet = (2 * ghosts, width)
    parts = rows * slots
    ghost_total = turns * ghosts
    parts_scratch = [pltpu.VMEM((parts, width), f32)]
    null_view = jnp.transpose(near_null, (0, 2, 1, 3))
    pattern_view = jnp.transpose(pattern, (2, 0, 1))

    def swap(array):
        return lax.ppermute(array, "coarse", flip)

    packs = call(
        pack_kernel,
        [(ghosts, width * width // 128, 128)] * turns,
        [VMEM] + [ANY] * REPEATS,
        [margin_blocks] * (1 + REPEATS),
        name="pack_margin",
    )
    gathered = [partner(packs[turn], "sub", bits[turn]) for turn in range(turns)]
    offset, mine = call(
        restrict_kernel,
        [((rows, 128), jnp.int32), (1, 128)],
        [VMEM, VMEM, SMEM],
        [right_side, null_view, aggregate],
        name="restrict",
    )
    theirs = swap(mine)
    pick, spread, send, back = call(
        table_kernel,
        [
            ((parts, 3 * extent), bf16),
            ((extent, 3 * parts), bf16),
            ((ghost_total, 3 * rows), bf16),
            ((rows, 3 * ghost_total), bf16),
        ],
        [SMEM, SMEM],
        [pattern_view, send_rows],
        scratch=[pltpu.VMEM((parts, 128), f32), pltpu.VMEM((ghost_total, 128), f32)],
        name="tables",
    )
    source, null_modes, held, solver = right_side, null_view, blocks, coarse_inverse
    combined, z, own, *packets = call(
        functools.partial(first_kernel, turns),
        [(rows, width, width), row_shape, row_shape] + [packet] * turns,
        [VMEM] * (turns + 10) + [SMEM],
        [source, inverse_blocks, *gathered[::-1], mine, theirs, solver, null_modes, offset, held, spread, send]
        + [send_rows],
        scratch=parts_scratch,
        name="first_spread",
    )
    values = [source]
    fields = [z]
    for step in range(ITERS):
        arrived = [partner(packets[turn], "sub", bits[turn]) for turn in range(turns)]
        if step + 1 == ITERS:
            break
        following, mine = call(
            functools.partial(apply_kernel, turns),
            [row_shape, (1, 128)],
            [VMEM] * (turns + 8),
            [values[-1], fields[-1], own, *arrived, held, pick, back, null_modes, offset],
            scratch=parts_scratch,
            name="apply",
        )
        values.append(following)
        theirs = swap(mine)
        column, row = call(
            local_kernel,
            [(rows, width, 128), row_shape],
            [VMEM, VMEM],
            [following, combined],
            name="local_inverse",
        )
        z, own, *packets = call(
            functools.partial(spread_kernel, turns),
            [row_shape, row_shape] + [packet] * turns,
            [VMEM] * 10,
            [column, row, mine, theirs, solver, null_modes, offset, held, spread, send],
            scratch=parts_scratch,
            name="spread",
        )
        fields.append(z)
    following, dots = call(
        functools.partial(last_kernel, turns, ITERS),
        [row_shape, (devices, 1, 128)],
        [VMEM] * (2 * ITERS + 1 + turns + 3),
        [*values, *fields, own, *arrived, held, pick, back],
        scratch=parts_scratch,
        name="last_apply",
    )
    values.append(following)
    exchanged = lax.all_to_all(dots, ("sub", "coarse"), 0, 0)
    answer, left_over = call(
        functools.partial(finish_kernel, ITERS),
        [right_side.shape] * 2,
        [VMEM] * (2 * ITERS + 2),
        [exchanged, *values, *fields],
        name="finish",
    )
    return answer, left_over


def solution(mesh):
    in_specs = (
        P("coarse", "sub", None),
        P("coarse", "sub", None, None, None),
        P("coarse", "sub", None),
        P("coarse", "sub", None),
        P("coarse", "sub", None, None),
        P("coarse", "sub", None, None),
        P("coarse", "sub", None, None),
        P("coarse", "sub"),
        P("sub", None, None),
    )
    out_specs = (P("coarse", "sub", None), P("coarse", "sub", None))
    return jax.shard_map(
        on_device, mesh=mesh, in_specs=in_specs, out_specs=out_specs, check_vma=False
    )
```

time: 68.8 us -> 57 us (0.83)
  local copies, waits for them, and re-layouts: 10.3 us -> 1.16 us
  blocking collectives: 11.9 us -> 9.63 us
  Pallas kernels: 11 us -> 9.2 us
  starting transfers between devices: 22.9 us -> 24.3 us
    unnamed x24 -> x18, local copies, waits for them, and re-layouts: 10.3 us -> 1.16 us
    all_to_all x1, blocking collectives: 11.9 us -> 9.63 us  [on_device(): exchanged = lax.all_to_all(dots, ('sub', 'coarse'), 0, 0)]
    pallas_call x11 -> x12, Pallas kernels: 11 us -> 9.2 us  [call(): pl.pallas_call(kernel, out_shape=[jax.ShapeDtypeStruct(*(out if isinstanc...]
    ppermute x16, starting transfers between devices: 22.7 us -> 24.1 us  [partner(): lax.ppermute(array, axis, [(i, i ^ 1 << bit) for i in range(lax.axis_size...]
  transfers between devices with their start and end apart: 19 -> 19, of which waited for: 12 -> 12; matrix products, arithmetic and copies ran while one was open for 2% -> 0% of each run, Pallas kernels for 2% -> 4%
where the time goes in v2:
time: 57 us; the launch traced here: 56.8 us
  starting transfers between devices  24.3 us (43%)
  waiting for transfers between devices  11.8 us (21%)
  blocking collectives  9.63 us (17%)
  Pallas kernels  9.2 us (16%)
  local copies, waits for them, and re-layouts  1.16 us (2%)
  between operations  0.8 us (1%)
    ppermute x16, starting transfers between devices, partner(): lax.ppermute(array, axis, [(i, i ^ 1 << bit) for i in range(lax.axis_size...  24.1 us
    ppermute x16, waiting for transfers between devices, partner(): lax.ppermute(array, axis, [(i, i ^ 1 << bit) for i in range(lax.axis_size...  9.83 us
    all_to_all x1, blocking collectives, on_device(): exchanged = lax.all_to_all(dots, ('sub', 'coarse'), 0, 0)  9.63 us
    pallas_call x12, Pallas kernels, call(): pl.pallas_call(kernel, out_shape=[jax.ShapeDtypeStruct(*(out if isinstanc...  9.2 us
    ppermute x3, waiting for transfers between devices, swap(): return lax.ppermute(array, 'coarse', flip)  1.93 us
    unnamed x18, local copies, waits for them, and re-layouts  1.16 us
  transfers between devices with their start and end apart: 19, of which 12 were waited for; matrix products, arithmetic and copies ran while one was open for 0% of the time, Pallas kernels for 4%

profile of v2, /device:TPU:0, one launch (start us, length us, event | category | flops | bytes accessed | tf_op | source)
XLA Modules:
  0.0 56.8 jit_solution(11934038657665535139)
XLA Ops:
  0.6 1.1 %copy-done = f32[1,16,96,96]{3,2,1,0:T(8,128)S(1)} copy-done((f32[1,16,96,96]{3,2,1,0:T(8,128)S(1)}, f32[1,16,96,96]{3,2,1,0:T(8,128)}, u32[]{:S(2)}) %copy-start) | copy-done | bytes 589848
  1.8 0.2 pack_margin.1
  2.0 4.1 %collective-permute-start = (f32[4,72,128]{2,1,0:T(8,128)S(1)}, f32[4,72,128]{2,1,0:T(8,128)S(1)}, u32[]{:S(2)}, u32[]{:S(2)}) collective-permute-start(f32[4,72,128]{2,1,0:T(8,128)S(1)} %get-tuple-element.41), channel_id=1, source_target_pairs={{0,16},{2,18},{4,20},{6,22},{8,24},{10,26},{12,28},{14,30},{16,0},... | collective-permute-start | bytes 442376 | tf_op jit(solution)/shard_map/ppermute | solution.py:22
  6.1 1.6 %collective-permute-start.1 = (f32[4,72,128]{2,1,0:T(8,128)S(1)}, f32[4,72,128]{2,1,0:T(8,128)S(1)}, u32[]{:S(2)}, u32[]{:S(2)}) collective-permute-start(f32[4,72,128]{2,1,0:T(8,128)S(1)} %get-tuple-element.42), channel_id=1, source_target_pairs={{0,8},{2,10},{4,12},{6,14},{8,0},{10,2},{12,4},{14,6},{16,24},{18,... | collective-permute-start | bytes 442376 | tf_op jit(solution)/shard_map/ppermute | solution.py:22
  7.7 1.5 %collective-permute-start.2 = (f32[4,72,128]{2,1,0:T(8,128)S(1)}, f32[4,72,128]{2,1,0:T(8,128)S(1)}, u32[]{:S(2)}, u32[]{:S(2)}) collective-permute-start(f32[4,72,128]{2,1,0:T(8,128)S(1)} %get-tuple-element.43), channel_id=1, source_target_pairs={{0,4},{2,6},{4,0},{6,2},{8,12},{10,14},{12,8},{14,10},{16,20},{18,... | collective-permute-start | bytes 442376 | tf_op jit(solution)/shard_map/ppermute | solution.py:22
  9.2 1.5 %collective-permute-start.3 = (f32[4,72,128]{2,1,0:T(8,128)S(1)}, f32[4,72,128]{2,1,0:T(8,128)S(1)}, u32[]{:S(2)}, u32[]{:S(2)}) collective-permute-start(f32[4,72,128]{2,1,0:T(8,128)S(1)} %get-tuple-element.44), channel_id=1, source_target_pairs={{0,2},{2,0},{4,6},{6,4},{8,10},{10,8},{12,14},{14,12},{16,18},{18,... | collective-permute-start | bytes 442376 | tf_op jit(solution)/shard_map/ppermute | solution.py:22
  10.7 0.6 %restrict.1 = (s32[16,128]{1,0:T(8,128)S(1)}, f32[1,128]{1,0:T(1,128)S(1)}) custom-call(f32[1,16,96]{2,1,0:T(8,128)S(1)} %copy-done.5, f32[1,6,16,96]{3,2,1,0:T(8,128)S(1)} %bitcast.2, s32[1,16]{1,0:T(1,128)S(1)} %copy-done.8), custom_call_target="tpu_custom_call" | custom-call | bytes 100000 | tf_op jit(solution)/shard_map/restrict/pallas_call | solution.py:26
  11.4 0.1 collective-permute-start.4
  11.5 0.8 %tables.1 = (bf16[96,96]{1,0:T(8,128)(2,1)S(1)}, bf16[32,288]{1,0:T(8,128)(2,1)S(1)}, bf16[16,48]{1,0:T(8,128)(2,1)S(1)}, bf16[16,48]{1,0:T(8,128)(2,1)S(1)}) custom-call(s32[6,1,16]{2,1,0:T(1,128)S(1)} %bitcast.8, s32[1,4,4]{2,1,0:T(4,128)S(1)} %copy-done.6), custom_call_target="tpu_custom_call" | custom-call | bytes 100000 | tf_op jit(solution)/shard_map/tables/pallas_call | solution.py:26
  12.3 0.3 collective-permute-done.4.refs_5_
  12.6 0.7 %collective-permute-done.refs_0_ = f32[4,72,128]{2,1,0:T(8,128)S(1)} collective-permute-done((f32[4,72,128]{2,1,0:T(8,128)S(1)}, f32[4,72,128]{2,1,0:T(8,128)S(1)}, u32[]{:S(2)}, u32[]{:S(2)}) %collective-permute-start) | collective-permute-done | bytes 147488 | tf_op jit(solution)/shard_map/ppermute | solution.py:22
  13.3 0.2 collective-permute-done.1.refs_1_
  13.4 0.0 collective-permute-done.2.refs_2_
  13.5 0.9 %collective-permute-done.3.refs_3_ = f32[4,72,128]{2,1,0:T(8,128)S(1)} collective-permute-done((f32[4,72,128]{2,1,0:T(8,128)S(1)}, f32[4,72,128]{2,1,0:T(8,128)S(1)}, u32[]{:S(2)}, u32[]{:S(2)}) %collective-permute-start.3) | collective-permute-done | bytes 147488 | tf_op jit(solution)/shard_map/ppermute | solution.py:22
  14.4 2.0 %first_spread.1 = (f32[16,96,96]{2,1,0:T(8,128)S(1)}, f32[16,96]{1,0:T(8,128)S(1)}, f32[16,96]{1,0:T(8,128)S(1)}, f32[8,96]{1,0:T(8,128)S(1)}, f32[8,96]{1,0:T(8...) custom-call(f32[1,16,96]{2,1,0:T(8,128)S(1)} %copy-done.5, f32[1,16,96,96]{3,2,1,0:T(8,128)S(1)} %copy-done.3, ...), custom_call_target="tpu_custom_call" | custom-call | bytes 100000 | tf_op jit(solution)/shard_map/first_spread/pallas_call | solution.py:26
  16.4 1.6 %collective-permute-start.5 = (f32[8,96]{1,0:T(8,128)S(1)}, f32[8,96]{1,0:T(8,128)S(1)}, u32[]{:S(2)}, u32[]{:S(2)}) collective-permute-start(f32[8,96]{1,0:T(8,128)S(1)} %get-tuple-element.51), channel_id=1, source_target_pairs={{0,2},{2,0},{4,6},{6,4},{8,10},{10,8},{12,14},{14,12},{16,18},{18,... | collective-permute-start | bytes 9224 | tf_op jit(solution)/shard_map/ppermute | solution.py:22
  18.0 0.7 %collective-permute-start.6 = (f32[8,96]{1,0:T(8,128)S(1)}, f32[8,96]{1,0:T(8,128)S(1)}, u32[]{:S(2)}, u32[]{:S(2)}) collective-permute-start(f32[8,96]{1,0:T(8,128)S(1)} %get-tuple-element.52), channel_id=1, source_target_pairs={{0,4},{2,6},{4,0},{6,2},{8,12},{10,14},{12,8},{14,10},{16,20},{18,... | collective-permute-start | bytes 9224 | tf_op jit(solution)/shard_map/ppermute | solution.py:22
  18.6 1.4 %collective-permute-start.7 = (f32[8,96]{1,0:T(8,128)S(1)}, f32[8,96]{1,0:T(8,128)S(1)}, u32[]{:S(2)}, u32[]{:S(2)}) collective-permute-start(f32[8,96]{1,0:T(8,128)S(1)} %get-tuple-element.53), channel_id=1, source_target_pairs={{0,8},{2,10},{4,12},{6,14},{8,0},{10,2},{12,4},{14,6},{16,24},{18,... | collective-permute-start | bytes 9224 | tf_op jit(solution)/shard_map/ppermute | solution.py:22
  20.1 2.3 %collective-permute-start.8 = (f32[8,96]{1,0:T(8,128)S(1)}, f32[8,96]{1,0:T(8,128)S(1)}, u32[]{:S(2)}, u32[]{:S(2)}) collective-permute-start(f32[8,96]{1,0:T(8,128)S(1)} %get-tuple-element.54), channel_id=1, source_target_pairs={{0,16},{2,18},{4,20},{6,22},{8,24},{10,26},{12,28},{14,30},{16,0},... | collective-permute-start | bytes 9224 | tf_op jit(solution)/shard_map/ppermute | solution.py:22
  22.4 0.0 collective-permute-done.6.refs_1_
  22.4 0.0 collective-permute-done.7.refs_2_
  22.4 2.2 %collective-permute-done.8.refs_3_ = f32[8,96]{1,0:T(8,128)S(1)} collective-permute-done((f32[8,96]{1,0:T(8,128)S(1)}, f32[8,96]{1,0:T(8,128)S(1)}, u32[]{:S(2)}, u32[]{:S(2)}) %collective-permute-start.8) | collective-permute-done | bytes 3104 | tf_op jit(solution)/shard_map/ppermute | solution.py:22
  24.6 0.7 %apply.2 = (f32[16,96]{1,0:T(8,128)S(1)}, f32[1,128]{1,0:T(1,128)S(1)}) custom-call(f32[1,16,96]{2,1,0:T(8,128)S(1)} %copy-done.5, f32[16,96]{1,0:T(8,128)S(1)} %get-tuple-element.49.z_ref.refs_3_.refs_4_, f32[16,96]{1,0:T(8,128)S(1)} %get-tuple-element.50.own_ref, f32[8,96]{1,0:T(8,128)S(1)} %collective-permute-done.5.refs_0_, ...), custom_call_target="tpu_custom_call" | custom-call | bytes 100000 | tf_op jit(solution)/shard_map/apply/pallas_call | solution.py:26
  25.3 0.1 collective-permute-start.9
  25.4 0.3 local_inverse.2
  25.6 0.8 %collective-permute-done.9.theirs_ref = f32[1,128]{1,0:T(1,128)S(1)} collective-permute-done((f32[1,128]{1,0:T(1,128)S(1)}, f32[1,128]{1,0:T(1,128)S(1)}, u32[]{:S(2)}, u32[]{:S(2)}) %collective-permute-start.9) | collective-permute-done | bytes 544 | tf_op jit(solution)/shard_map/ppermute | solution.py:395
  26.5 1.1 %spread.2 = (f32[16,96]{1,0:T(8,128)S(1)}, f32[16,96]{1,0:T(8,128)S(1)}, f32[8,96]{1,0:T(8,128)S(1)}, f32[8,96]{1,0:T(8,128)S(1)}, f32[8,96]{1,0:T(8,128)S(1)}, /*index=5*/f32[8,96]{1,0:T(8,128)S(1)}) custom-call(f32[16,96,128]{2,1,0:T(8,128)S(1)} %get-tuple-element.59.column_ref, f32[16,96]{1,0:T(8,128)S(1)} %get-tuple-element.60.row_ref, ...), custom_call_target="tpu_custom_call" | custom-call | bytes 100000 | tf_op jit(solution)/shard_map/spread/pallas_call | solution.py:26
  27.5 0.6 %collective-permute-start.10 = (f32[8,96]{1,0:T(8,128)S(1)}, f32[8,96]{1,0:T(8,128)S(1)}, u32[]{:S(2)}, u32[]{:S(2)}) collective-permute-start(f32[8,96]{1,0:T(8,128)S(1)} %get-tuple-element.64), channel_id=1, source_target_pairs={{0,2},{2,0},{4,6},{6,4},{8,10},{10,8},{12,14},{14,12},{16,18},{18,... | collective-permute-start | bytes 9224 | tf_op jit(solution)/shard_map/ppermute | solution.py:22
  28.1 0.5 collective-permute-start.11
  28.6 1.5 %collective-permute-start.12 = (f32[8,96]{1,0:T(8,128)S(1)}, f32[8,96]{1,0:T(8,128)S(1)}, u32[]{:S(2)}, u32[]{:S(2)}) collective-permute-start(f32[8,96]{1,0:T(8,128)S(1)} %get-tuple-element.66), channel_id=1, source_target_pairs={{0,8},{2,10},{4,12},{6,14},{8,0},{10,2},{12,4},{14,6},{16,24},{18,... | collective-permute-start | bytes 9224 | tf_op jit(solution)/shard_map/ppermute | solution.py:22
  30.1 0.9 %collective-permute-start.13 = (f32[8,96]{1,0:T(8,128)S(1)}, f32[8,96]{1,0:T(8,128)S(1)}, u32[]{:S(2)}, u32[]{:S(2)}) collective-permute-start(f32[8,96]{1,0:T(8,128)S(1)} %get-tuple-element.67), channel_id=1, source_target_pairs={{0,16},{2,18},{4,20},{6,22},{8,24},{10,26},{12,28},{14,30},{16,0},... | collective-permute-start | bytes 9224 | tf_op jit(solution)/shard_map/ppermute | solution.py:22
  31.0 0.2 collective-permute-done.10.refs_0_
  31.2 0.5 collective-permute-done.11.refs_1_
  31.7 0.5 collective-permute-done.12.refs_2_
  32.2 2.4 %collective-permute-done.13.refs_3_ = f32[8,96]{1,0:T(8,128)S(1)} collective-permute-done((f32[8,96]{1,0:T(8,128)S(1)}, f32[8,96]{1,0:T(8,128)S(1)}, u32[]{:S(2)}, u32[]{:S(2)}) %collective-permute-start.13) | collective-permute-done | bytes 3104 | tf_op jit(solution)/shard_map/ppermute | solution.py:22
  34.6 0.7 %apply.3 = (f32[16,96]{1,0:T(8,128)S(1)}, f32[1,128]{1,0:T(1,128)S(1)}) custom-call(f32[16,96]{1,0:T(8,128)S(1)} %get-tuple-element.57.field_ref.refs_1_, f32[16,96]{1,0:T(8,128)S(1)} %get-tuple-element.62.z_ref.refs_4_.refs_5_, f32[16,96]{1,0:T(8,128)S(1)} %get-tuple-element.63.own_ref, f32[8,96]{1,0:T(8,128)S(1)} %collective-permute-done.10.refs_0_, ...), custom_call_target="tpu_custom_call" | custom-call | bytes 100000 | tf_op jit(solution)/shard_map/apply/pallas_call | solution.py:26
  35.3 0.1 collective-permute-start.14
  35.4 0.3 local_inverse.3
  35.7 0.8 %collective-permute-done.14.theirs_ref = f32[1,128]{1,0:T(1,128)S(1)} collective-permute-done((f32[1,128]{1,0:T(1,128)S(1)}, f32[1,128]{1,0:T(1,128)S(1)}, u32[]{:S(2)}, u32[]{:S(2)}) %collective-permute-start.14) | collective-permute-done | bytes 544 | tf_op jit(solution)/shard_map/ppermute | solution.py:395
  36.5 1.1 %spread.3 = (f32[16,96]{1,0:T(8,128)S(1)}, f32[16,96]{1,0:T(8,128)S(1)}, f32[8,96]{1,0:T(8,128)S(1)}, f32[8,96]{1,0:T(8,128)S(1)}, f32[8,96]{1,0:T(8,128)S(1)}, /*index=5*/f32[8,96]{1,0:T(8,128)S(1)}) custom-call(f32[16,96,128]{2,1,0:T(8,128)S(1)} %get-tuple-element.69.column_ref, f32[16,96]{1,0:T(8,128)S(1)} %get-tuple-element.70.row_ref, ...), custom_call_target="tpu_custom_call" | custom-call | bytes 100000 | tf_op jit(solution)/shard_map/spread/pallas_call | solution.py:26
  37.5 1.6 %collective-permute-start.15 = (f32[8,96]{1,0:T(8,128)S(1)}, f32[8,96]{1,0:T(8,128)S(1)}, u32[]{:S(2)}, u32[]{:S(2)}) collective-permute-start(f32[8,96]{1,0:T(8,128)S(1)} %get-tuple-element.74), channel_id=1, source_target_pairs={{0,2},{2,0},{4,6},{6,4},{8,10},{10,8},{12,14},{14,12},{16,18},{18,... | collective-permute-start | bytes 9224 | tf_op jit(solution)/shard_map/ppermute | solution.py:22
  39.1 0.7 %collective-permute-start.16 = (f32[8,96]{1,0:T(8,128)S(1)}, f32[8,96]{1,0:T(8,128)S(1)}, u32[]{:S(2)}, u32[]{:S(2)}) collective-permute-start(f32[8,96]{1,0:T(8,128)S(1)} %get-tuple-element.75), channel_id=1, source_target_pairs={{0,4},{2,6},{4,0},{6,2},{8,12},{10,14},{12,8},{14,10},{16,20},{18,... | collective-permute-start | bytes 9224 | tf_op jit(solution)/shard_map/ppermute | solution.py:22
  39.7 1.4 %collective-permute-start.17 = (f32[8,96]{1,0:T(8,128)S(1)}, f32[8,96]{1,0:T(8,128)S(1)}, u32[]{:S(2)}, u32[]{:S(2)}) collective-permute-start(f32[8,96]{1,0:T(8,128)S(1)} %get-tuple-element.76), channel_id=1, source_target_pairs={{0,8},{2,10},{4,12},{6,14},{8,0},{10,2},{12,4},{14,6},{16,24},{18,... | collective-permute-start | bytes 9224 | tf_op jit(solution)/shard_map/ppermute | solution.py:22
  41.2 2.3 %collective-permute-start.18 = (f32[8,96]{1,0:T(8,128)S(1)}, f32[8,96]{1,0:T(8,128)S(1)}, u32[]{:S(2)}, u32[]{:S(2)}) collective-permute-start(f32[8,96]{1,0:T(8,128)S(1)} %get-tuple-element.77), channel_id=1, source_target_pairs={{0,16},{2,18},{4,20},{6,22},{8,24},{10,26},{12,28},{14,30},{16,0},... | collective-permute-start | bytes 9224 | tf_op jit(solution)/shard_map/ppermute | solution.py:22
  43.5 2.2 %collective-permute-done.18.refs_10_ = f32[8,96]{1,0:T(8,128)S(1)} collective-permute-done((f32[8,96]{1,0:T(8,128)S(1)}, f32[8,96]{1,0:T(8,128)S(1)}, u32[]{:S(2)}, u32[]{:S(2)}) %collective-permute-start.18) | collective-permute-done | bytes 3104 | tf_op jit(solution)/shard_map/ppermute | solution.py:22
  45.7 0.7 %last_apply.1 = (f32[16,96]{1,0:T(8,128)S(1)}, f32[32,1,128]{2,1,0:T(1,128)S(1)}) custom-call(f32[1,16,96]{2,1,0:T(8,128)S(1)} %copy-done.5, f32[16,96]{1,0:T(8,128)S(1)} %get-tuple-element.57.field_ref.refs_1_, f32[16,96]{1,0:T(8,128)S(1)} %get-tuple-element.68.field_ref.refs_2_, f32[16,96]{1,0:T(8,128)S(1)} %get-tuple-element.49.z_ref.refs_3_.refs_4_, ...), custom_call_target="tpu_custom_call" | custom-call | bytes 100000 | tf_op jit(solution)/shard_map/last_apply/pallas_call | solution.py:26
  46.4 9.6 %all_to_all.5.dots_ref = f32[32,1,128]{2,1,0:T(1,128)S(1)} all-to-all(f32[32,1,128]{2,1,0:T(1,128)S(1)} %get-tuple-element.78), channel_id=1, replica_groups=mesh['sub'=16,'coarse'=2] {'sub','coarse'}, dimensions={0} | all-to-all | bytes 32768 | tf_op jit(solution)/shard_map/all_to_all | solution.py:477
  56.0 0.8 %finish.1 = (f32[1,16,96]{2,1,0:T(8,128)}, f32[1,16,96]{2,1,0:T(8,128)}) custom-call(f32[32,1,128]{2,1,0:T(1,128)S(1)} %all_to_all.5.dots_ref, f32[1,16,96]{2,1,0:T(8,128)S(1)} %copy-done.5, f32[16,96]{1,0:T(8,128)S(1)} %get-tuple-element.57.field_ref.refs_1_, f32[16,96]{1,0:T(8,128)S(1)} %get-tuple-element.68.field_ref.refs_2_, ...), custom_call_target="tpu_custom_call" | custom-call | bytes 100000 | tf_op jit(solution)/shard_map/finish/pallas_call | solution.py:26
  (21 shorter events, 0.0 us)
Async XLA Ops:
  0.6 1.1 %copy-start = (f32[1,16,96,96]{3,2,1,0:T(8,128)S(1)}, f32[1,16,96,96]{3,2,1,0:T(8,128)}, u32[]{:S(2)}) copy-start(f32[1,16,96,96]{3,2,1,0:T(8,128)} %refs_15_.1) | copy-start | bytes 1769476
  1.8 9.0 %copy-start.2 = (f32[1,16,6,96]{3,1,2,0:T(8,128)S(1)}, f32[1,16,6,96]{3,1,2,0:T(8,128)}, u32[]{:S(2)}) copy-start(f32[1,16,6,96]{3,1,2,0:T(8,128)} %param.15) | copy-start | bytes 110596
  1.8 9.0 %copy-start.5 = (f32[1,16,96]{2,1,0:T(8,128)S(1)}, f32[1,16,96]{2,1,0:T(8,128)}, u32[]{:S(2)}) copy-start(f32[1,16,96]{2,1,0:T(8,128)} %refs_0_.5) | copy-start | bytes 18436
  1.8 9.0 %copy-start.8 = (s32[1,16]{1,0:T(1,128)S(1)}, s32[1,16]{1,0:T(1,128)}, u32[]{:S(2)}) copy-start(s32[1,16]{1,0:T(1,128)} %aggregate_ref.1) | copy-start | bytes 196
  1.8 9.7 %copy-start.6 = (s32[1,4,4]{2,1,0:T(4,128)S(1)}, s32[1,4,4]{2,1,0:T(4,128)}, u32[]{:S(2)}) copy-start(s32[1,4,4]{2,1,0:T(4,128)} %refs_12_.3) | copy-start | bytes 196
  1.8 9.7 %copy-start.7 = (s32[1,16,6]{1,0,2:T(1,128)S(1)}, s32[1,16,6]{1,0,2:T(1,128)}, u32[]{:S(2)}) copy-start(s32[1,16,6]{1,0,2:T(1,128)} %param.11) | copy-start | bytes 1156
  1.8 12.6 %copy-start.1 = (f32[1,16,6,96,96]{4,3,2,1,0:T(8,128)S(1)}, f32[1,16,6,96,96]{4,3,2,1,0:T(8,128)}, u32[]{:S(2)}) copy-start(f32[1,16,6,96,96]{4,3,2,1,0:T(8,128)} %refs_11_.3) | copy-start | bytes 10616836
  1.8 12.6 %copy-start.3 = (f32[1,16,96,96]{3,2,1,0:T(8,128)S(1)}, f32[1,16,96,96]{3,2,1,0:T(8,128)}, u32[]{:S(2)}) copy-start(f32[1,16,96,96]{3,2,1,0:T(8,128)} %inverse_ref.1) | copy-start | bytes 1769476
  1.8 12.6 %copy-start.4 = (f32[1,48,48]{2,1,0:T(8,128)S(1)}, f32[1,48,48]{2,1,0:T(8,128)}, u32[]{:S(2)}) copy-start(f32[1,48,48]{2,1,0:T(8,128)} %solver_ref.3) | copy-start | bytes 27652
  2.0 11.2 %collective-permute-start = (f32[4,72,128]{2,1,0:T(8,128)S(1)}, f32[4,72,128]{2,1,0:T(8,128)S(1)}, u32[]{:S(2)}, u32[]{:S(2)}) collective-permute-start(f32[4,72,128]{2,1,0:T(8,128)S(1)} %get-tuple-element.41), channel_id=1, source_target_pairs={{0,16},{2,18},{4,20},{6,22},{8,24},{10,26},{12,28},{14,30},{16,0},... | collective-permute-start | bytes 442376 | tf_op jit(solution)/shard_map/ppermute | solution.py:22
  6.1 7.3 %collective-permute-start.1 = (f32[4,72,128]{2,1,0:T(8,128)S(1)}, f32[4,72,128]{2,1,0:T(8,128)S(1)}, u32[]{:S(2)}, u32[]{:S(2)}) collective-permute-start(f32[4,72,128]{2,1,0:T(8,128)S(1)} %get-tuple-element.42), channel_id=1, source_target_pairs={{0,8},{2,10},{4,12},{6,14},{8,0},{10,2},{12,4},{14,6},{16,24},{18,... | collective-permute-start | bytes 442376 | tf_op jit(solution)/shard_map/ppermute | solution.py:22
  7.7 5.7 %collective-permute-start.2 = (f32[4,72,128]{2,1,0:T(8,128)S(1)}, f32[4,72,128]{2,1,0:T(8,128)S(1)}, u32[]{:S(2)}, u32[]{:S(2)}) collective-permute-start(f32[4,72,128]{2,1,0:T(8,128)S(1)} %get-tuple-element.43), channel_id=1, source_target_pairs={{0,4},{2,6},{4,0},{6,2},{8,12},{10,14},{12,8},{14,10},{16,20},{18,... | collective-permute-start | bytes 442376 | tf_op jit(solution)/shard_map/ppermute | solution.py:22
  9.2 5.1 %collective-permute-start.3 = (f32[4,72,128]{2,1,0:T(8,128)S(1)}, f32[4,72,128]{2,1,0:T(8,128)S(1)}, u32[]{:S(2)}, u32[]{:S(2)}) collective-permute-start(f32[4,72,128]{2,1,0:T(8,128)S(1)} %get-tuple-element.44), channel_id=1, source_target_pairs={{0,2},{2,0},{4,6},{6,4},{8,10},{10,8},{12,14},{14,12},{16,18},{18,... | collective-permute-start | bytes 442376 | tf_op jit(solution)/shard_map/ppermute | solution.py:22
  11.4 1.2 %collective-permute-start.4 = (f32[1,128]{1,0:T(1,128)S(1)}, f32[1,128]{1,0:T(1,128)S(1)}, u32[]{:S(2)}, u32[]{:S(2)}) collective-permute-start(f32[1,128]{1,0:T(1,128)S(1)} %get-tuple-element.45.refs_4_), channel_id=1, source_target_pairs={{0,1},{1,0},{2,3},{3,2},{4,5},{5,4},{6,7},{7,6},{8,9},{9,8},{10,11... | collective-permute-start | bytes 1544 | tf_op jit(solution)/shard_map/ppermute | solution.py:395
  16.4 6.0 %collective-permute-start.5 = (f32[8,96]{1,0:T(8,128)S(1)}, f32[8,96]{1,0:T(8,128)S(1)}, u32[]{:S(2)}, u32[]{:S(2)}) collective-permute-start(f32[8,96]{1,0:T(8,128)S(1)} %get-tuple-element.51), channel_id=1, source_target_pairs={{0,2},{2,0},{4,6},{6,4},{8,10},{10,8},{12,14},{14,12},{16,18},{18,... | collective-permute-start | bytes 9224 | tf_op jit(solution)/shard_map/ppermute | solution.py:22
  18.0 4.4 %collective-permute-start.6 = (f32[8,96]{1,0:T(8,128)S(1)}, f32[8,96]{1,0:T(8,128)S(1)}, u32[]{:S(2)}, u32[]{:S(2)}) collective-permute-start(f32[8,96]{1,0:T(8,128)S(1)} %get-tuple-element.52), channel_id=1, source_target_pairs={{0,4},{2,6},{4,0},{6,2},{8,12},{10,14},{12,8},{14,10},{16,20},{18,... | collective-permute-start | bytes 9224 | tf_op jit(solution)/shard_map/ppermute | solution.py:22
  18.6 3.8 %collective-permute-start.7 = (f32[8,96]{1,0:T(8,128)S(1)}, f32[8,96]{1,0:T(8,128)S(1)}, u32[]{:S(2)}, u32[]{:S(2)}) collective-permute-start(f32[8,96]{1,0:T(8,128)S(1)} %get-tuple-element.53), channel_id=1, source_target_pairs={{0,8},{2,10},{4,12},{6,14},{8,0},{10,2},{12,4},{14,6},{16,24},{18,... | collective-permute-start | bytes 9224 | tf_op jit(solution)/shard_map/ppermute | solution.py:22
  20.1 4.5 %collective-permute-start.8 = (f32[8,96]{1,0:T(8,128)S(1)}, f32[8,96]{1,0:T(8,128)S(1)}, u32[]{:S(2)}, u32[]{:S(2)}) collective-permute-start(f32[8,96]{1,0:T(8,128)S(1)} %get-tuple-element.54), channel_id=1, source_target_pairs={{0,16},{2,18},{4,20},{6,22},{8,24},{10,26},{12,28},{14,30},{16,0},... | collective-permute-start | bytes 9224 | tf_op jit(solution)/shard_map/ppermute | solution.py:22
  25.3 1.2 %collective-permute-start.9 = (f32[1,128]{1,0:T(1,128)S(1)}, f32[1,128]{1,0:T(1,128)S(1)}, u32[]{:S(2)}, u32[]{:S(2)}) collective-permute-start(f32[1,128]{1,0:T(1,128)S(1)} %get-tuple-element.61.mine_ref), channel_id=1, source_target_pairs={{0,1},{1,0},{2,3},{3,2},{4,5},{5,4},{6,7},{7,6},{8,9},{9,8},{10,11... | collective-permute-start | bytes 1544 | tf_op jit(solution)/shard_map/ppermute | solution.py:395
  27.5 3.7 %collective-permute-start.10 = (f32[8,96]{1,0:T(8,128)S(1)}, f32[8,96]{1,0:T(8,128)S(1)}, u32[]{:S(2)}, u32[]{:S(2)}) collective-permute-start(f32[8,96]{1,0:T(8,128)S(1)} %get-tuple-element.64), channel_id=1, source_target_pairs={{0,2},{2,0},{4,6},{6,4},{8,10},{10,8},{12,14},{14,12},{16,18},{18,... | collective-permute-start | bytes 9224 | tf_op jit(solution)/shard_map/ppermute | solution.py:22
  28.1 3.6 %collective-permute-start.11 = (f32[8,96]{1,0:T(8,128)S(1)}, f32[8,96]{1,0:T(8,128)S(1)}, u32[]{:S(2)}, u32[]{:S(2)}) collective-permute-start(f32[8,96]{1,0:T(8,128)S(1)} %get-tuple-element.65), channel_id=1, source_target_pairs={{0,4},{2,6},{4,0},{6,2},{8,12},{10,14},{12,8},{14,10},{16,20},{18,... | collective-permute-start | bytes 9224 | tf_op jit(solution)/shard_map/ppermute | solution.py:22
  28.6 3.6 %collective-permute-start.12 = (f32[8,96]{1,0:T(8,128)S(1)}, f32[8,96]{1,0:T(8,128)S(1)}, u32[]{:S(2)}, u32[]{:S(2)}) collective-permute-start(f32[8,96]{1,0:T(8,128)S(1)} %get-tuple-element.66), channel_id=1, source_target_pairs={{0,8},{2,10},{4,12},{6,14},{8,0},{10,2},{12,4},{14,6},{16,24},{18,... | collective-permute-start | bytes 9224 | tf_op jit(solution)/shard_map/ppermute | solution.py:22
  30.1 4.5 %collective-permute-start.13 = (f32[8,96]{1,0:T(8,128)S(1)}, f32[8,96]{1,0:T(8,128)S(1)}, u32[]{:S(2)}, u32[]{:S(2)}) collective-permute-start(f32[8,96]{1,0:T(8,128)S(1)} %get-tuple-element.67), channel_id=1, source_target_pairs={{0,16},{2,18},{4,20},{6,22},{8,24},{10,26},{12,28},{14,30},{16,0},... | collective-permute-start | bytes 9224 | tf_op jit(solution)/shard_map/ppermute | solution.py:22
  35.3 1.2 %collective-permute-start.14 = (f32[1,128]{1,0:T(1,128)S(1)}, f32[1,128]{1,0:T(1,128)S(1)}, u32[]{:S(2)}, u32[]{:S(2)}) collective-permute-start(f32[1,128]{1,0:T(1,128)S(1)} %get-tuple-element.71.mine_ref), channel_id=1, source_target_pairs={{0,1},{1,0},{2,3},{3,2},{4,5},{5,4},{6,7},{7,6},{8,9},{9,8},{10,11... | collective-permute-start | bytes 1544 | tf_op jit(solution)/shard_map/ppermute | solution.py:395
  37.5 6.0 %collective-permute-start.15 = (f32[8,96]{1,0:T(8,128)S(1)}, f32[8,96]{1,0:T(8,128)S(1)}, u32[]{:S(2)}, u32[]{:S(2)}) collective-permute-start(f32[8,96]{1,0:T(8,128)S(1)} %get-tuple-element.74), channel_id=1, source_target_pairs={{0,2},{2,0},{4,6},{6,4},{8,10},{10,8},{12,14},{14,12},{16,18},{18,... | collective-permute-start | bytes 9224 | tf_op jit(solution)/shard_map/ppermute | solution.py:22
  39.1 4.4 %collective-permute-start.16 = (f32[8,96]{1,0:T(8,128)S(1)}, f32[8,96]{1,0:T(8,128)S(1)}, u32[]{:S(2)}, u32[]{:S(2)}) collective-permute-start(f32[8,96]{1,0:T(8,128)S(1)} %get-tuple-element.75), channel_id=1, source_target_pairs={{0,4},{2,6},{4,0},{6,2},{8,12},{10,14},{12,8},{14,10},{16,20},{18,... | collective-permute-start | bytes 9224 | tf_op jit(solution)/shard_map/ppermute | solution.py:22
  39.7 3.8 %collective-permute-start.17 = (f32[8,96]{1,0:T(8,128)S(1)}, f32[8,96]{1,0:T(8,128)S(1)}, u32[]{:S(2)}, u32[]{:S(2)}) collective-permute-start(f32[8,96]{1,0:T(8,128)S(1)} %get-tuple-element.76), channel_id=1, source_target_pairs={{0,8},{2,10},{4,12},{6,14},{8,0},{10,2},{12,4},{14,6},{16,24},{18,... | collective-permute-start | bytes 9224 | tf_op jit(solution)/shard_map/ppermute | solution.py:22
  41.2 4.5 %collective-permute-start.18 = (f32[8,96]{1,0:T(8,128)S(1)}, f32[8,96]{1,0:T(8,128)S(1)}, u32[]{:S(2)}, u32[]{:S(2)}) collective-permute-start(f32[8,96]{1,0:T(8,128)S(1)} %get-tuple-element.77), channel_id=1, source_target_pairs={{0,16},{2,18},{4,20},{6,22},{8,24},{10,26},{12,28},{14,30},{16,0},... | collective-permute-start | bytes 9224 | tf_op jit(solution)/shard_map/ppermute | solution.py:22

commit v3 on v2

--- a/solution.py
+++ b/solution.py
@@ -117,30 +117,37 @@
 
 
 def table_kernel(
-    pattern_ref, senders_ref, pick_ref, spread_ref, send_ref, back_ref, table_ref, send_table_ref
+    pattern_ref, senders_ref, pick_ref, send_ref, back_ref, index_ref, table_ref, send_table_ref
 ):
     slots, _, rows = pattern_ref.shape
     turns, ghosts = senders_ref.shape[1:]
     extent = pick_ref.shape[1] // 3
     lane = lax.broadcasted_iota(jnp.int32, (1, 128), 1)
+    columns = jnp.zeros((1, 128), jnp.int32)
     for i in range(rows):
         for j in range(slots):
             at = i * slots + j
             table_ref[at : at + 1, :] = jnp.where(lane == pattern_ref[j, 0, i], 1.0, 0.0)
+            columns = jnp.where(lane == at, pattern_ref[j, 0, i], columns)
+    index_ref[0:1, :] = columns
+    sent = jnp.zeros((1, 128), jnp.int32)
     for turn in range(turns):
         for g in range(ghosts):
             at = turn * ghosts + g
             send_table_ref[at : at + 1, :] = jnp.where(lane == senders_ref[0, turn, g], 1.0, 0.0)
+            sent = jnp.where(lane == at, senders_ref[0, turn, g], sent)
+    index_ref[1:2, :] = sent
     table = table_ref[...]
     pick_ref[...] = triple(table[:, :extent])
-    spread_ref[...] = triple(table.T[:extent])
     send_table = send_table_ref[...]
     send_ref[...] = triple(send_table[:, :rows])
     back_ref[...] = triple(send_table.T[:rows])
 
 
 def local_kernel(field_ref, inverse_ref, column_ref, row_ref):
-    rows, width = field_ref.shape
+    rows, width = row_ref.shape
+    field_ref = field_ref.reshape(rows, width)
+    inverse_ref = inverse_ref.reshape(rows, width, width)
     eye = eye_mask(width)
     for i in range(rows):
         column = jnp.sum(inverse_ref[i] * field_ref[i : i + 1, :], axis=1, keepdims=True)
@@ -149,49 +156,76 @@
 
 
 def spread_block_row(blocks_ref, parts_ref, i, column):
-    slots = blocks_ref.shape[2]
+    slots, width = blocks_ref.shape[2:4]
     for j in range(slots):
+        part = blocks_ref[0, i, j, 0:8, :] * column[0:8]
+        for start in range(8, width, 8):
+            part = part + blocks_ref[0, i, j, start : start + 8, :] * column[start : start + 8]
         at = i * slots + j
-        parts_ref[at : at + 1, :] = jnp.sum(blocks_ref[0, i, j] * column, axis=0, keepdims=True)
-
-
-def finish_spread(parts_ref, spread_ref, send_ref, z, own_ref, packets):
+        parts_ref[at : at + 1, :] = jnp.sum(part, axis=0, keepdims=True)
+
+
+def finish_spread(parts_ref, slots_ref, indices_ref, z_ref, own_ref, packets):
     turns = len(packets)
-    rows = z.shape[0]
-    sent = select_rows(send_ref, z)
-    spread = select_rows(spread_ref, parts_ref[...])
+    rows = z_ref.shape[0]
+    ghosts = packets[0].shape[0] // 2
+    slots = slots_ref.shape[0]
+    for i in range(rows):
+        slots_ref[0, i : i + 1, :] = parts_ref[i * slots : i * slots + 1, :]
+        for j in range(1, slots):
+            at = i * slots + j
+            slots_ref[j, pl.ds(indices_ref[0, at], 1), :] = parts_ref[at : at + 1, :]
+    for turn in range(turns):
+        for g in range(ghosts):
+            at = indices_ref[1, turn * ghosts + g]
+            packets[turn][g : g + 1, :] = z_ref[pl.ds(at, 1), :]
+    spread = slots_ref[0]
+    for j in range(1, slots):
+        spread = spread + slots_ref[j]
     own_ref[...] = spread[:rows]
-    ghosts = sent.shape[0] // turns
     for turn in range(turns):
-        start = turn * ghosts
-        packets[turn][0:ghosts, :] = sent[start : start + ghosts]
-        packets[turn][ghosts:, :] = spread[rows + start : rows + start + ghosts]
-
-
-def first_kernel(turns, field_ref, inverse_ref, *refs):
-    gathered = refs[:turns][::-1]
-    (
-        mine_ref,
-        theirs_ref,
-        solver_ref,
-        null_ref,
-        offset_ref,
-        blocks_ref,
-        spread_ref,
-        send_ref,
-        senders_ref,
-        combined_ref,
-        z_ref,
-        own_ref,
-    ) = refs[turns : turns + 12]
-    packets = refs[turns + 12 : 2 * turns + 12]
-    (parts_ref,) = refs[2 * turns + 12 :]
-    rows, width = z_ref.shape
-    tall = width * width // 128
+        start = rows + turn * ghosts
+        packets[turn][ghosts:, :] = spread[start : start + ghosts]
+
+
+def margin_row(packed_ref, g, row, eye):
+    tall = packed_ref.shape[1]
+    width = row.shape[1]
     side = 128 - width
     rest = width - tall
-    ghosts = senders_ref.shape[2]
-    eye = eye_mask(width)
+    column = jnp.sum(packed_ref[g, :, 0:width] * row, axis=1, keepdims=True)
+    beside = jnp.zeros((rest, side), f32)
+    for piece in range(width // side):
+        beside = (
+            beside
+            + packed_ref[g, piece * rest : (piece + 1) * rest, width:128]
+            * row[:, piece * side : (piece + 1) * side]
+        )
+    beside = jnp.sum(beside, axis=1, keepdims=True)
+    return to_row(column, eye[:tall]) + to_row(beside, eye[tall:])
+
+
+def margin_kernel(turns, field_ref, send_ref, *refs):
+    early = refs[:turns][::-1]
+    out_ref, picked_ref = refs[turns:]
+    ghosts = early[0].shape[0]
+    eye = eye_mask(out_ref.shape[1])
+    picked_ref[...] = select_rows(send_ref, field_ref[0])
+    first = out_ref.shape[0] // ghosts - turns
+    out_ref[...] = picked_ref[...]
+    for turn in range(turns):
+        for g in range(ghosts):
+            at = (first + turn) * ghosts + g
+            out_ref[at : at + 1, :] = margin_row(early[turn], g, picked_ref[at : at + 1, :], eye)
+
+
+def combine_kernel(turns, inverse_ref, senders_ref, *refs):
+    gathered = refs[:turns]
+    (combined_ref,) = refs[turns:]
+    ghosts, tall = gathered[0].shape[:2]
+    width = inverse_ref.shape[2]
+    side = 128 - width
+    rest = width - tall
     combined_ref[...] = inverse_ref[0]
     for turn in range(turns):
         for g in range(ghosts):
@@ -201,13 +235,40 @@
                 combined_ref[at, tall:, piece * side : (piece + 1) * side] += gathered[turn][
                     g, piece * rest : (piece + 1) * rest, width:128
                 ]
+
+
+def first_kernel(turns, column_ref, row_ref, margin_ref, late_ref, *refs):
+    (
+        mine_ref,
+        theirs_ref,
+        solver_ref,
+        null_ref,
+        offset_ref,
+        back_ref,
+        blocks_ref,
+        index_ref,
+        z_ref,
+        own_ref,
+    ) = refs[:10]
+    packets = refs[10 : turns + 10]
+    parts_ref, slots_ref, indices_ref, sem = refs[turns + 10 :]
+    fetch = pltpu.make_async_copy(index_ref, indices_ref, sem)
+    fetch.start()
+    slots_ref[...] = jnp.zeros(slots_ref.shape, f32)
+    rows, width = z_ref.shape
+    ghosts = late_ref.shape[0]
+    eye = eye_mask(width)
+    late = [margin_row(late_ref, g, margin_ref[g : g + 1, :], eye) for g in range(ghosts)]
+    margin = jnp.concatenate(late + [margin_ref[ghosts:, :]], axis=0)
     coarse = coarse_field(mine_ref, theirs_ref, solver_ref, null_ref, offset_ref)
+    added = coarse + select_rows(back_ref, margin)
+    z = row_ref[...] + added
+    z_ref[...] = z
     for i in range(rows):
-        product = combined_ref[i] * field_ref[0, i : i + 1, :] + jnp.where(eye, coarse[i : i + 1], 0.0)
-        column = jnp.sum(product, axis=1, keepdims=True)
-        z_ref[i : i + 1, :] = to_row(column, eye)
+        column = column_ref[i][:, :width] + to_column(added[i : i + 1], eye)
         spread_block_row(blocks_ref, parts_ref, i, column)
-    finish_spread(parts_ref, spread_ref, send_ref, z_ref[...], own_ref, packets)
+    fetch.wait()
+    finish_spread(parts_ref, slots_ref, indices_ref, z_ref, own_ref, packets)
 
 
 def spread_kernel(
@@ -220,14 +281,16 @@
     null_ref,
     offset_ref,
     blocks_ref,
-    spread_ref,
-    send_ref,
+    index_ref,
     z_ref,
     own_ref,
     *refs,
 ):
     packets = refs[:turns]
-    (parts_ref,) = refs[turns:]
+    parts_ref, slots_ref, indices_ref, sem = refs[turns:]
+    fetch = pltpu.make_async_copy(index_ref, indices_ref, sem)
+    fetch.start()
+    slots_ref[...] = jnp.zeros(slots_ref.shape, f32)
     rows, width = z_ref.shape
     eye = eye_mask(width)
     coarse = coarse_field(mine_ref, theirs_ref, solver_ref, null_ref, offset_ref)
@@ -236,7 +299,8 @@
     for i in range(rows):
         column = column_ref[i][:, :width] + to_column(coarse[i : i + 1], eye)
         spread_block_row(blocks_ref, parts_ref, i, column)
-    finish_spread(parts_ref, spread_ref, send_ref, z, own_ref, packets)
+    fetch.wait()
+    finish_spread(parts_ref, slots_ref, indices_ref, z_ref, own_ref, packets)
 
 
 def apply_rows(arrived, z, own_ref, blocks_ref, pick_ref, back_ref, picked_ref):
@@ -261,7 +325,7 @@
 
 
 def apply_kernel(turns, field_ref, z_ref, own_ref, *refs):
-    arrived = refs[:turns]
+    arrived = refs[:turns][::-1]
     (
         blocks_ref,
         pick_ref,
@@ -282,7 +346,7 @@
     field_refs = refs[:fields]
     z_refs = refs[fields : 2 * fields]
     own_ref = refs[2 * fields]
-    arrived = refs[2 * fields + 1 : 2 * fields + 1 + turns]
+    arrived = refs[2 * fields + 1 : 2 * fields + 1 + turns][::-1]
     blocks_ref, pick_ref, back_ref, next_ref, dots_ref, picked_ref = refs[2 * fields + 1 + turns :]
     image = apply_rows(
         arrived, z_refs[-1][...], own_ref, blocks_ref, pick_ref, back_ref, picked_ref
@@ -388,6 +452,11 @@
     parts = rows * slots
     ghost_total = turns * ghosts
     parts_scratch = [pltpu.VMEM((parts, width), f32)]
+    spread_scratch = parts_scratch + [
+        pltpu.VMEM((slots, extent, width), f32),
+        pltpu.SMEM((2, 128), jnp.int32),
+        pltpu.SemaphoreType.DMA,
+    ]
     null_view = jnp.transpose(near_null, (0, 2, 1, 3))
     pattern_view = jnp.transpose(pattern, (2, 0, 1))
 
@@ -410,13 +479,13 @@
         name="restrict",
     )
     theirs = swap(mine)
-    pick, spread, send, back = call(
+    pick, send, back, index = call(
         table_kernel,
         [
             ((parts, 3 * extent), bf16),
-            ((extent, 3 * parts), bf16),
             ((ghost_total, 3 * rows), bf16),
             ((rows, 3 * ghost_total), bf16),
+            ((2, 128), jnp.int32),
         ],
         [SMEM, SMEM],
         [pattern_view, send_rows],
@@ -424,26 +493,51 @@
         name="tables",
     )
     source, null_modes, held, solver = right_side, null_view, blocks, coarse_inverse
-    combined, z, own, *packets = call(
+    column, row = call(
+        local_kernel,
+        [(rows, width, 128), row_shape],
+        [VMEM, VMEM],
+        [right_side, inverse_blocks],
+        name="local_inverse",
+    )
+    (margin,) = call(
+        functools.partial(margin_kernel, turns - 1),
+        [(ghost_total, width)],
+        [VMEM] * (turns + 1),
+        [source, send, *gathered[:0:-1]],
+        scratch=[pltpu.VMEM((ghost_total, width), f32)],
+        name="margin_rows",
+    )
+    z, own, *packets = call(
         functools.partial(first_kernel, turns),
-        [(rows, width, width), row_shape, row_shape] + [packet] * turns,
-        [VMEM] * (turns + 10) + [SMEM],
-        [source, inverse_blocks, *gathered[::-1], mine, theirs, solver, null_modes, offset, held, spread, send]
-        + [send_rows],
-        scratch=parts_scratch,
+        [row_shape, row_shape] + [packet] * turns,
+        [VMEM] * 12,
+        [column, row, margin, gathered[0], mine, theirs, solver, null_modes, offset, back]
+        + [held, index],
+        scratch=spread_scratch,
         name="first_spread",
+    )
+    (combined,) = call(
+        functools.partial(combine_kernel, turns),
+        [(rows, width, width)],
+        [VMEM, SMEM] + [VMEM] * turns,
+        [inverse_blocks, send_rows, *gathered],
+        name="combine",
     )
     values = [source]
     fields = [z]
     for step in range(ITERS):
         arrived = [partner(packets[turn], "sub", bits[turn]) for turn in range(turns)]
+        if step == 0:
+            combined, *arrived = lax.optimization_barrier([combined, *arrived[::-1]])
+            arrived = arrived[::-1]
         if step + 1 == ITERS:
             break
         following, mine = call(
             functools.partial(apply_kernel, turns),
             [row_shape, (1, 128)],
             [VMEM] * (turns + 8),
-            [values[-1], fields[-1], own, *arrived, held, pick, back, null_modes, offset],
+            [values[-1], fields[-1], own, *arrived[::-1], held, pick, back, null_modes, offset],
             scratch=parts_scratch,
             name="apply",
         )
@@ -459,9 +553,9 @@
         z, own, *packets = call(
             functools.partial(spread_kernel, turns),
             [row_shape, row_shape] + [packet] * turns,
-            [VMEM] * 10,
-            [column, row, mine, theirs, solver, null_modes, offset, held, spread, send],
-            scratch=parts_scratch,
+            [VMEM] * 9,
+            [column, row, mine, theirs, solver, null_modes, offset, held, index],
+            scratch=spread_scratch,
             name="spread",
         )
         fields.append(z)
@@ -469,7 +563,7 @@
         functools.partial(last_kernel, turns, ITERS),
         [row_shape, (devices, 1, 128)],
         [VMEM] * (2 * ITERS + 1 + turns + 3),
-        [*values, *fields, own, *arrived, held, pick, back],
+        [*values, *fields, own, *arrived[::-1], held, pick, back],
         scratch=parts_scratch,
         name="last_apply",
     )

time: 57 us -> 54.8 us (0.961)
  waiting for transfers between devices: 11.8 us -> 7.83 us
  starting transfers between devices: 24.3 us -> 25.9 us
  Pallas kernels: 9.2 us -> 10 us
  blocking collectives: 9.63 us -> 8.88 us
    ppermute x16, waiting for transfers between devices: 9.83 us -> 6.2 us  [partner(): lax.ppermute(array, axis, [(i, i ^ 1 << bit) for i in range(lax.axis_size...]
    ppermute x16, starting transfers between devices: 24.1 us -> 25.7 us  [partner(): lax.ppermute(array, axis, [(i, i ^ 1 << bit) for i in range(lax.axis_size...]
    pallas_call x12 -> x15, Pallas kernels: 9.2 us -> 10 us  [call(): pl.pallas_call(kernel, out_shape=[jax.ShapeDtypeStruct(*(out if isinstanc...]
    all_to_all x1, blocking collectives: 9.63 us -> 8.88 us  [on_device(): exchanged = lax.all_to_all(dots, ('sub', 'coarse'), 0, 0)]
  transfers between devices with their start and end apart: 19 -> 19, of which waited for: 12 -> 10; matrix products, arithmetic and copies ran while one was open for 0% -> 0% of each run, Pallas kernels for 4% -> 8%
where the time goes in v3:
time: 54.8 us; the launch traced here: 54.6 us
  starting transfers between devices  25.9 us (47%)
  Pallas kernels  10 us (18%)
  blocking collectives  8.88 us (16%)
  waiting for transfers between devices  7.83 us (14%)
  local copies, waits for them, and re-layouts  1.16 us (2%)
  between operations  0.87 us (2%)
    ppermute x16, starting transfers between devices, partner(): lax.ppermute(array, axis, [(i, i ^ 1 << bit) for i in range(lax.axis_size...  25.7 us
    pallas_call x15, Pallas kernels, call(): pl.pallas_call(kernel, out_shape=[jax.ShapeDtypeStruct(*(out if isinstanc...  10 us
    all_to_all x1, blocking collectives, on_device(): exchanged = lax.all_to_all(dots, ('sub', 'coarse'), 0, 0)  8.88 us
    ppermute x16, waiting for transfers between devices, partner(): lax.ppermute(array, axis, [(i, i ^ 1 << bit) for i in range(lax.axis_size...  6.2 us
    ppermute x3, waiting for transfers between devices, swap(): return lax.ppermute(array, 'coarse', flip)  1.63 us
    unnamed x18, local copies, waits for them, and re-layouts  1.16 us
  transfers between devices with their start and end apart: 19, of which 10 were waited for; matrix products, arithmetic and copies ran while one was open for 0% of the time, Pallas kernels for 8%

profile of v3, /device:TPU:0, one launch (start us, length us, event | category | flops | bytes accessed | tf_op | source)
XLA Modules:
  0.0 54.6 jit_solution(9605060973980890530)
XLA Ops:
  0.6 1.1 %copy-done = f32[1,16,96,96]{3,2,1,0:T(8,128)S(1)} copy-done((f32[1,16,96,96]{3,2,1,0:T(8,128)S(1)}, f32[1,16,96,96]{3,2,1,0:T(8,128)}, u32[]{:S(2)}) %copy-start) | copy-done | bytes 589848
  1.8 0.2 pack_margin.1
  2.0 4.1 %collective-permute-start = (f32[4,72,128]{2,1,0:T(8,128)S(1)}, f32[4,72,128]{2,1,0:T(8,128)S(1)}, u32[]{:S(2)}, u32[]{:S(2)}) collective-permute-start(f32[4,72,128]{2,1,0:T(8,128)S(1)} %get-tuple-element.50), channel_id=1, source_target_pairs={{0,16},{2,18},{4,20},{6,22},{8,24},{10,26},{12,28},{14,30},{16,0},... | collective-permute-start | bytes 442376 | tf_op jit(solution)/shard_map/ppermute | solution.py:22
  6.1 1.6 %collective-permute-start.1 = (f32[4,72,128]{2,1,0:T(8,128)S(1)}, f32[4,72,128]{2,1,0:T(8,128)S(1)}, u32[]{:S(2)}, u32[]{:S(2)}) collective-permute-start(f32[4,72,128]{2,1,0:T(8,128)S(1)} %get-tuple-element.51), channel_id=1, source_target_pairs={{0,8},{2,10},{4,12},{6,14},{8,0},{10,2},{12,4},{14,6},{16,24},{18,... | collective-permute-start | bytes 442376 | tf_op jit(solution)/shard_map/ppermute | solution.py:22
  7.7 1.5 %collective-permute-start.2 = (f32[4,72,128]{2,1,0:T(8,128)S(1)}, f32[4,72,128]{2,1,0:T(8,128)S(1)}, u32[]{:S(2)}, u32[]{:S(2)}) collective-permute-start(f32[4,72,128]{2,1,0:T(8,128)S(1)} %get-tuple-element.52), channel_id=1, source_target_pairs={{0,4},{2,6},{4,0},{6,2},{8,12},{10,14},{12,8},{14,10},{16,20},{18,... | collective-permute-start | bytes 442376 | tf_op jit(solution)/shard_map/ppermute | solution.py:22
  9.2 1.5 %collective-permute-start.3 = (f32[4,72,128]{2,1,0:T(8,128)S(1)}, f32[4,72,128]{2,1,0:T(8,128)S(1)}, u32[]{:S(2)}, u32[]{:S(2)}) collective-permute-start(f32[4,72,128]{2,1,0:T(8,128)S(1)} %get-tuple-element.53), channel_id=1, source_target_pairs={{0,2},{2,0},{4,6},{6,4},{8,10},{10,8},{12,14},{14,12},{16,18},{18,... | collective-permute-start | bytes 442376 | tf_op jit(solution)/shard_map/ppermute | solution.py:22
  10.7 0.6 %restrict.1 = (s32[16,128]{1,0:T(8,128)S(1)}, f32[1,128]{1,0:T(1,128)S(1)}) custom-call(f32[1,16,96]{2,1,0:T(8,128)S(1)} %copy-done.4, f32[1,6,16,96]{3,2,1,0:T(8,128)S(1)} %bitcast.2, s32[1,16]{1,0:T(1,128)S(1)} %copy-done.8), custom_call_target="tpu_custom_call" | custom-call | bytes 100000 | tf_op jit(solution)/shard_map/restrict/pallas_call | solution.py:26
  11.4 0.1 collective-permute-start.4
  11.5 0.3 local_inverse.3
  11.8 0.8 %tables.1 = (bf16[96,96]{1,0:T(8,128)(2,1)S(1)}, bf16[16,48]{1,0:T(8,128)(2,1)S(1)}, bf16[16,48]{1,0:T(8,128)(2,1)S(1)}, s32[2,128]{1,0:T(2,128)S(1)}) custom-call(s32[6,1,16]{2,1,0:T(1,128)S(1)} %bitcast.8, s32[1,4,4]{2,1,0:T(4,128)S(1)} %copy-done.6), custom_call_target="tpu_custom_call" | custom-call | bytes 100000 | tf_op jit(solution)/shard_map/tables/pallas_call | solution.py:26
  12.6 0.7 %collective-permute-done.refs_0_.refs_3_ = f32[4,72,128]{2,1,0:T(8,128)S(1)} collective-permute-done((f32[4,72,128]{2,1,0:T(8,128)S(1)}, f32[4,72,128]{2,1,0:T(8,128)S(1)}, u32[]{:S(2)}, u32[]{:S(2)}) %collective-permute-start) | collective-permute-done | bytes 147488 | tf_op jit(solution)/shard_map/ppermute | solution.py:22
  13.3 0.2 collective-permute-done.1.refs_1_.refs_2_
  13.4 0.0 collective-permute-done.2.refs_2_.refs_1_
  13.5 1.0 %margin_rows.1.margin_ref = f32[16,96]{1,0:T(8,128)S(1)} custom-call(f32[1,16,96]{2,1,0:T(8,128)S(1)} %copy-done.4, bf16[16,48]{1,0:T(8,128)(2,1)S(1)} %get-tuple-element.49.send_ref, f32[4,72,128]{2,1,0:T(8,128)S(1)} %collective-permute-done.refs_0_.refs_3_, f32[4,72,128]{2,1,0:T(8,128)S(1)} %collective-permute-done.1.refs_1_.refs_2_, ...), custom_call_target="tpu_custom_call" | custom-call | bytes 100000 | tf_op jit(solution)/shard_map/margin_rows/pallas_call | solution.py:26
  14.4 0.0 collective-permute-done.3.late_ref.refs_0_
  14.5 1.0 %first_spread.1 = (f32[16,96]{1,0:T(8,128)S(1)}, f32[16,96]{1,0:T(8,128)S(1)}, f32[8,96]{1,0:T(8,128)S(1)}, f32[8,96]{1,0:T(8,128)S(1)}, f32[8,96]{1,0:T(8,128)S(1)}, /*index=5*/f32[8,96]{1,0:T(8,128)S(1)}) custom-call(f32[16,96,128]{2,1,0:T(8,128)S(1)} %get-tuple-element.47.column_ref, f32[16,96]{1,0:T(8,128)S(1)} %get-tuple-element.48.row_ref, ...), custom_call_target="tpu_custom_call" | custom-call | bytes 100000 | tf_op jit(solution)/shard_map/first_spread/pallas_call | solution.py:26
  15.5 1.4 %collective-permute-start.5 = (f32[8,96]{1,0:T(8,128)S(1)}, f32[8,96]{1,0:T(8,128)S(1)}, u32[]{:S(2)}, u32[]{:S(2)}) collective-permute-start(f32[8,96]{1,0:T(8,128)S(1)} %get-tuple-element.60), channel_id=1, source_target_pairs={{0,16},{2,18},{4,20},{6,22},{8,24},{10,26},{12,28},{14,30},{16,0},... | collective-permute-start | bytes 9224 | tf_op jit(solution)/shard_map/ppermute | solution.py:22
  17.0 2.4 %collective-permute-start.6 = (f32[8,96]{1,0:T(8,128)S(1)}, f32[8,96]{1,0:T(8,128)S(1)}, u32[]{:S(2)}, u32[]{:S(2)}) collective-permute-start(f32[8,96]{1,0:T(8,128)S(1)} %get-tuple-element.61), channel_id=1, source_target_pairs={{0,8},{2,10},{4,12},{6,14},{8,0},{10,2},{12,4},{14,6},{16,24},{18,... | collective-permute-start | bytes 9224 | tf_op jit(solution)/shard_map/ppermute | solution.py:22
  19.4 1.5 %collective-permute-start.7 = (f32[8,96]{1,0:T(8,128)S(1)}, f32[8,96]{1,0:T(8,128)S(1)}, u32[]{:S(2)}, u32[]{:S(2)}) collective-permute-start(f32[8,96]{1,0:T(8,128)S(1)} %get-tuple-element.62), channel_id=1, source_target_pairs={{0,4},{2,6},{4,0},{6,2},{8,12},{10,14},{12,8},{14,10},{16,20},{18,... | collective-permute-start | bytes 9224 | tf_op jit(solution)/shard_map/ppermute | solution.py:22
  20.9 1.5 %collective-permute-start.8 = (f32[8,96]{1,0:T(8,128)S(1)}, f32[8,96]{1,0:T(8,128)S(1)}, u32[]{:S(2)}, u32[]{:S(2)}) collective-permute-start(f32[8,96]{1,0:T(8,128)S(1)} %get-tuple-element.63), channel_id=1, source_target_pairs={{0,2},{2,0},{4,6},{6,4},{8,10},{10,8},{12,14},{14,12},{16,18},{18,... | collective-permute-start | bytes 9224 | tf_op jit(solution)/shard_map/ppermute | solution.py:22
  22.4 1.0 %combine.1.inverse_ref = f32[16,96,96]{2,1,0:T(8,128)S(1)} custom-call(f32[1,16,96,96]{3,2,1,0:T(8,128)S(1)} %copy-done.2, s32[1,4,4]{2,1,0:T(4,128)S(1)} %copy-done.6, f32[4,72,128]{2,1,0:T(8,128)S(1)} %collective-permute-done.3.late_ref.refs_0_, f32[4,72,128]{2,1,0:T(8,128)S(1)} %collective-permute-done.2.refs_2_.refs_1_, ...), custom_call_target="tpu_custom_call" | custom-call | bytes 100000 | tf_op jit(solution)/shard_map/combine/pallas_call | solution.py:26
  23.4 1.1 %collective-permute-done.8.refs_3_ = f32[8,96]{1,0:T(8,128)S(1)} collective-permute-done((f32[8,96]{1,0:T(8,128)S(1)}, f32[8,96]{1,0:T(8,128)S(1)}, u32[]{:S(2)}, u32[]{:S(2)}) %collective-permute-start.8) | collective-permute-done | bytes 3104 | tf_op jit(solution)/shard_map/ppermute | solution.py:22
  24.5 0.7 %apply.2 = (f32[16,96]{1,0:T(8,128)S(1)}, f32[1,128]{1,0:T(1,128)S(1)}) custom-call(f32[1,16,96]{2,1,0:T(8,128)S(1)} %copy-done.4, f32[16,96]{1,0:T(8,128)S(1)} %get-tuple-element.58.z_ref.refs_3_.refs_4_, f32[16,96]{1,0:T(8,128)S(1)} %get-tuple-element.59.own_ref, f32[8,96]{1,0:T(8,128)S(1)} %collective-permute-done.5.refs_0_, ...), custom_call_target="tpu_custom_call" | custom-call | bytes 100000 | tf_op jit(solution)/shard_map/apply/pallas_call | solution.py:26
  25.2 0.1 collective-permute-start.9
  25.3 0.3 local_inverse.4
  25.6 0.8 %collective-permute-done.9.theirs_ref = f32[1,128]{1,0:T(1,128)S(1)} collective-permute-done((f32[1,128]{1,0:T(1,128)S(1)}, f32[1,128]{1,0:T(1,128)S(1)}, u32[]{:S(2)}, u32[]{:S(2)}) %collective-permute-start.9) | collective-permute-done | bytes 544 | tf_op jit(solution)/shard_map/ppermute | solution.py:464
  26.4 0.8 %spread.2 = (f32[16,96]{1,0:T(8,128)S(1)}, f32[16,96]{1,0:T(8,128)S(1)}, f32[8,96]{1,0:T(8,128)S(1)}, f32[8,96]{1,0:T(8,128)S(1)}, f32[8,96]{1,0:T(8,128)S(1)}, /*index=5*/f32[8,96]{1,0:T(8,128)S(1)}) custom-call(f32[16,96,128]{2,1,0:T(8,128)S(1)} %get-tuple-element.71.column_ref, f32[16,96]{1,0:T(8,128)S(1)} %get-tuple-element.72.row_ref, ...), custom_call_target="tpu_custom_call" | custom-call | bytes 100000 | tf_op jit(solution)/shard_map/spread/pallas_call | solution.py:26
  27.2 0.7 %collective-permute-start.10 = (f32[8,96]{1,0:T(8,128)S(1)}, f32[8,96]{1,0:T(8,128)S(1)}, u32[]{:S(2)}, u32[]{:S(2)}) collective-permute-start(f32[8,96]{1,0:T(8,128)S(1)} %get-tuple-element.76), channel_id=1, source_target_pairs={{0,16},{2,18},{4,20},{6,22},{8,24},{10,26},{12,28},{14,30},{16,0},... | collective-permute-start | bytes 9224 | tf_op jit(solution)/shard_map/ppermute | solution.py:22
  27.9 0.6 %collective-permute-start.11 = (f32[8,96]{1,0:T(8,128)S(1)}, f32[8,96]{1,0:T(8,128)S(1)}, u32[]{:S(2)}, u32[]{:S(2)}) collective-permute-start(f32[8,96]{1,0:T(8,128)S(1)} %get-tuple-element.77), channel_id=1, source_target_pairs={{0,8},{2,10},{4,12},{6,14},{8,0},{10,2},{12,4},{14,6},{16,24},{18,... | collective-permute-start | bytes 9224 | tf_op jit(solution)/shard_map/ppermute | solution.py:22
  28.5 0.5 collective-permute-start.12
  29.0 1.5 %collective-permute-start.13 = (f32[8,96]{1,0:T(8,128)S(1)}, f32[8,96]{1,0:T(8,128)S(1)}, u32[]{:S(2)}, u32[]{:S(2)}) collective-permute-start(f32[8,96]{1,0:T(8,128)S(1)} %get-tuple-element.79), channel_id=1, source_target_pairs={{0,2},{2,0},{4,6},{6,4},{8,10},{10,8},{12,14},{14,12},{16,18},{18,... | collective-permute-start | bytes 9224 | tf_op jit(solution)/shard_map/ppermute | solution.py:22
  30.5 1.3 %collective-permute-done.10.refs_0_ = f32[8,96]{1,0:T(8,128)S(1)} collective-permute-done((f32[8,96]{1,0:T(8,128)S(1)}, f32[8,96]{1,0:T(8,128)S(1)}, u32[]{:S(2)}, u32[]{:S(2)}) %collective-permute-start.10) | collective-permute-done | bytes 3104 | tf_op jit(solution)/shard_map/ppermute | solution.py:22
  31.8 0.3 collective-permute-done.12.refs_2_
  32.1 0.5 collective-permute-done.13.refs_3_
  32.6 0.7 %apply.3 = (f32[16,96]{1,0:T(8,128)S(1)}, f32[1,128]{1,0:T(1,128)S(1)}) custom-call(f32[16,96]{1,0:T(8,128)S(1)} %get-tuple-element.69.field_ref.refs_1_, f32[16,96]{1,0:T(8,128)S(1)} %get-tuple-element.74.z_ref.refs_4_.refs_5_, f32[16,96]{1,0:T(8,128)S(1)} %get-tuple-element.75.own_ref, f32[8,96]{1,0:T(8,128)S(1)} %collective-permute-done.10.refs_0_, ...), custom_call_target="tpu_custom_call" | custom-call | bytes 100000 | tf_op jit(solution)/shard_map/apply/pallas_call | solution.py:26
  33.2 0.1 collective-permute-start.14
  33.3 0.3 local_inverse.5
  33.6 0.8 %collective-permute-done.14.theirs_ref = f32[1,128]{1,0:T(1,128)S(1)} collective-permute-done((f32[1,128]{1,0:T(1,128)S(1)}, f32[1,128]{1,0:T(1,128)S(1)}, u32[]{:S(2)}, u32[]{:S(2)}) %collective-permute-start.14) | collective-permute-done | bytes 544 | tf_op jit(solution)/shard_map/ppermute | solution.py:464
  34.4 0.8 %spread.3 = (f32[16,96]{1,0:T(8,128)S(1)}, f32[16,96]{1,0:T(8,128)S(1)}, f32[8,96]{1,0:T(8,128)S(1)}, f32[8,96]{1,0:T(8,128)S(1)}, f32[8,96]{1,0:T(8,128)S(1)}, /*index=5*/f32[8,96]{1,0:T(8,128)S(1)}) custom-call(f32[16,96,128]{2,1,0:T(8,128)S(1)} %get-tuple-element.81.column_ref, f32[16,96]{1,0:T(8,128)S(1)} %get-tuple-element.82.row_ref, ...), custom_call_target="tpu_custom_call" | custom-call | bytes 100000 | tf_op jit(solution)/shard_map/spread/pallas_call | solution.py:26
  35.3 1.9 %collective-permute-start.15 = (f32[8,96]{1,0:T(8,128)S(1)}, f32[8,96]{1,0:T(8,128)S(1)}, u32[]{:S(2)}, u32[]{:S(2)}) collective-permute-start(f32[8,96]{1,0:T(8,128)S(1)} %get-tuple-element.86), channel_id=1, source_target_pairs={{0,16},{2,18},{4,20},{6,22},{8,24},{10,26},{12,28},{14,30},{16,0},... | collective-permute-start | bytes 9224 | tf_op jit(solution)/shard_map/ppermute | solution.py:22
  37.1 2.0 %collective-permute-start.16 = (f32[8,96]{1,0:T(8,128)S(1)}, f32[8,96]{1,0:T(8,128)S(1)}, u32[]{:S(2)}, u32[]{:S(2)}) collective-permute-start(f32[8,96]{1,0:T(8,128)S(1)} %get-tuple-element.87), channel_id=1, source_target_pairs={{0,8},{2,10},{4,12},{6,14},{8,0},{10,2},{12,4},{14,6},{16,24},{18,... | collective-permute-start | bytes 9224 | tf_op jit(solution)/shard_map/ppermute | solution.py:22
  39.1 1.5 %collective-permute-start.17 = (f32[8,96]{1,0:T(8,128)S(1)}, f32[8,96]{1,0:T(8,128)S(1)}, u32[]{:S(2)}, u32[]{:S(2)}) collective-permute-start(f32[8,96]{1,0:T(8,128)S(1)} %get-tuple-element.88), channel_id=1, source_target_pairs={{0,4},{2,6},{4,0},{6,2},{8,12},{10,14},{12,8},{14,10},{16,20},{18,... | collective-permute-start | bytes 9224 | tf_op jit(solution)/shard_map/ppermute | solution.py:22
  40.7 1.5 %collective-permute-start.18 = (f32[8,96]{1,0:T(8,128)S(1)}, f32[8,96]{1,0:T(8,128)S(1)}, u32[]{:S(2)}, u32[]{:S(2)}) collective-permute-start(f32[8,96]{1,0:T(8,128)S(1)} %get-tuple-element.89), channel_id=1, source_target_pairs={{0,2},{2,0},{4,6},{6,4},{8,10},{10,8},{12,14},{14,12},{16,18},{18,... | collective-permute-start | bytes 9224 | tf_op jit(solution)/shard_map/ppermute | solution.py:22
  42.2 0.6 %collective-permute-done.17.refs_9_ = f32[8,96]{1,0:T(8,128)S(1)} collective-permute-done((f32[8,96]{1,0:T(8,128)S(1)}, f32[8,96]{1,0:T(8,128)S(1)}, u32[]{:S(2)}, u32[]{:S(2)}) %collective-permute-start.17) | collective-permute-done | bytes 3104 | tf_op jit(solution)/shard_map/ppermute | solution.py:22
  42.8 1.5 %collective-permute-done.18.refs_10_ = f32[8,96]{1,0:T(8,128)S(1)} collective-permute-done((f32[8,96]{1,0:T(8,128)S(1)}, f32[8,96]{1,0:T(8,128)S(1)}, u32[]{:S(2)}, u32[]{:S(2)}) %collective-permute-start.18) | collective-permute-done | bytes 3104 | tf_op jit(solution)/shard_map/ppermute | solution.py:22
  44.3 0.7 %last_apply.1 = (f32[16,96]{1,0:T(8,128)S(1)}, f32[32,1,128]{2,1,0:T(1,128)S(1)}) custom-call(f32[1,16,96]{2,1,0:T(8,128)S(1)} %copy-done.4, f32[16,96]{1,0:T(8,128)S(1)} %get-tuple-element.69.field_ref.refs_1_, f32[16,96]{1,0:T(8,128)S(1)} %get-tuple-element.80.field_ref.refs_2_, f32[16,96]{1,0:T(8,128)S(1)} %get-tuple-element.58.z_ref.refs_3_.refs_4_, ...), custom_call_target="tpu_custom_call" | custom-call | bytes 100000 | tf_op jit(solution)/shard_map/last_apply/pallas_call | solution.py:26
  45.0 8.9 %all_to_all.5.dots_ref = f32[32,1,128]{2,1,0:T(1,128)S(1)} all-to-all(f32[32,1,128]{2,1,0:T(1,128)S(1)} %get-tuple-element.90), channel_id=1, replica_groups=mesh['sub'=16,'coarse'=2] {'sub','coarse'}, dimensions={0} | all-to-all | bytes 32768 | tf_op jit(solution)/shard_map/all_to_all | solution.py:571
  53.9 0.8 %finish.1 = (f32[1,16,96]{2,1,0:T(8,128)}, f32[1,16,96]{2,1,0:T(8,128)}) custom-call(f32[32,1,128]{2,1,0:T(1,128)S(1)} %all_to_all.5.dots_ref, f32[1,16,96]{2,1,0:T(8,128)S(1)} %copy-done.4, f32[16,96]{1,0:T(8,128)S(1)} %get-tuple-element.69.field_ref.refs_1_, f32[16,96]{1,0:T(8,128)S(1)} %get-tuple-element.80.field_ref.refs_2_, ...), custom_call_target="tpu_custom_call" | custom-call | bytes 100000 | tf_op jit(solution)/shard_map/finish/pallas_call | solution.py:26
  (24 shorter events, 0.1 us)
Async XLA Ops:
  0.6 1.1 %copy-start = (f32[1,16,96,96]{3,2,1,0:T(8,128)S(1)}, f32[1,16,96,96]{3,2,1,0:T(8,128)}, u32[]{:S(2)}) copy-start(f32[1,16,96,96]{3,2,1,0:T(8,128)} %refs_15_.1) | copy-start | bytes 1769476
  1.8 9.0 %copy-start.3 = (f32[1,16,6,96]{3,1,2,0:T(8,128)S(1)}, f32[1,16,6,96]{3,1,2,0:T(8,128)}, u32[]{:S(2)}) copy-start(f32[1,16,6,96]{3,1,2,0:T(8,128)} %param.15) | copy-start | bytes 110596
  1.8 9.0 %copy-start.4 = (f32[1,16,96]{2,1,0:T(8,128)S(1)}, f32[1,16,96]{2,1,0:T(8,128)}, u32[]{:S(2)}) copy-start(f32[1,16,96]{2,1,0:T(8,128)} %refs_0_.5) | copy-start | bytes 18436
  1.8 9.0 %copy-start.8 = (s32[1,16]{1,0:T(1,128)S(1)}, s32[1,16]{1,0:T(1,128)}, u32[]{:S(2)}) copy-start(s32[1,16]{1,0:T(1,128)} %aggregate_ref.1) | copy-start | bytes 196
  1.8 9.7 %copy-start.2 = (f32[1,16,96,96]{3,2,1,0:T(8,128)S(1)}, f32[1,16,96,96]{3,2,1,0:T(8,128)}, u32[]{:S(2)}) copy-start(f32[1,16,96,96]{3,2,1,0:T(8,128)} %inverse_ref.3) | copy-start | bytes 1769476
  1.8 10.0 %copy-start.6 = (s32[1,4,4]{2,1,0:T(4,128)S(1)}, s32[1,4,4]{2,1,0:T(4,128)}, u32[]{:S(2)}) copy-start(s32[1,4,4]{2,1,0:T(4,128)} %senders_ref.3) | copy-start | bytes 196
  1.8 10.0 %copy-start.7 = (s32[1,16,6]{1,0,2:T(1,128)S(1)}, s32[1,16,6]{1,0,2:T(1,128)}, u32[]{:S(2)}) copy-start(s32[1,16,6]{1,0,2:T(1,128)} %param.11) | copy-start | bytes 1156
  1.8 12.7 %copy-start.1 = (f32[1,16,6,96,96]{4,3,2,1,0:T(8,128)S(1)}, f32[1,16,6,96,96]{4,3,2,1,0:T(8,128)}, u32[]{:S(2)}) copy-start(f32[1,16,6,96,96]{4,3,2,1,0:T(8,128)} %refs_11_.3) | copy-start | bytes 10616836
  1.8 12.7 %copy-start.5 = (f32[1,48,48]{2,1,0:T(8,128)S(1)}, f32[1,48,48]{2,1,0:T(8,128)}, u32[]{:S(2)}) copy-start(f32[1,48,48]{2,1,0:T(8,128)} %solver_ref.3) | copy-start | bytes 27652
  2.0 11.2 %collective-permute-start = (f32[4,72,128]{2,1,0:T(8,128)S(1)}, f32[4,72,128]{2,1,0:T(8,128)S(1)}, u32[]{:S(2)}, u32[]{:S(2)}) collective-permute-start(f32[4,72,128]{2,1,0:T(8,128)S(1)} %get-tuple-element.50), channel_id=1, source_target_pairs={{0,16},{2,18},{4,20},{6,22},{8,24},{10,26},{12,28},{14,30},{16,0},... | collective-permute-start | bytes 442376 | tf_op jit(solution)/shard_map/ppermute | solution.py:22
  6.1 7.3 %collective-permute-start.1 = (f32[4,72,128]{2,1,0:T(8,128)S(1)}, f32[4,72,128]{2,1,0:T(8,128)S(1)}, u32[]{:S(2)}, u32[]{:S(2)}) collective-permute-start(f32[4,72,128]{2,1,0:T(8,128)S(1)} %get-tuple-element.51), channel_id=1, source_target_pairs={{0,8},{2,10},{4,12},{6,14},{8,0},{10,2},{12,4},{14,6},{16,24},{18,... | collective-permute-start | bytes 442376 | tf_op jit(solution)/shard_map/ppermute | solution.py:22
  7.7 5.7 %collective-permute-start.2 = (f32[4,72,128]{2,1,0:T(8,128)S(1)}, f32[4,72,128]{2,1,0:T(8,128)S(1)}, u32[]{:S(2)}, u32[]{:S(2)}) collective-permute-start(f32[4,72,128]{2,1,0:T(8,128)S(1)} %get-tuple-element.52), channel_id=1, source_target_pairs={{0,4},{2,6},{4,0},{6,2},{8,12},{10,14},{12,8},{14,10},{16,20},{18,... | collective-permute-start | bytes 442376 | tf_op jit(solution)/shard_map/ppermute | solution.py:22
  9.2 5.2 %collective-permute-start.3 = (f32[4,72,128]{2,1,0:T(8,128)S(1)}, f32[4,72,128]{2,1,0:T(8,128)S(1)}, u32[]{:S(2)}, u32[]{:S(2)}) collective-permute-start(f32[4,72,128]{2,1,0:T(8,128)S(1)} %get-tuple-element.53), channel_id=1, source_target_pairs={{0,2},{2,0},{4,6},{6,4},{8,10},{10,8},{12,14},{14,12},{16,18},{18,... | collective-permute-start | bytes 442376 | tf_op jit(solution)/shard_map/ppermute | solution.py:22
  11.4 3.1 %collective-permute-start.4 = (f32[1,128]{1,0:T(1,128)S(1)}, f32[1,128]{1,0:T(1,128)S(1)}, u32[]{:S(2)}, u32[]{:S(2)}) collective-permute-start(f32[1,128]{1,0:T(1,128)S(1)} %get-tuple-element.54.refs_0_), channel_id=1, source_target_pairs={{0,1},{1,0},{2,3},{3,2},{4,5},{5,4},{6,7},{7,6},{8,9},{9,8},{10,11... | collective-permute-start | bytes 1544 | tf_op jit(solution)/shard_map/ppermute | solution.py:464
  15.5 7.9 %collective-permute-start.5 = (f32[8,96]{1,0:T(8,128)S(1)}, f32[8,96]{1,0:T(8,128)S(1)}, u32[]{:S(2)}, u32[]{:S(2)}) collective-permute-start(f32[8,96]{1,0:T(8,128)S(1)} %get-tuple-element.60), channel_id=1, source_target_pairs={{0,16},{2,18},{4,20},{6,22},{8,24},{10,26},{12,28},{14,30},{16,0},... | collective-permute-start | bytes 9224 | tf_op jit(solution)/shard_map/ppermute | solution.py:22
  17.0 6.4 %collective-permute-start.6 = (f32[8,96]{1,0:T(8,128)S(1)}, f32[8,96]{1,0:T(8,128)S(1)}, u32[]{:S(2)}, u32[]{:S(2)}) collective-permute-start(f32[8,96]{1,0:T(8,128)S(1)} %get-tuple-element.61), channel_id=1, source_target_pairs={{0,8},{2,10},{4,12},{6,14},{8,0},{10,2},{12,4},{14,6},{16,24},{18,... | collective-permute-start | bytes 9224 | tf_op jit(solution)/shard_map/ppermute | solution.py:22
  19.4 4.0 %collective-permute-start.7 = (f32[8,96]{1,0:T(8,128)S(1)}, f32[8,96]{1,0:T(8,128)S(1)}, u32[]{:S(2)}, u32[]{:S(2)}) collective-permute-start(f32[8,96]{1,0:T(8,128)S(1)} %get-tuple-element.62), channel_id=1, source_target_pairs={{0,4},{2,6},{4,0},{6,2},{8,12},{10,14},{12,8},{14,10},{16,20},{18,... | collective-permute-start | bytes 9224 | tf_op jit(solution)/shard_map/ppermute | solution.py:22
  20.9 3.6 %collective-permute-start.8 = (f32[8,96]{1,0:T(8,128)S(1)}, f32[8,96]{1,0:T(8,128)S(1)}, u32[]{:S(2)}, u32[]{:S(2)}) collective-permute-start(f32[8,96]{1,0:T(8,128)S(1)} %get-tuple-element.63), channel_id=1, source_target_pairs={{0,2},{2,0},{4,6},{6,4},{8,10},{10,8},{12,14},{14,12},{16,18},{18,... | collective-permute-start | bytes 9224 | tf_op jit(solution)/shard_map/ppermute | solution.py:22
  25.2 1.2 %collective-permute-start.9 = (f32[1,128]{1,0:T(1,128)S(1)}, f32[1,128]{1,0:T(1,128)S(1)}, u32[]{:S(2)}, u32[]{:S(2)}) collective-permute-start(f32[1,128]{1,0:T(1,128)S(1)} %get-tuple-element.73.mine_ref), channel_id=1, source_target_pairs={{0,1},{1,0},{2,3},{3,2},{4,5},{5,4},{6,7},{7,6},{8,9},{9,8},{10,11... | collective-permute-start | bytes 1544 | tf_op jit(solution)/shard_map/ppermute | solution.py:464
  27.2 4.6 %collective-permute-start.10 = (f32[8,96]{1,0:T(8,128)S(1)}, f32[8,96]{1,0:T(8,128)S(1)}, u32[]{:S(2)}, u32[]{:S(2)}) collective-permute-start(f32[8,96]{1,0:T(8,128)S(1)} %get-tuple-element.76), channel_id=1, source_target_pairs={{0,16},{2,18},{4,20},{6,22},{8,24},{10,26},{12,28},{14,30},{16,0},... | collective-permute-start | bytes 9224 | tf_op jit(solution)/shard_map/ppermute | solution.py:22
  27.9 3.9 %collective-permute-start.11 = (f32[8,96]{1,0:T(8,128)S(1)}, f32[8,96]{1,0:T(8,128)S(1)}, u32[]{:S(2)}, u32[]{:S(2)}) collective-permute-start(f32[8,96]{1,0:T(8,128)S(1)} %get-tuple-element.77), channel_id=1, source_target_pairs={{0,8},{2,10},{4,12},{6,14},{8,0},{10,2},{12,4},{14,6},{16,24},{18,... | collective-permute-start | bytes 9224 | tf_op jit(solution)/shard_map/ppermute | solution.py:22
  28.5 3.6 %collective-permute-start.12 = (f32[8,96]{1,0:T(8,128)S(1)}, f32[8,96]{1,0:T(8,128)S(1)}, u32[]{:S(2)}, u32[]{:S(2)}) collective-permute-start(f32[8,96]{1,0:T(8,128)S(1)} %get-tuple-element.78), channel_id=1, source_target_pairs={{0,4},{2,6},{4,0},{6,2},{8,12},{10,14},{12,8},{14,10},{16,20},{18,... | collective-permute-start | bytes 9224 | tf_op jit(solution)/shard_map/ppermute | solution.py:22
  29.0 3.6 %collective-permute-start.13 = (f32[8,96]{1,0:T(8,128)S(1)}, f32[8,96]{1,0:T(8,128)S(1)}, u32[]{:S(2)}, u32[]{:S(2)}) collective-permute-start(f32[8,96]{1,0:T(8,128)S(1)} %get-tuple-element.79), channel_id=1, source_target_pairs={{0,2},{2,0},{4,6},{6,4},{8,10},{10,8},{12,14},{14,12},{16,18},{18,... | collective-permute-start | bytes 9224 | tf_op jit(solution)/shard_map/ppermute | solution.py:22
  33.2 1.2 %collective-permute-start.14 = (f32[1,128]{1,0:T(1,128)S(1)}, f32[1,128]{1,0:T(1,128)S(1)}, u32[]{:S(2)}, u32[]{:S(2)}) collective-permute-start(f32[1,128]{1,0:T(1,128)S(1)} %get-tuple-element.83.mine_ref), channel_id=1, source_target_pairs={{0,1},{1,0},{2,3},{3,2},{4,5},{5,4},{6,7},{7,6},{8,9},{9,8},{10,11... | collective-permute-start | bytes 1544 | tf_op jit(solution)/shard_map/ppermute | solution.py:464
  35.3 6.9 %collective-permute-start.15 = (f32[8,96]{1,0:T(8,128)S(1)}, f32[8,96]{1,0:T(8,128)S(1)}, u32[]{:S(2)}, u32[]{:S(2)}) collective-permute-start(f32[8,96]{1,0:T(8,128)S(1)} %get-tuple-element.86), channel_id=1, source_target_pairs={{0,16},{2,18},{4,20},{6,22},{8,24},{10,26},{12,28},{14,30},{16,0},... | collective-permute-start | bytes 9224 | tf_op jit(solution)/shard_map/ppermute | solution.py:22
  37.1 5.0 %collective-permute-start.16 = (f32[8,96]{1,0:T(8,128)S(1)}, f32[8,96]{1,0:T(8,128)S(1)}, u32[]{:S(2)}, u32[]{:S(2)}) collective-permute-start(f32[8,96]{1,0:T(8,128)S(1)} %get-tuple-element.87), channel_id=1, source_target_pairs={{0,8},{2,10},{4,12},{6,14},{8,0},{10,2},{12,4},{14,6},{16,24},{18,... | collective-permute-start | bytes 9224 | tf_op jit(solution)/shard_map/ppermute | solution.py:22
  39.1 3.6 %collective-permute-start.17 = (f32[8,96]{1,0:T(8,128)S(1)}, f32[8,96]{1,0:T(8,128)S(1)}, u32[]{:S(2)}, u32[]{:S(2)}) collective-permute-start(f32[8,96]{1,0:T(8,128)S(1)} %get-tuple-element.88), channel_id=1, source_target_pairs={{0,4},{2,6},{4,0},{6,2},{8,12},{10,14},{12,8},{14,10},{16,20},{18,... | collective-permute-start | bytes 9224 | tf_op jit(solution)/shard_map/ppermute | solution.py:22
  40.7 3.6 %collective-permute-start.18 = (f32[8,96]{1,0:T(8,128)S(1)}, f32[8,96]{1,0:T(8,128)S(1)}, u32[]{:S(2)}, u32[]{:S(2)}) collective-permute-start(f32[8,96]{1,0:T(8,128)S(1)} %get-tuple-element.89), channel_id=1, source_target_pairs={{0,2},{2,0},{4,6},{6,4},{8,10},{10,8},{12,14},{14,12},{16,18},{18,... | collective-permute-start | bytes 9224 | tf_op jit(solution)/shard_map/ppermute | solution.py:22

commit v4 on v3

--- a/solution.py
+++ b/solution.py
@@ -93,7 +93,7 @@
 def pack_kernel(margin_ref, *refs):
     outs = refs[REPEATS:]
     turns = len(outs)
-    ghosts = margin_ref.shape[1] // turns
+    ghosts, _, _ = outs[0].shape
     width = margin_ref.shape[2]
     tall = width * width // 128
     side = 128 - width
@@ -165,58 +165,85 @@
         parts_ref[at : at + 1, :] = jnp.sum(part, axis=0, keepdims=True)
 
 
-def finish_spread(parts_ref, slots_ref, indices_ref, z_ref, own_ref, packets):
-    turns = len(packets)
-    rows = z_ref.shape[0]
-    ghosts = packets[0].shape[0] // 2
+def scatter_rows(parts_ref, slots_ref, indices_ref, rows):
     slots = slots_ref.shape[0]
     for i in range(rows):
         slots_ref[0, i : i + 1, :] = parts_ref[i * slots : i * slots + 1, :]
         for j in range(1, slots):
             at = i * slots + j
             slots_ref[j, pl.ds(indices_ref[0, at], 1), :] = parts_ref[at : at + 1, :]
+    spread = slots_ref[0]
+    for j in range(1, slots):
+        spread = spread + slots_ref[j]
+    return spread
+
+
+def finish_spread(parts_ref, slots_ref, indices_ref, z_ref, own_ref, packets):
+    turns = len(packets)
+    rows = z_ref.shape[0]
+    ghosts = packets[0].shape[0] // 2
+    spread = scatter_rows(parts_ref, slots_ref, indices_ref, rows)
+    own_ref[...] = spread[:rows]
     for turn in range(turns):
         for g in range(ghosts):
             at = indices_ref[1, turn * ghosts + g]
             packets[turn][g : g + 1, :] = z_ref[pl.ds(at, 1), :]
-    spread = slots_ref[0]
-    for j in range(1, slots):
-        spread = spread + slots_ref[j]
-    own_ref[...] = spread[:rows]
-    for turn in range(turns):
         start = rows + turn * ghosts
         packets[turn][ghosts:, :] = spread[start : start + ghosts]
 
 
-def margin_row(packed_ref, g, row, eye):
+def margin_row(packed_ref, g, wide_ref, at, eye, inside):
+    pieces = wide_ref.shape[0]
     tall = packed_ref.shape[1]
-    width = row.shape[1]
+    rest = tall // pieces
+    products = [
+        packed_ref[g, piece * rest : (piece + 1) * rest, :] * wide_ref[piece, at : at + 1, :]
+        for piece in range(pieces)
+    ]
+    beside = products[0]
+    for product in products[1:]:
+        beside = beside + product
+    main = [jnp.where(inside, product, 0.0) for product in products]
+    columns = [jnp.sum(part, axis=1, keepdims=True) for part in main]
+    columns.append(jnp.sum(jnp.where(inside, 0.0, beside), axis=1, keepdims=True))
+    row = None
+    for piece, column in enumerate(columns):
+        part = jnp.where(eye[piece * rest : (piece + 1) * rest], column, 0.0)
+        row = part if row is None else row + part
+    return jnp.sum(row, axis=0, keepdims=True)
+
+
+def margin_rows(packed, wide_ref, eye):
+    ghosts = packed[0].shape[0]
+    width = eye.shape[0]
+    inside = lax.broadcasted_iota(jnp.int32, (1, 128), 1) < width
+    out = []
+    for turn, ref in enumerate(packed):
+        for g in range(ghosts):
+            out.append(margin_row(ref, g, wide_ref, turn * ghosts + g, eye, inside))
+    return jnp.concatenate(out, axis=0)
+
+
+def base_kernel(
+    field_ref,
+    send_ref,
+    row_ref,
+    mine_ref,
+    theirs_ref,
+    solver_ref,
+    null_ref,
+    offset_ref,
+    base_ref,
+    wide_ref,
+):
+    picked = select_rows(send_ref, field_ref[0])
+    width = picked.shape[1]
     side = 128 - width
-    rest = width - tall
-    column = jnp.sum(packed_ref[g, :, 0:width] * row, axis=1, keepdims=True)
-    beside = jnp.zeros((rest, side), f32)
-    for piece in range(width // side):
-        beside = (
-            beside
-            + packed_ref[g, piece * rest : (piece + 1) * rest, width:128]
-            * row[:, piece * side : (piece + 1) * side]
-        )
-    beside = jnp.sum(beside, axis=1, keepdims=True)
-    return to_row(column, eye[:tall]) + to_row(beside, eye[tall:])
-
-
-def margin_kernel(turns, field_ref, send_ref, *refs):
-    early = refs[:turns][::-1]
-    out_ref, picked_ref = refs[turns:]
-    ghosts = early[0].shape[0]
-    eye = eye_mask(out_ref.shape[1])
-    picked_ref[...] = select_rows(send_ref, field_ref[0])
-    first = out_ref.shape[0] // ghosts - turns
-    out_ref[...] = picked_ref[...]
-    for turn in range(turns):
-        for g in range(ghosts):
-            at = (first + turn) * ghosts + g
-            out_ref[at : at + 1, :] = margin_row(early[turn], g, picked_ref[at : at + 1, :], eye)
+    for piece in range(wide_ref.shape[0]):
+        wide_ref[piece, :, :width] = picked
+        wide_ref[piece, :, width:] = picked[:, piece * side : (piece + 1) * side]
+    coarse = coarse_field(mine_ref, theirs_ref, solver_ref, null_ref, offset_ref)
+    base_ref[...] = row_ref[...] + coarse
 
 
 def combine_kernel(turns, inverse_ref, senders_ref, *refs):
@@ -237,42 +264,26 @@
                 ]
 
 
-def first_kernel(turns, column_ref, row_ref, margin_ref, late_ref, *refs):
-    (
-        mine_ref,
-        theirs_ref,
-        solver_ref,
-        null_ref,
-        offset_ref,
-        back_ref,
-        blocks_ref,
-        index_ref,
-        z_ref,
-        own_ref,
-    ) = refs[:10]
-    packets = refs[10 : turns + 10]
-    parts_ref, slots_ref, indices_ref, sem = refs[turns + 10 :]
+def first_kernel(turns, *refs):
+    packed = refs[:turns][::-1]
+    base_ref, wide_ref, back_ref, blocks_ref, index_ref, z_ref, own_ref = refs[turns : turns + 7]
+    packets = refs[turns + 7 : 2 * turns + 7]
+    parts_ref, slots_ref, indices_ref, sem = refs[2 * turns + 7 :]
     fetch = pltpu.make_async_copy(index_ref, indices_ref, sem)
     fetch.start()
     slots_ref[...] = jnp.zeros(slots_ref.shape, f32)
     rows, width = z_ref.shape
-    ghosts = late_ref.shape[0]
     eye = eye_mask(width)
-    late = [margin_row(late_ref, g, margin_ref[g : g + 1, :], eye) for g in range(ghosts)]
-    margin = jnp.concatenate(late + [margin_ref[ghosts:, :]], axis=0)
-    coarse = coarse_field(mine_ref, theirs_ref, solver_ref, null_ref, offset_ref)
-    added = coarse + select_rows(back_ref, margin)
-    z = row_ref[...] + added
+    margin = margin_rows(packed, wide_ref, eye)
+    z = base_ref[...] + select_rows(back_ref, margin)
     z_ref[...] = z
     for i in range(rows):
-        column = column_ref[i][:, :width] + to_column(added[i : i + 1], eye)
-        spread_block_row(blocks_ref, parts_ref, i, column)
+        spread_block_row(blocks_ref, parts_ref, i, to_column(z[i : i + 1], eye))
     fetch.wait()
     finish_spread(parts_ref, slots_ref, indices_ref, z_ref, own_ref, packets)
 
 
-def spread_kernel(
-    turns,
+def spread_rows(
     column_ref,
     row_ref,
     mine_ref,
@@ -281,36 +292,108 @@
     null_ref,
     offset_ref,
     blocks_ref,
-    index_ref,
     z_ref,
-    own_ref,
-    *refs,
+    parts_ref,
 ):
-    packets = refs[:turns]
-    parts_ref, slots_ref, indices_ref, sem = refs[turns:]
+    rows, width = z_ref.shape
+    eye = eye_mask(width)
+    coarse = coarse_field(mine_ref, theirs_ref, solver_ref, null_ref, offset_ref)
+    z_ref[...] = row_ref[...] + coarse
+    for i in range(rows):
+        column = column_ref[i][:, :width] + to_column(coarse[i : i + 1], eye)
+        spread_block_row(blocks_ref, parts_ref, i, column)
+
+
+def spread_kernel(turns, *refs):
+    index_ref, z_ref, own_ref = refs[8:11]
+    packets = refs[11 : 11 + turns]
+    parts_ref, slots_ref, indices_ref, sem = refs[11 + turns :]
     fetch = pltpu.make_async_copy(index_ref, indices_ref, sem)
     fetch.start()
     slots_ref[...] = jnp.zeros(slots_ref.shape, f32)
-    rows, width = z_ref.shape
-    eye = eye_mask(width)
-    coarse = coarse_field(mine_ref, theirs_ref, solver_ref, null_ref, offset_ref)
-    z = row_ref[...] + coarse
-    z_ref[...] = z
-    for i in range(rows):
-        column = column_ref[i][:, :width] + to_column(coarse[i : i + 1], eye)
-        spread_block_row(blocks_ref, parts_ref, i, column)
+    spread_rows(*refs[:8], z_ref, parts_ref)
     fetch.wait()
     finish_spread(parts_ref, slots_ref, indices_ref, z_ref, own_ref, packets)
 
 
-def apply_rows(arrived, z, own_ref, blocks_ref, pick_ref, back_ref, picked_ref):
+def dot_at(lane, at, first, second, packed):
+    dot = jnp.sum(jnp.sum(first * second, axis=0, keepdims=True), axis=1, keepdims=True)
+    return jnp.where(lane == at, dot, packed)
+
+
+def early_dots_kernel(fields, *refs):
+    value_refs = refs[:fields]
+    z_refs = refs[fields:-1]
+    rows, width = z_refs[0].shape
+    lane = lax.broadcasted_iota(jnp.int32, (1, 128), 1)
+    packed = jnp.zeros((1, 128), f32)
+    for a in range(fields):
+        value = value_refs[a][...].reshape(rows, width)
+        for c, z_at in enumerate(z_refs):
+            packed = dot_at(lane, width + a * fields + c, value, z_at[...], packed)
+    refs[-1][...] = packed
+
+
+def last_spread_kernel(fields, *refs):
+    index_ref, early_ref = refs[8:10]
+    value_refs = refs[10 : 10 + fields]
+    z_ref, own_ref, payload_ref, parts_ref, slots_ref, line_ref, indices_ref, sem = refs[10 + fields :]
+    fetch = pltpu.make_async_copy(index_ref, indices_ref, sem)
+    fetch.start()
+    slots_ref[...] = jnp.zeros(slots_ref.shape, f32)
+    line_ref[...] = jnp.zeros(line_ref.shape, f32)
+    spread_rows(*refs[:8], z_ref, parts_ref)
+    rows, width = z_ref.shape
+    ghosts = line_ref.shape[0] // 2
+    z = z_ref[...]
+    lane = lax.broadcasted_iota(jnp.int32, (1, 128), 1)
+    packed = early_ref[...]
+    for a in range(fields):
+        value = value_refs[a][...].reshape(rows, width)
+        packed = dot_at(lane, width + a * fields + fields - 1, value, z, packed)
+    fetch.wait()
+    spread = scatter_rows(parts_ref, slots_ref, indices_ref, rows)
+    own = spread[:rows]
+    own_ref[...] = own
+    packed = dot_at(lane, width + fields * fields, z, own, packed)
+    line_ref[0:1, :] = packed
+    line_ref[0:ghosts, :width] = spread[rows:]
+    for at in range(ghosts):
+        line_ref[ghosts + at : ghosts + at + 1, :width] = z_ref[pl.ds(indices_ref[1, at], 1), :]
+    line = line_ref[...]
+    for device in range(payload_ref.shape[0]):
+        payload_ref[device] = line
+
+
+def total_kernel(bits, fields, width, lines_ref, out_ref):
+    devices, height = lines_ref.shape[:2]
+    ghosts = height // 2
+    each = ghosts // len(bits)
+    lane = lax.broadcasted_iota(jnp.int32, (1, 128), 1)
+    packed = lines_ref[0, 0:1, :]
+    for device in range(1, devices):
+        packed = packed + lines_ref[device, 0:1, :]
+    crossed = jnp.zeros((each, 128), f32)
+    for device in range(devices):
+        for turn, bit in enumerate(bits):
+            start = turn * each
+            crossed = crossed + (
+                lines_ref[device, start : start + each, :]
+                * lines_ref[device ^ (1 << bit), ghosts + start : ghosts + start + each, :]
+            )
+    crossed = jnp.where(lane < width, jnp.sum(crossed, axis=0, keepdims=True), 0.0)
+    crossed = jnp.sum(crossed, axis=1, keepdims=True)
+    at = lane == width + fields * fields
+    out_ref[...] = packed + jnp.where(at, crossed, 0.0)
+
+
+def apply_rows(rims, returned, z, own_ref, blocks_ref, pick_ref, back_ref, picked_ref):
     rows, width = z.shape
     slots = blocks_ref.shape[2]
-    ghosts = arrived[0].shape[0] // 2
     eye = eye_mask(width)
-    extended = jnp.concatenate([z] + [ref[0:ghosts, :] for ref in arrived], axis=0)
+    extended = jnp.concatenate([z] + rims, axis=0)
     picked_ref[...] = select_rows(pick_ref, extended)
-    returned = jnp.concatenate([ref[ghosts:, :] for ref in arrived], axis=0)
+    returned = jnp.concatenate(returned, axis=0)
     back = own_ref[...] + select_rows(back_ref, returned)
     image = []
     for i in range(rows):
@@ -336,48 +419,63 @@
         coarse_ref,
         picked_ref,
     ) = refs[turns:]
-    image = apply_rows(arrived, z_ref[...], own_ref, blocks_ref, pick_ref, back_ref, picked_ref)
+    ghosts = arrived[0].shape[0] // 2
+    rims = [ref[0:ghosts, :] for ref in arrived]
+    returned = [ref[ghosts:, :] for ref in arrived]
+    image = apply_rows(
+        rims, returned, z_ref[...], own_ref, blocks_ref, pick_ref, back_ref, picked_ref
+    )
     following = image - SHIFT * field_ref[...].reshape(image.shape)
     next_ref[...] = following
     coarse_ref[...] = restrict(null_ref, offset_ref, following)
 
 
-def last_kernel(turns, fields, *refs):
-    field_refs = refs[:fields]
-    z_refs = refs[fields : 2 * fields]
-    own_ref = refs[2 * fields]
-    arrived = refs[2 * fields + 1 : 2 * fields + 1 + turns][::-1]
-    blocks_ref, pick_ref, back_ref, next_ref, dots_ref, picked_ref = refs[2 * fields + 1 + turns :]
+def last_kernel(
+    bits,
+    field_ref,
+    z_ref,
+    own_ref,
+    lines_ref,
+    blocks_ref,
+    pick_ref,
+    back_ref,
+    next_ref,
+    picked_ref,
+):
+    width = z_ref.shape[1]
+    ghosts = lines_ref.shape[1] // 2
+    each = ghosts // len(bits)
+    here = lax.axis_index("sub")
+    rims = []
+    returned = []
+    for turn, bit in enumerate(bits):
+        start = turn * each
+        there = jnp.bitwise_xor(here, 1 << bit)
+        returned.append(lines_ref[there, start : start + each, :width])
+        rims.append(lines_ref[there, ghosts + start : ghosts + start + each, :width])
     image = apply_rows(
-        arrived, z_refs[-1][...], own_ref, blocks_ref, pick_ref, back_ref, picked_ref
-    )
-    following = image - SHIFT * field_refs[-1][...]
-    next_ref[...] = following
-    lane = lax.broadcasted_iota(jnp.int32, (1, 128), 1)
-    values = [ref[...].reshape(image.shape) for ref in field_refs] + [following]
-    packed = jnp.zeros((1, 128), f32)
-    for a, value in enumerate(values):
-        for c, z_at in enumerate(z_refs):
-            column = jnp.sum(value * z_at[...], axis=0, keepdims=True)
-            dot = jnp.sum(column, axis=1, keepdims=True)
-            packed = jnp.where(lane == a * fields + c, dot, packed)
-    dots_ref[...] = jnp.broadcast_to(packed.reshape(1, 1, 128), dots_ref.shape)
-
-
-def finish_kernel(fields, dots_ref, *refs):
+        rims, returned, z_ref[...], own_ref, blocks_ref, pick_ref, back_ref, picked_ref
+    )
+    next_ref[...] = image - SHIFT * field_ref[...]
+
+
+def finish_kernel(fields, mine_ref, theirs_ref, *refs):
     value_refs = refs[: fields + 1]
     z_refs = refs[fields + 1 : 2 * fields + 1]
     solution_ref, residual_ref = refs[2 * fields + 1 :]
-    total = jnp.sum(dots_ref[...], axis=0)
+    total = mine_ref[...] + theirs_ref[...]
     lane = lax.broadcasted_iota(jnp.int32, (1, 128), 1)
     shape = solution_ref.shape[1:]
-    gram = [
-        [
-            jnp.sum(jnp.where(lane == a * fields + c, total, 0.0), axis=1, keepdims=True)
-            for c in range(fields)
-        ]
-        for a in range(fields + 1)
-    ]
+    width = shape[1]
+
+    def product(at):
+        return jnp.sum(jnp.where(lane == width + at, total, 0.0), axis=1, keepdims=True)
+
+    gram = [[product(a * fields + c) for c in range(fields)] for a in range(fields)]
+    last = fields - 1
+    final = [gram[c + 1][last] + SHIFT * gram[c][last] for c in range(last)]
+    final.append(product(fields * fields))
+    gram.append([final[c] - SHIFT * gram[last][c] for c in range(fields)])
     zero = jnp.zeros((1, 1), f32)
     one = jnp.ones((1, 1), f32)
 
@@ -445,7 +543,6 @@
     modes = near_null.shape[2]
     levels = lax.axis_size("sub").bit_length() - 1
     bits = [turn * levels // turns for turn in range(turns)]
-    devices = lax.axis_size("sub") * lax.axis_size("coarse")
     flip = [(0, 1), (1, 0)]
     row_shape = (rows, width)
     packet = (2 * ghosts, width)
@@ -493,27 +590,25 @@
         name="tables",
     )
     source, null_modes, held, solver = right_side, null_view, blocks, coarse_inverse
-    column, row = call(
+    _, row = call(
         local_kernel,
         [(rows, width, 128), row_shape],
         [VMEM, VMEM],
         [right_side, inverse_blocks],
         name="local_inverse",
     )
-    (margin,) = call(
-        functools.partial(margin_kernel, turns - 1),
-        [(ghost_total, width)],
-        [VMEM] * (turns + 1),
-        [source, send, *gathered[:0:-1]],
-        scratch=[pltpu.VMEM((ghost_total, width), f32)],
-        name="margin_rows",
+    base, wide = call(
+        base_kernel,
+        [row_shape, (width // (128 - width), ghost_total, 128)],
+        [VMEM] * 8,
+        [source, send, row, mine, theirs, solver, null_modes, offset],
+        name="first_base",
     )
     z, own, *packets = call(
         functools.partial(first_kernel, turns),
         [row_shape, row_shape] + [packet] * turns,
-        [VMEM] * 12,
-        [column, row, margin, gathered[0], mine, theirs, solver, null_modes, offset, back]
-        + [held, index],
+        [VMEM] * (turns + 5),
+        [*gathered[::-1], base, wide, back, held, index],
         scratch=spread_scratch,
         name="first_spread",
     )
@@ -526,13 +621,11 @@
     )
     values = [source]
     fields = [z]
-    for step in range(ITERS):
+    for step in range(ITERS - 1):
         arrived = [partner(packets[turn], "sub", bits[turn]) for turn in range(turns)]
         if step == 0:
             combined, *arrived = lax.optimization_barrier([combined, *arrived[::-1]])
             arrived = arrived[::-1]
-        if step + 1 == ITERS:
-            break
         following, mine = call(
             functools.partial(apply_kernel, turns),
             [row_shape, (1, 128)],
@@ -550,30 +643,58 @@
             [following, combined],
             name="local_inverse",
         )
-        z, own, *packets = call(
-            functools.partial(spread_kernel, turns),
-            [row_shape, row_shape] + [packet] * turns,
-            [VMEM] * 9,
-            [column, row, mine, theirs, solver, null_modes, offset, held, index],
-            scratch=spread_scratch,
-            name="spread",
-        )
+        inputs = [column, row, mine, theirs, solver, null_modes, offset, held, index]
+        if step + 2 < ITERS:
+            z, own, *packets = call(
+                functools.partial(spread_kernel, turns),
+                [row_shape, row_shape] + [packet] * turns,
+                [VMEM] * 9,
+                inputs,
+                scratch=spread_scratch,
+                name="spread",
+            )
+        else:
+            (early,) = call(
+                functools.partial(early_dots_kernel, ITERS),
+                [(1, 128)],
+                [VMEM] * (2 * ITERS - 1),
+                [*values, *fields],
+                name="early_dots",
+            )
+            z, own, payload = call(
+                functools.partial(last_spread_kernel, ITERS),
+                [row_shape, row_shape, (lax.axis_size("sub"), 2 * ghost_total, 128)],
+                [VMEM] * (10 + ITERS),
+                [*inputs, early, *values],
+                scratch=spread_scratch[:2]
+                + [pltpu.VMEM((2 * ghost_total, 128), f32)]
+                + spread_scratch[2:],
+                name="last_spread",
+            )
         fields.append(z)
-    following, dots = call(
-        functools.partial(last_kernel, turns, ITERS),
-        [row_shape, (devices, 1, 128)],
-        [VMEM] * (2 * ITERS + 1 + turns + 3),
-        [*values, *fields, own, *arrived[::-1], held, pick, back],
+    lines = lax.all_to_all(payload, "sub", 0, 0)
+    (mine,) = call(
+        functools.partial(total_kernel, bits, ITERS, width),
+        [(1, 128)],
+        [VMEM],
+        [lines],
+        name="totals",
+    )
+    theirs = swap(mine)
+    (following,) = call(
+        functools.partial(last_kernel, bits),
+        [row_shape],
+        [VMEM] * 7,
+        [values[-1], z, own, lines, held, pick, back],
         scratch=parts_scratch,
         name="last_apply",
     )
     values.append(following)
-    exchanged = lax.all_to_all(dots, ("sub", "coarse"), 0, 0)
     answer, left_over = call(
         functools.partial(finish_kernel, ITERS),
         [right_side.shape] * 2,
-        [VMEM] * (2 * ITERS + 2),
-        [exchanged, *values, *fields],
+        [VMEM] * (2 * ITERS + 3),
+        [mine, theirs, *values, *fields],
         name="finish",
     )
     return answer, left_over

time: 54.8 us -> 53.4 us (0.974)
  starting transfers between devices: 25.9 us -> 19 us
  blocking collectives: 8.88 us -> 15.6 us
  waiting for transfers between devices: 7.83 us -> 6.03 us
  Pallas kernels: 10 us -> 10.6 us
    ppermute x16 -> x12, starting transfers between devices: 25.7 us -> 18.8 us  [partner(): lax.ppermute(array, axis, [(i, i ^ 1 << bit) for i in range(lax.axis_size...]
    all_to_all x1, blocking collectives: 8.88 us -> 15.6 us  [on_device(): lines = lax.all_to_all(payload, 'sub', 0, 0)]
    ppermute x16 -> x12, waiting for transfers between devices: 6.2 us -> 3.98 us  [partner(): lax.ppermute(array, axis, [(i, i ^ 1 << bit) for i in range(lax.axis_size...]
    pallas_call x15 -> x17, Pallas kernels: 10 us -> 10.6 us  [call(): pl.pallas_call(kernel, out_shape=[jax.ShapeDtypeStruct(*(out if isinstanc...]
    ppermute x3 -> x4, waiting for transfers between devices: 1.63 us -> 2.04 us  [swap(): return lax.ppermute(array, 'coarse', flip)]
  transfers between devices with their start and end apart: 19 -> 16, of which waited for: 10 -> 8; matrix products, arithmetic and copies ran while one was open for 0% -> 0% of each run, Pallas kernels for 8% -> 9%
where the time goes in v4:
time: 53.4 us; the launch traced here: 53.2 us
  starting transfers between devices  19 us (36%)
  blocking collectives  15.6 us (29%)
  Pallas kernels  10.6 us (20%)
  waiting for transfers between devices  6.03 us (11%)
  local copies, waits for them, and re-layouts  1.16 us (2%)
  between operations  0.84 us (2%)
    ppermute x12, starting transfers between devices, partner(): lax.ppermute(array, axis, [(i, i ^ 1 << bit) for i in range(lax.axis_size...  18.8 us
    all_to_all x1, blocking collectives, on_device(): lines = lax.all_to_all(payload, 'sub', 0, 0)  15.6 us
    pallas_call x17, Pallas kernels, call(): pl.pallas_call(kernel, out_shape=[jax.ShapeDtypeStruct(*(out if isinstanc...  10.6 us
    ppermute x12, waiting for transfers between devices, partner(): lax.ppermute(array, axis, [(i, i ^ 1 << bit) for i in range(lax.axis_size...  3.98 us
    ppermute x4, waiting for transfers between devices, swap(): return lax.ppermute(array, 'coarse', flip)  2.04 us
    unnamed x18, local copies, waits for them, and re-layouts  1.16 us
  transfers between devices with their start and end apart: 16, of which 8 were waited for; matrix products, arithmetic and copies ran while one was open for 0% of the time, Pallas kernels for 9%

profile of v4, /device:TPU:0, one launch (start us, length us, event | category | flops | bytes accessed | tf_op | source)
XLA Modules:
  0.0 53.2 jit_solution(2007699109395041486)
XLA Ops:
  0.6 1.1 %copy-done = f32[1,16,96,96]{3,2,1,0:T(8,128)S(1)} copy-done((f32[1,16,96,96]{3,2,1,0:T(8,128)S(1)}, f32[1,16,96,96]{3,2,1,0:T(8,128)}, u32[]{:S(2)}) %copy-start) | copy-done | bytes 589848
  1.8 0.2 pack_margin.1
  2.0 4.1 %collective-permute-start = (f32[4,72,128]{2,1,0:T(8,128)S(1)}, f32[4,72,128]{2,1,0:T(8,128)S(1)}, u32[]{:S(2)}, u32[]{:S(2)}) collective-permute-start(f32[4,72,128]{2,1,0:T(8,128)S(1)} %get-tuple-element.43), channel_id=1, source_target_pairs={{0,16},{2,18},{4,20},{6,22},{8,24},{10,26},{12,28},{14,30},{16,0},... | collective-permute-start | bytes 442376 | tf_op jit(solution)/shard_map/ppermute | solution.py:22
  6.1 1.6 %collective-permute-start.1 = (f32[4,72,128]{2,1,0:T(8,128)S(1)}, f32[4,72,128]{2,1,0:T(8,128)S(1)}, u32[]{:S(2)}, u32[]{:S(2)}) collective-permute-start(f32[4,72,128]{2,1,0:T(8,128)S(1)} %get-tuple-element.44), channel_id=1, source_target_pairs={{0,8},{2,10},{4,12},{6,14},{8,0},{10,2},{12,4},{14,6},{16,24},{18,... | collective-permute-start | bytes 442376 | tf_op jit(solution)/shard_map/ppermute | solution.py:22
  7.7 1.5 %collective-permute-start.2 = (f32[4,72,128]{2,1,0:T(8,128)S(1)}, f32[4,72,128]{2,1,0:T(8,128)S(1)}, u32[]{:S(2)}, u32[]{:S(2)}) collective-permute-start(f32[4,72,128]{2,1,0:T(8,128)S(1)} %get-tuple-element.45), channel_id=1, source_target_pairs={{0,4},{2,6},{4,0},{6,2},{8,12},{10,14},{12,8},{14,10},{16,20},{18,... | collective-permute-start | bytes 442376 | tf_op jit(solution)/shard_map/ppermute | solution.py:22
  9.2 1.5 %collective-permute-start.3 = (f32[4,72,128]{2,1,0:T(8,128)S(1)}, f32[4,72,128]{2,1,0:T(8,128)S(1)}, u32[]{:S(2)}, u32[]{:S(2)}) collective-permute-start(f32[4,72,128]{2,1,0:T(8,128)S(1)} %get-tuple-element.46), channel_id=1, source_target_pairs={{0,2},{2,0},{4,6},{6,4},{8,10},{10,8},{12,14},{14,12},{16,18},{18,... | collective-permute-start | bytes 442376 | tf_op jit(solution)/shard_map/ppermute | solution.py:22
  10.7 0.6 %restrict.1 = (s32[16,128]{1,0:T(8,128)S(1)}, f32[1,128]{1,0:T(1,128)S(1)}) custom-call(f32[1,16,96]{2,1,0:T(8,128)S(1)} %copy-done.4, f32[1,6,16,96]{3,2,1,0:T(8,128)S(1)} %bitcast.2, s32[1,16]{1,0:T(1,128)S(1)} %copy-done.8), custom_call_target="tpu_custom_call" | custom-call | bytes 100000 | tf_op jit(solution)/shard_map/restrict/pallas_call | solution.py:26
  11.4 0.1 collective-permute-start.4
  11.5 1.2 %local_inverse.3 = (f32[16,96,128]{2,1,0:T(8,128)}, f32[16,96]{1,0:T(8,128)S(1)}) custom-call(f32[1,16,96]{2,1,0:T(8,128)S(1)} %copy-done.4, f32[1,16,96,96]{3,2,1,0:T(8,128)S(1)} %copy-done.2), custom_call_target="tpu_custom_call" | custom-call | bytes 100000 | tf_op jit(solution)/shard_map/local_inverse/pallas_call | solution.py:26
  12.6 0.8 %tables.1 = (bf16[96,96]{1,0:T(8,128)(2,1)S(1)}, bf16[16,48]{1,0:T(8,128)(2,1)S(1)}, bf16[16,48]{1,0:T(8,128)(2,1)S(1)}, s32[2,128]{1,0:T(2,128)S(1)}) custom-call(s32[6,1,16]{2,1,0:T(1,128)S(1)} %bitcast.8, s32[1,4,4]{2,1,0:T(4,128)S(1)} %copy-done.6), custom_call_target="tpu_custom_call" | custom-call | bytes 100000 | tf_op jit(solution)/shard_map/tables/pallas_call | solution.py:26
  13.4 0.0 collective-permute-done.4.theirs_ref
  13.4 0.2 first_base.1
  13.6 0.0 collective-permute-done.1.refs_1_.refs_2_
  13.6 0.0 collective-permute-done.2.refs_2_.refs_1_
  13.7 0.7 %collective-permute-done.3.refs_3_.refs_0_ = f32[4,72,128]{2,1,0:T(8,128)S(1)} collective-permute-done((f32[4,72,128]{2,1,0:T(8,128)S(1)}, f32[4,72,128]{2,1,0:T(8,128)S(1)}, u32[]{:S(2)}, u32[]{:S(2)}) %collective-permute-start.3) | collective-permute-done | bytes 147488 | tf_op jit(solution)/shard_map/ppermute | solution.py:22
  14.4 1.0 %first_spread.1 = (f32[16,96]{1,0:T(8,128)S(1)}, f32[16,96]{1,0:T(8,128)S(1)}, f32[8,96]{1,0:T(8,128)S(1)}, f32[8,96]{1,0:T(8,128)S(1)}, f32[8,96]{1,0:T(8,128)S(1)}, /*index=5*/f32[8,96]{1,0:T(8,128)S(1)}) custom-call(f32[4,72,128]{2,1,0:T(8,128)S(1)} %collective-permute-done.refs_0_.refs_3_, f32[4,72,128]{2,1,0:T(8,128)S(1)} %collective-permute-done.1.refs_1_.refs_2_, ...), custom_call_target="tpu_custom_call" | custom-call | bytes 100000 | tf_op jit(solution)/shard_map/first_spread/pallas_call | solution.py:26
  15.4 0.5 collective-permute-start.5
  15.9 2.4 %collective-permute-start.6 = (f32[8,96]{1,0:T(8,128)S(1)}, f32[8,96]{1,0:T(8,128)S(1)}, u32[]{:S(2)}, u32[]{:S(2)}) collective-permute-start(f32[8,96]{1,0:T(8,128)S(1)} %get-tuple-element.58), channel_id=1, source_target_pairs={{0,8},{2,10},{4,12},{6,14},{8,0},{10,2},{12,4},{14,6},{16,24},{18,... | collective-permute-start | bytes 9224 | tf_op jit(solution)/shard_map/ppermute | solution.py:22
  18.4 1.5 %collective-permute-start.7 = (f32[8,96]{1,0:T(8,128)S(1)}, f32[8,96]{1,0:T(8,128)S(1)}, u32[]{:S(2)}, u32[]{:S(2)}) collective-permute-start(f32[8,96]{1,0:T(8,128)S(1)} %get-tuple-element.59), channel_id=1, source_target_pairs={{0,4},{2,6},{4,0},{6,2},{8,12},{10,14},{12,8},{14,10},{16,20},{18,... | collective-permute-start | bytes 9224 | tf_op jit(solution)/shard_map/ppermute | solution.py:22
  19.9 1.5 %collective-permute-start.8 = (f32[8,96]{1,0:T(8,128)S(1)}, f32[8,96]{1,0:T(8,128)S(1)}, u32[]{:S(2)}, u32[]{:S(2)}) collective-permute-start(f32[8,96]{1,0:T(8,128)S(1)} %get-tuple-element.60), channel_id=1, source_target_pairs={{0,2},{2,0},{4,6},{6,4},{8,10},{10,8},{12,14},{14,12},{16,18},{18,... | collective-permute-start | bytes 9224 | tf_op jit(solution)/shard_map/ppermute | solution.py:22
  21.4 1.0 %combine.1.inverse_ref = f32[16,96,96]{2,1,0:T(8,128)S(1)} custom-call(f32[1,16,96,96]{3,2,1,0:T(8,128)S(1)} %copy-done.2, s32[1,4,4]{2,1,0:T(4,128)S(1)} %copy-done.6, f32[4,72,128]{2,1,0:T(8,128)S(1)} %collective-permute-done.3.refs_3_.refs_0_, f32[4,72,128]{2,1,0:T(8,128)S(1)} %collective-permute-done.2.refs_2_.refs_1_, ...), custom_call_target="tpu_custom_call" | custom-call | bytes 100000 | tf_op jit(solution)/shard_map/combine/pallas_call | solution.py:26
  22.3 0.0 collective-permute-done.5.refs_0_
  22.3 0.0 collective-permute-done.6.refs_1_
  22.4 1.1 %collective-permute-done.8.refs_3_ = f32[8,96]{1,0:T(8,128)S(1)} collective-permute-done((f32[8,96]{1,0:T(8,128)S(1)}, f32[8,96]{1,0:T(8,128)S(1)}, u32[]{:S(2)}, u32[]{:S(2)}) %collective-permute-start.8) | collective-permute-done | bytes 3104 | tf_op jit(solution)/shard_map/ppermute | solution.py:22
  23.5 0.7 %apply.2 = (f32[16,96]{1,0:T(8,128)S(1)}, f32[1,128]{1,0:T(1,128)S(1)}) custom-call(f32[1,16,96]{2,1,0:T(8,128)S(1)} %copy-done.4, f32[16,96]{1,0:T(8,128)S(1)} %get-tuple-element.55.z_ref.refs_3_.refs_4_, f32[16,96]{1,0:T(8,128)S(1)} %get-tuple-element.56.own_ref, f32[8,96]{1,0:T(8,128)S(1)} %collective-permute-done.5.refs_0_, ...), custom_call_target="tpu_custom_call" | custom-call | bytes 100000 | tf_op jit(solution)/shard_map/apply/pallas_call | solution.py:26
  24.2 0.1 collective-permute-start.9
  24.3 0.3 local_inverse.4
  24.5 0.8 %collective-permute-done.9.refs_3_ = f32[1,128]{1,0:T(1,128)S(1)} collective-permute-done((f32[1,128]{1,0:T(1,128)S(1)}, f32[1,128]{1,0:T(1,128)S(1)}, u32[]{:S(2)}, u32[]{:S(2)}) %collective-permute-start.9) | collective-permute-done | bytes 544 | tf_op jit(solution)/shard_map/ppermute | solution.py:561
  25.4 0.8 %spread.1 = (f32[16,96]{1,0:T(8,128)S(1)}, f32[16,96]{1,0:T(8,128)S(1)}, f32[8,96]{1,0:T(8,128)S(1)}, f32[8,96]{1,0:T(8,128)S(1)}, f32[8,96]{1,0:T(8,128)S(1)}, /*index=5*/f32[8,96]{1,0:T(8,128)S(1)}) custom-call(f32[16,96,128]{2,1,0:T(8,128)S(1)} %get-tuple-element.68.refs_0_, f32[16,96]{1,0:T(8,128)S(1)} %get-tuple-element.69.refs_1_, ...), custom_call_target="tpu_custom_call" | custom-call | bytes 100000 | tf_op jit(solution)/shard_map/spread/pallas_call | solution.py:26
  26.1 0.7 %collective-permute-start.10 = (f32[8,96]{1,0:T(8,128)S(1)}, f32[8,96]{1,0:T(8,128)S(1)}, u32[]{:S(2)}, u32[]{:S(2)}) collective-permute-start(f32[8,96]{1,0:T(8,128)S(1)} %get-tuple-element.73), channel_id=1, source_target_pairs={{0,16},{2,18},{4,20},{6,22},{8,24},{10,26},{12,28},{14,30},{16,0},... | collective-permute-start | bytes 9224 | tf_op jit(solution)/shard_map/ppermute | solution.py:22
  26.8 0.6 %collective-permute-start.11 = (f32[8,96]{1,0:T(8,128)S(1)}, f32[8,96]{1,0:T(8,128)S(1)}, u32[]{:S(2)}, u32[]{:S(2)}) collective-permute-start(f32[8,96]{1,0:T(8,128)S(1)} %get-tuple-element.74), channel_id=1, source_target_pairs={{0,8},{2,10},{4,12},{6,14},{8,0},{10,2},{12,4},{14,6},{16,24},{18,... | collective-permute-start | bytes 9224 | tf_op jit(solution)/shard_map/ppermute | solution.py:22
  27.4 1.4 %collective-permute-start.12 = (f32[8,96]{1,0:T(8,128)S(1)}, f32[8,96]{1,0:T(8,128)S(1)}, u32[]{:S(2)}, u32[]{:S(2)}) collective-permute-start(f32[8,96]{1,0:T(8,128)S(1)} %get-tuple-element.75), channel_id=1, source_target_pairs={{0,4},{2,6},{4,0},{6,2},{8,12},{10,14},{12,8},{14,10},{16,20},{18,... | collective-permute-start | bytes 9224 | tf_op jit(solution)/shard_map/ppermute | solution.py:22
  28.8 1.5 %collective-permute-start.13 = (f32[8,96]{1,0:T(8,128)S(1)}, f32[8,96]{1,0:T(8,128)S(1)}, u32[]{:S(2)}, u32[]{:S(2)}) collective-permute-start(f32[8,96]{1,0:T(8,128)S(1)} %get-tuple-element.76), channel_id=1, source_target_pairs={{0,2},{2,0},{4,6},{6,4},{8,10},{10,8},{12,14},{14,12},{16,18},{18,... | collective-permute-start | bytes 9224 | tf_op jit(solution)/shard_map/ppermute | solution.py:22
  30.3 0.4 collective-permute-done.10.refs_0_
  30.7 0.3 collective-permute-done.12.refs_2_
  31.0 1.4 %collective-permute-done.13.refs_3_ = f32[8,96]{1,0:T(8,128)S(1)} collective-permute-done((f32[8,96]{1,0:T(8,128)S(1)}, f32[8,96]{1,0:T(8,128)S(1)}, u32[]{:S(2)}, u32[]{:S(2)}) %collective-permute-start.13) | collective-permute-done | bytes 3104 | tf_op jit(solution)/shard_map/ppermute | solution.py:22
  32.4 0.7 %apply.3 = (f32[16,96]{1,0:T(8,128)S(1)}, f32[1,128]{1,0:T(1,128)S(1)}) custom-call(f32[16,96]{1,0:T(8,128)S(1)} %get-tuple-element.66.field_ref.refs_1_.refs_11_, f32[16,96]{1,0:T(8,128)S(1)} %get-tuple-element.71.z_ref.refs_4_.refs_5_, f32[16,96]{1,0:T(8,128)S(1)} %get-tuple-element.72.own_ref, f32[8,96]{1,0:T(8,128)S(1)} %collective-permute-done.10.refs_0_, ...), custom_call_target="tpu_custom_call" | custom-call | bytes 100000 | tf_op jit(solution)/shard_map/apply/pallas_call | solution.py:26
  33.1 0.1 collective-permute-start.14
  33.1 0.1 early_dots.1.refs_9_
  33.2 0.3 local_inverse.5
  33.5 0.7 %collective-permute-done.14.refs_3_ = f32[1,128]{1,0:T(1,128)S(1)} collective-permute-done((f32[1,128]{1,0:T(1,128)S(1)}, f32[1,128]{1,0:T(1,128)S(1)}, u32[]{:S(2)}, u32[]{:S(2)}) %collective-permute-start.14) | collective-permute-done | bytes 544 | tf_op jit(solution)/shard_map/ppermute | solution.py:561
  34.3 1.3 %last_spread.1 = (f32[16,96]{1,0:T(8,128)S(1)}, f32[16,96]{1,0:T(8,128)S(1)}, f32[16,32,128]{2,1,0:T(8,128)S(1)}) custom-call(f32[16,96,128]{2,1,0:T(8,128)S(1)} %get-tuple-element.78.refs_0_, f32[16,96]{1,0:T(8,128)S(1)} %get-tuple-element.79.refs_1_, f32[1,128]{1,0:T(1,128)S(1)} %get-tuple-element.80.refs_2_, ...), custom_call_target="tpu_custom_call" | custom-call | bytes 100000 | tf_op jit(solution)/shard_map/last_spread/pallas_call | solution.py:26
  35.5 15.6 %all_to_all.5.lines_ref = f32[16,32,128]{2,1,0:T(8,128)S(1)} all-to-all(f32[16,32,128]{2,1,0:T(8,128)S(1)} %get-tuple-element.81), channel_id=1, replica_groups=mesh['sub'=16,'coarse'=2] {'sub'}, dimensions={0} | all-to-all | bytes 524288 | tf_op jit(solution)/shard_map/all_to_all | solution.py:675
  51.2 0.2 totals.1.mine_ref
  51.3 0.0 collective-permute-start.15
  51.3 0.6 %last_apply.1.refs_3_ = f32[16,96]{1,0:T(8,128)S(1)} custom-call(f32[16,96]{1,0:T(8,128)S(1)} %get-tuple-element.77.field_ref.refs_2_.refs_12_, f32[16,96]{1,0:T(8,128)S(1)} %get-tuple-element.82.z_ref.refs_6_, f32[16,96]{1,0:T(8,128)S(1)} %get-tuple-element.83.own_ref, f32[16,32,128]{2,1,0:T(8,128)S(1)} %all_to_all.5.lines_ref, ...), custom_call_target="tpu_custom_call" | custom-call | bytes 100000 | tf_op jit(solution)/shard_map/last_apply/pallas_call | solution.py:26
  52.0 0.5 collective-permute-done.15.theirs_ref
  52.5 0.8 %finish.1 = (f32[1,16,96]{2,1,0:T(8,128)}, f32[1,16,96]{2,1,0:T(8,128)}) custom-call(f32[1,128]{1,0:T(1,128)S(1)} %totals.1.mine_ref, f32[1,128]{1,0:T(1,128)S(1)} %collective-permute-done.15.theirs_ref, f32[1,16,96]{2,1,0:T(8,128)S(1)} %copy-done.4, f32[16,96]{1,0:T(8,128)S(1)} %get-tuple-element.66.field_ref.refs_1_.refs_11_, ...), custom_call_target="tpu_custom_call" | custom-call | bytes 100000 | tf_op jit(solution)/shard_map/finish/pallas_call | solution.py:26
  (20 shorter events, 0.0 us)
Async XLA Ops:
  0.6 1.1 %copy-start = (f32[1,16,96,96]{3,2,1,0:T(8,128)S(1)}, f32[1,16,96,96]{3,2,1,0:T(8,128)}, u32[]{:S(2)}) copy-start(f32[1,16,96,96]{3,2,1,0:T(8,128)} %refs_15_.1) | copy-start | bytes 1769476
  1.8 9.0 %copy-start.3 = (f32[1,16,6,96]{3,1,2,0:T(8,128)S(1)}, f32[1,16,6,96]{3,1,2,0:T(8,128)}, u32[]{:S(2)}) copy-start(f32[1,16,6,96]{3,1,2,0:T(8,128)} %param.15) | copy-start | bytes 110596
  1.8 9.0 %copy-start.4 = (f32[1,16,96]{2,1,0:T(8,128)S(1)}, f32[1,16,96]{2,1,0:T(8,128)}, u32[]{:S(2)}) copy-start(f32[1,16,96]{2,1,0:T(8,128)} %refs_0_.5) | copy-start | bytes 18436
  1.8 9.0 %copy-start.8 = (s32[1,16]{1,0:T(1,128)S(1)}, s32[1,16]{1,0:T(1,128)}, u32[]{:S(2)}) copy-start(s32[1,16]{1,0:T(1,128)} %aggregate_ref.1) | copy-start | bytes 196
  1.8 9.7 %copy-start.2 = (f32[1,16,96,96]{3,2,1,0:T(8,128)S(1)}, f32[1,16,96,96]{3,2,1,0:T(8,128)}, u32[]{:S(2)}) copy-start(f32[1,16,96,96]{3,2,1,0:T(8,128)} %inverse_ref.3) | copy-start | bytes 1769476
  1.8 10.9 %copy-start.6 = (s32[1,4,4]{2,1,0:T(4,128)S(1)}, s32[1,4,4]{2,1,0:T(4,128)}, u32[]{:S(2)}) copy-start(s32[1,4,4]{2,1,0:T(4,128)} %senders_ref.3) | copy-start | bytes 196
  1.8 10.9 %copy-start.7 = (s32[1,16,6]{1,0,2:T(1,128)S(1)}, s32[1,16,6]{1,0,2:T(1,128)}, u32[]{:S(2)}) copy-start(s32[1,16,6]{1,0,2:T(1,128)} %param.11) | copy-start | bytes 1156
  1.8 11.6 %copy-start.5 = (f32[1,48,48]{2,1,0:T(8,128)S(1)}, f32[1,48,48]{2,1,0:T(8,128)}, u32[]{:S(2)}) copy-start(f32[1,48,48]{2,1,0:T(8,128)} %refs_4_.9) | copy-start | bytes 27652
  1.8 12.6 %copy-start.1 = (f32[1,16,6,96,96]{4,3,2,1,0:T(8,128)S(1)}, f32[1,16,6,96,96]{4,3,2,1,0:T(8,128)}, u32[]{:S(2)}) copy-start(f32[1,16,6,96,96]{4,3,2,1,0:T(8,128)} %blocks_ref.1) | copy-start | bytes 10616836
  2.0 11.6 %collective-permute-start = (f32[4,72,128]{2,1,0:T(8,128)S(1)}, f32[4,72,128]{2,1,0:T(8,128)S(1)}, u32[]{:S(2)}, u32[]{:S(2)}) collective-permute-start(f32[4,72,128]{2,1,0:T(8,128)S(1)} %get-tuple-element.43), channel_id=1, source_target_pairs={{0,16},{2,18},{4,20},{6,22},{8,24},{10,26},{12,28},{14,30},{16,0},... | collective-permute-start | bytes 442376 | tf_op jit(solution)/shard_map/ppermute | solution.py:22
  6.1 7.5 %collective-permute-start.1 = (f32[4,72,128]{2,1,0:T(8,128)S(1)}, f32[4,72,128]{2,1,0:T(8,128)S(1)}, u32[]{:S(2)}, u32[]{:S(2)}) collective-permute-start(f32[4,72,128]{2,1,0:T(8,128)S(1)} %get-tuple-element.44), channel_id=1, source_target_pairs={{0,8},{2,10},{4,12},{6,14},{8,0},{10,2},{12,4},{14,6},{16,24},{18,... | collective-permute-start | bytes 442376 | tf_op jit(solution)/shard_map/ppermute | solution.py:22
  7.7 5.9 %collective-permute-start.2 = (f32[4,72,128]{2,1,0:T(8,128)S(1)}, f32[4,72,128]{2,1,0:T(8,128)S(1)}, u32[]{:S(2)}, u32[]{:S(2)}) collective-permute-start(f32[4,72,128]{2,1,0:T(8,128)S(1)} %get-tuple-element.45), channel_id=1, source_target_pairs={{0,4},{2,6},{4,0},{6,2},{8,12},{10,14},{12,8},{14,10},{16,20},{18,... | collective-permute-start | bytes 442376 | tf_op jit(solution)/shard_map/ppermute | solution.py:22
  9.2 5.1 %collective-permute-start.3 = (f32[4,72,128]{2,1,0:T(8,128)S(1)}, f32[4,72,128]{2,1,0:T(8,128)S(1)}, u32[]{:S(2)}, u32[]{:S(2)}) collective-permute-start(f32[4,72,128]{2,1,0:T(8,128)S(1)} %get-tuple-element.46), channel_id=1, source_target_pairs={{0,2},{2,0},{4,6},{6,4},{8,10},{10,8},{12,14},{14,12},{16,18},{18,... | collective-permute-start | bytes 442376 | tf_op jit(solution)/shard_map/ppermute | solution.py:22
  11.4 2.0 %collective-permute-start.4 = (f32[1,128]{1,0:T(1,128)S(1)}, f32[1,128]{1,0:T(1,128)S(1)}, u32[]{:S(2)}, u32[]{:S(2)}) collective-permute-start(f32[1,128]{1,0:T(1,128)S(1)} %get-tuple-element.49.mine_ref), channel_id=1, source_target_pairs={{0,1},{1,0},{2,3},{3,2},{4,5},{5,4},{6,7},{7,6},{8,9},{9,8},{10,11... | collective-permute-start | bytes 1544 | tf_op jit(solution)/shard_map/ppermute | solution.py:561
  15.4 6.9 %collective-permute-start.5 = (f32[8,96]{1,0:T(8,128)S(1)}, f32[8,96]{1,0:T(8,128)S(1)}, u32[]{:S(2)}, u32[]{:S(2)}) collective-permute-start(f32[8,96]{1,0:T(8,128)S(1)} %get-tuple-element.57), channel_id=1, source_target_pairs={{0,16},{2,18},{4,20},{6,22},{8,24},{10,26},{12,28},{14,30},{16,0},... | collective-permute-start | bytes 9224 | tf_op jit(solution)/shard_map/ppermute | solution.py:22
  15.9 6.4 %collective-permute-start.6 = (f32[8,96]{1,0:T(8,128)S(1)}, f32[8,96]{1,0:T(8,128)S(1)}, u32[]{:S(2)}, u32[]{:S(2)}) collective-permute-start(f32[8,96]{1,0:T(8,128)S(1)} %get-tuple-element.58), channel_id=1, source_target_pairs={{0,8},{2,10},{4,12},{6,14},{8,0},{10,2},{12,4},{14,6},{16,24},{18,... | collective-permute-start | bytes 9224 | tf_op jit(solution)/shard_map/ppermute | solution.py:22
  18.4 4.0 %collective-permute-start.7 = (f32[8,96]{1,0:T(8,128)S(1)}, f32[8,96]{1,0:T(8,128)S(1)}, u32[]{:S(2)}, u32[]{:S(2)}) collective-permute-start(f32[8,96]{1,0:T(8,128)S(1)} %get-tuple-element.59), channel_id=1, source_target_pairs={{0,4},{2,6},{4,0},{6,2},{8,12},{10,14},{12,8},{14,10},{16,20},{18,... | collective-permute-start | bytes 9224 | tf_op jit(solution)/shard_map/ppermute | solution.py:22
  19.9 3.6 %collective-permute-start.8 = (f32[8,96]{1,0:T(8,128)S(1)}, f32[8,96]{1,0:T(8,128)S(1)}, u32[]{:S(2)}, u32[]{:S(2)}) collective-permute-start(f32[8,96]{1,0:T(8,128)S(1)} %get-tuple-element.60), channel_id=1, source_target_pairs={{0,2},{2,0},{4,6},{6,4},{8,10},{10,8},{12,14},{14,12},{16,18},{18,... | collective-permute-start | bytes 9224 | tf_op jit(solution)/shard_map/ppermute | solution.py:22
  24.2 1.2 %collective-permute-start.9 = (f32[1,128]{1,0:T(1,128)S(1)}, f32[1,128]{1,0:T(1,128)S(1)}, u32[]{:S(2)}, u32[]{:S(2)}) collective-permute-start(f32[1,128]{1,0:T(1,128)S(1)} %get-tuple-element.70.refs_2_), channel_id=1, source_target_pairs={{0,1},{1,0},{2,3},{3,2},{4,5},{5,4},{6,7},{7,6},{8,9},{9,8},{10,11... | collective-permute-start | bytes 1544 | tf_op jit(solution)/shard_map/ppermute | solution.py:561
  26.1 4.6 %collective-permute-start.10 = (f32[8,96]{1,0:T(8,128)S(1)}, f32[8,96]{1,0:T(8,128)S(1)}, u32[]{:S(2)}, u32[]{:S(2)}) collective-permute-start(f32[8,96]{1,0:T(8,128)S(1)} %get-tuple-element.73), channel_id=1, source_target_pairs={{0,16},{2,18},{4,20},{6,22},{8,24},{10,26},{12,28},{14,30},{16,0},... | collective-permute-start | bytes 9224 | tf_op jit(solution)/shard_map/ppermute | solution.py:22
  26.8 3.9 %collective-permute-start.11 = (f32[8,96]{1,0:T(8,128)S(1)}, f32[8,96]{1,0:T(8,128)S(1)}, u32[]{:S(2)}, u32[]{:S(2)}) collective-permute-start(f32[8,96]{1,0:T(8,128)S(1)} %get-tuple-element.74), channel_id=1, source_target_pairs={{0,8},{2,10},{4,12},{6,14},{8,0},{10,2},{12,4},{14,6},{16,24},{18,... | collective-permute-start | bytes 9224 | tf_op jit(solution)/shard_map/ppermute | solution.py:22
  27.4 3.6 %collective-permute-start.12 = (f32[8,96]{1,0:T(8,128)S(1)}, f32[8,96]{1,0:T(8,128)S(1)}, u32[]{:S(2)}, u32[]{:S(2)}) collective-permute-start(f32[8,96]{1,0:T(8,128)S(1)} %get-tuple-element.75), channel_id=1, source_target_pairs={{0,4},{2,6},{4,0},{6,2},{8,12},{10,14},{12,8},{14,10},{16,20},{18,... | collective-permute-start | bytes 9224 | tf_op jit(solution)/shard_map/ppermute | solution.py:22
  28.8 3.6 %collective-permute-start.13 = (f32[8,96]{1,0:T(8,128)S(1)}, f32[8,96]{1,0:T(8,128)S(1)}, u32[]{:S(2)}, u32[]{:S(2)}) collective-permute-start(f32[8,96]{1,0:T(8,128)S(1)} %get-tuple-element.76), channel_id=1, source_target_pairs={{0,2},{2,0},{4,6},{6,4},{8,10},{10,8},{12,14},{14,12},{16,18},{18,... | collective-permute-start | bytes 9224 | tf_op jit(solution)/shard_map/ppermute | solution.py:22
  33.1 1.2 %collective-permute-start.14 = (f32[1,128]{1,0:T(1,128)S(1)}, f32[1,128]{1,0:T(1,128)S(1)}, u32[]{:S(2)}, u32[]{:S(2)}) collective-permute-start(f32[1,128]{1,0:T(1,128)S(1)} %get-tuple-element.80.refs_2_), channel_id=1, source_target_pairs={{0,1},{1,0},{2,3},{3,2},{4,5},{5,4},{6,7},{7,6},{8,9},{9,8},{10,11... | collective-permute-start | bytes 1544 | tf_op jit(solution)/shard_map/ppermute | solution.py:561
  51.3 1.1 %collective-permute-start.15 = (f32[1,128]{1,0:T(1,128)S(1)}, f32[1,128]{1,0:T(1,128)S(1)}, u32[]{:S(2)}, u32[]{:S(2)}) collective-permute-start(f32[1,128]{1,0:T(1,128)S(1)} %totals.1.mine_ref), channel_id=1, source_target_pairs={{0,1},{1,0},{2,3},{3,2},{4,5},{5,4},{6,7},{7,6},{8,9},{9,8},{10,11... | collective-permute-start | bytes 1544 | tf_op jit(solution)/shard_map/ppermute | solution.py:561

commit v5 on v4

--- a/solution.py
+++ b/solution.py
@@ -10,6 +10,8 @@
 ITERS = 3
 SHIFT = 2.0
 REPEATS = 16
+LIMIT = 200.0
+LARGE = 1e30
 
 f32 = jnp.float32
 bf16 = jnp.bfloat16
@@ -144,10 +146,32 @@
     back_ref[...] = triple(send_table.T[:rows])
 
 
+def load_kernel(source_ref, out_ref, *sems):
+    quarter = source_ref.shape[1] // len(sems)
+    copies = [
+        pltpu.make_async_copy(
+            source_ref.at[:, pl.ds(at * quarter, quarter)],
+            out_ref.at[:, pl.ds(at * quarter, quarter)],
+            sem,
+        )
+        for at, sem in enumerate(sems)
+    ]
+    for copy in copies:
+        copy.start()
+    for copy in copies:
+        copy.wait()
+
+
+def local_row_kernel(field_ref, inverse_ref, row_ref):
+    rows, width = row_ref.shape
+    eye = eye_mask(width)
+    for i in range(rows):
+        column = jnp.sum(inverse_ref[0, i] * field_ref[0, i : i + 1, :], axis=1, keepdims=True)
+        row_ref[i : i + 1, :] = to_row(column, eye)
+
+
 def local_kernel(field_ref, inverse_ref, column_ref, row_ref):
     rows, width = row_ref.shape
-    field_ref = field_ref.reshape(rows, width)
-    inverse_ref = inverse_ref.reshape(rows, width, width)
     eye = eye_mask(width)
     for i in range(rows):
         column = jnp.sum(inverse_ref[i] * field_ref[i : i + 1, :], axis=1, keepdims=True)
@@ -459,14 +483,8 @@
     next_ref[...] = image - SHIFT * field_ref[...]
 
 
-def finish_kernel(fields, mine_ref, theirs_ref, *refs):
-    value_refs = refs[: fields + 1]
-    z_refs = refs[fields + 1 : 2 * fields + 1]
-    solution_ref, residual_ref = refs[2 * fields + 1 :]
-    total = mine_ref[...] + theirs_ref[...]
+def coefficients(total, fields, width):
     lane = lax.broadcasted_iota(jnp.int32, (1, 128), 1)
-    shape = solution_ref.shape[1:]
-    width = shape[1]
 
     def product(at):
         return jnp.sum(jnp.where(lane == width + at, total, 0.0), axis=1, keepdims=True)
@@ -476,17 +494,21 @@
     final = [gram[c + 1][last] + SHIFT * gram[c][last] for c in range(last)]
     final.append(product(fields * fields))
     gram.append([final[c] - SHIFT * gram[last][c] for c in range(fields)])
-    zero = jnp.zeros((1, 1), f32)
     one = jnp.ones((1, 1), f32)
+    checks = []
 
     def form(left, right):
-        value = zero
+        value = jnp.zeros((1, 1), f32)
+        size = jnp.zeros((1, 1), f32)
         for a, left_at in enumerate(left):
             if left_at is None:
                 continue
             for c, right_at in enumerate(right):
                 if right_at is not None:
-                    value = value + left_at * right_at * gram[a][c]
+                    term = left_at * right_at * gram[a][c]
+                    value = value + term
+                    size = size + jnp.abs(term)
+        checks.append((size <= LIMIT * jnp.abs(value)) & (size < LARGE) & (size > 1.0 / LARGE))
         return value
 
     def plus(first, second):
@@ -515,6 +537,23 @@
             beta = product_next / product_now
             direction = [plus(residual[c], scaled(beta, direction[c])) for c in range(fields)]
             product_now = product_next
+    sound = checks[0]
+    for check in checks[1:]:
+        sound = sound & check
+    return iterate, residual, sound
+
+
+def decide_kernel(fields, width, mine_ref, theirs_ref, out_ref):
+    _, _, sound = coefficients(mine_ref[...] + theirs_ref[...], fields, width)
+    out_ref[...] = jnp.broadcast_to(jnp.where(sound, 1.0, 0.0), out_ref.shape)
+
+
+def finish_kernel(fields, mine_ref, theirs_ref, *refs):
+    value_refs = refs[: fields + 1]
+    z_refs = refs[fields + 1 : 2 * fields + 1]
+    solution_ref, residual_ref = refs[2 * fields + 1 :]
+    shape = solution_ref.shape[1:]
+    iterate, residual, _ = coefficients(mine_ref[...] + theirs_ref[...], fields, shape[1])
     answer = iterate[0] * z_refs[0][...]
     for c in range(1, fields):
         answer = answer + iterate[c] * z_refs[c][...]
@@ -523,6 +562,76 @@
         left_over = left_over + residual[a] * value_refs[a][...]
     solution_ref[0] = answer
     residual_ref[0] = left_over
+
+
+def step_by_step(bits, source, matrix, columns, senders, inverse, null_modes, groups_of, coarse_inv):
+    highest = lax.Precision.HIGHEST
+    row_count, width = source.shape
+    turns, ghost_count = senders.shape
+    extent = row_count + turns * ghost_count
+    mode_count = null_modes.shape[1]
+    group_count = coarse_inv.shape[0] // mode_count
+
+    def table(size, index):
+        return (jnp.arange(size, dtype=jnp.int32)[:, None] == index[None, :]).astype(f32)
+
+    column_table = table(extent, columns.reshape(-1))
+    sender_table = table(row_count, senders.reshape(-1))
+    group_table = table(group_count, groups_of)
+
+    def precondition(residual):
+        local = jnp.einsum("rmb,rb->rm", null_modes, residual, precision=highest)
+        total = lax.psum(jnp.dot(group_table, local, precision=highest), "coarse")
+        solved = jnp.dot(coarse_inv, total.reshape(-1), precision=highest)
+        per_row = jnp.dot(
+            group_table.T, solved.reshape(group_count, mode_count), precision=highest
+        )
+        coarse = jnp.einsum("rmb,rm->rb", null_modes, per_row, precision=highest)
+        return jnp.einsum("rab,rb->ra", inverse, residual, precision=highest) + coarse
+
+    def operate(field):
+        transposed = jnp.einsum("rkab,ra->rkb", matrix, field, precision=highest)
+        spread = jnp.dot(column_table, transposed.reshape(-1, width), precision=highest)
+        sent = jnp.dot(sender_table.T, field, precision=highest)
+        rims = []
+        returned = []
+        for turn in range(turns):
+            start = turn * ghost_count
+            packet = jnp.concatenate(
+                [
+                    sent[start : start + ghost_count],
+                    spread[row_count + start : row_count + start + ghost_count],
+                ],
+                axis=0,
+            )
+            arrived = partner(packet, "sub", bits[turn])
+            rims.append(arrived[:ghost_count])
+            returned.append(arrived[ghost_count:])
+        extended = jnp.concatenate([field] + rims, axis=0)
+        picked = jnp.dot(column_table.T, extended, precision=highest)
+        picked = picked.reshape(row_count, -1, width)
+        forward = jnp.einsum("rkab,rkb->ra", matrix, picked, precision=highest)
+        back = jnp.dot(sender_table, jnp.concatenate(returned, axis=0), precision=highest)
+        return 0.5 * (forward + (spread[:row_count] + back))
+
+    def everywhere(first, second):
+        return lax.psum(jnp.sum(first * second), ("sub", "coarse"))
+
+    def body(step, state):
+        answer, residual, direction, product_now = state
+        precond = precondition(residual)
+        product_next = everywhere(residual, precond)
+        ratio = jnp.where(step == 0, 0.0, product_next / product_now)
+        direction = precond + ratio * direction
+        image = operate(direction)
+        alpha = product_next / everywhere(direction, image)
+        return (answer + alpha * direction, residual - alpha * image, direction, product_next)
+
+    zeros = jnp.zeros_like(source)
+    answer, residual, _, _ = lax.fori_loop(
+        0, ITERS, body, (zeros, source, zeros, jnp.ones((), f32))
+    )
+    return answer[None], residual[None]
 
 
 def on_device(
@@ -589,13 +698,22 @@
         scratch=[pltpu.VMEM((parts, 128), f32), pltpu.VMEM((ghost_total, 128), f32)],
         name="tables",
     )
-    source, null_modes, held, solver = right_side, null_view, blocks, coarse_inverse
-    _, row = call(
-        local_kernel,
-        [(rows, width, 128), row_shape],
+    source, null_modes, solver = right_side, null_view, coarse_inverse
+    (held,) = call(
+        load_kernel,
+        [blocks.shape],
+        [ANY],
+        [blocks],
+        scratch=[pltpu.SemaphoreType.DMA] * 4,
+        name="load_blocks",
+        cost=8000000,
+    )
+    (row,) = call(
+        local_row_kernel,
+        [row_shape],
         [VMEM, VMEM],
         [right_side, inverse_blocks],
-        name="local_inverse",
+        name="local_rows",
     )
     base, wide = call(
         base_kernel,
@@ -690,14 +808,41 @@
         name="last_apply",
     )
     values.append(following)
-    answer, left_over = call(
-        functools.partial(finish_kernel, ITERS),
-        [right_side.shape] * 2,
-        [VMEM] * (2 * ITERS + 3),
-        [mine, theirs, *values, *fields],
-        name="finish",
-    )
-    return answer, left_over
+    (sound,) = call(
+        functools.partial(decide_kernel, ITERS, width),
+        [(1, 128)],
+        [VMEM, VMEM],
+        [mine, theirs],
+        name="decide",
+    )
+
+    def finish():
+        return tuple(
+            call(
+                functools.partial(finish_kernel, ITERS),
+                [right_side.shape] * 2,
+                [VMEM] * (2 * ITERS + 3),
+                [mine, theirs, *values, *fields],
+                name="finish",
+            )
+        )
+
+    def again():
+        nought = sound[0, 0]
+        whole = nought.astype(jnp.int32)
+        return step_by_step(
+            bits,
+            right_side[0] + nought,
+            blocks[0] + nought,
+            pattern[0] + whole,
+            send_rows[0] + whole,
+            combined + nought,
+            near_null[0] + nought,
+            aggregate[0] + whole,
+            coarse_inverse[0] + nought,
+        )
+
+    return lax.cond(sound[0, 0] > 0.5, finish, again)
 
 
 def solution(mesh):

time: 53.4 us -> 53.8 us (level)
    pallas_call x17 -> x19, Pallas kernels: 10.6 us -> 10.8 us  [call(): pl.pallas_call(kernel, out_shape=[jax.ShapeDtypeStruct(*(out if isinstanc...]
  transfers between devices with their start and end apart: 16 -> 16, of which waited for: 8 -> 8; matrix products, arithmetic and copies ran while one was open for 0% -> 0% of each run, Pallas kernels for 9% -> 10%
where the time goes in v5:
time: 53.8 us; the launch traced here: 53.6 us
  starting transfers between devices  19 us (35%)
  blocking collectives  15.6 us (29%)
  Pallas kernels  10.8 us (20%)
  waiting for transfers between devices  5.83 us (11%)
  local copies, waits for them, and re-layouts  1.17 us (2%)
  between operations  0.92 us (2%)
    ppermute x12, starting transfers between devices, partner(): lax.ppermute(array, axis, [(i, i ^ 1 << bit) for i in range(lax.axis_size...  18.8 us
    all_to_all x1, blocking collectives, on_device(): lines = lax.all_to_all(payload, 'sub', 0, 0)  15.6 us
    pallas_call x19, Pallas kernels, call(): pl.pallas_call(kernel, out_shape=[jax.ShapeDtypeStruct(*(out if isinstanc...  10.8 us
    ppermute x12, waiting for transfers between devices, partner(): lax.ppermute(array, axis, [(i, i ^ 1 << bit) for i in range(lax.axis_size...  3.79 us
    ppermute x4, waiting for transfers between devices, swap(): return lax.ppermute(array, 'coarse', flip)  2.04 us
    unnamed x18, local copies, waits for them, and re-layouts  1.17 us
  transfers between devices with their start and end apart: 16, of which 8 were waited for; matrix products, arithmetic and copies ran while one was open for 0% of the time, Pallas kernels for 10%

profile of v5, /device:TPU:0, one launch (start us, length us, event | category | flops | bytes accessed | tf_op | source)
XLA Modules:
  0.0 53.6 jit_solution(7003900743483170722)
XLA Ops:
  0.6 1.1 %copy-done = f32[1,16,96,96]{3,2,1,0:T(8,128)S(1)} copy-done((f32[1,16,96,96]{3,2,1,0:T(8,128)S(1)}, f32[1,16,96,96]{3,2,1,0:T(8,128)}, u32[]{:S(2)}) %copy-start) | copy-done | bytes 589848
  1.8 0.0 copy-start.2
  1.8 0.2 pack_margin.1
  2.0 4.1 %collective-permute-start.4 = (f32[4,72,128]{2,1,0:T(8,128)S(1)}, f32[4,72,128]{2,1,0:T(8,128)S(1)}, u32[]{:S(2)}, u32[]{:S(2)}) collective-permute-start(f32[4,72,128]{2,1,0:T(8,128)S(1)} %get-tuple-element.296), channel_id=1, source_target_pairs={{0,16},{2,18},{4,20},{6,22},{8,24},{10,26},{12,28},{14,30},{16,0},... | collective-permute-start | bytes 442376 | tf_op jit(solution)/shard_map/ppermute | solution.py:24
  6.1 1.6 %collective-permute-start.5 = (f32[4,72,128]{2,1,0:T(8,128)S(1)}, f32[4,72,128]{2,1,0:T(8,128)S(1)}, u32[]{:S(2)}, u32[]{:S(2)}) collective-permute-start(f32[4,72,128]{2,1,0:T(8,128)S(1)} %get-tuple-element.297), channel_id=1, source_target_pairs={{0,8},{2,10},{4,12},{6,14},{8,0},{10,2},{12,4},{14,6},{16,24},{18,... | collective-permute-start | bytes 442376 | tf_op jit(solution)/shard_map/ppermute | solution.py:24
  7.7 1.5 %collective-permute-start.6 = (f32[4,72,128]{2,1,0:T(8,128)S(1)}, f32[4,72,128]{2,1,0:T(8,128)S(1)}, u32[]{:S(2)}, u32[]{:S(2)}) collective-permute-start(f32[4,72,128]{2,1,0:T(8,128)S(1)} %get-tuple-element.298), channel_id=1, source_target_pairs={{0,4},{2,6},{4,0},{6,2},{8,12},{10,14},{12,8},{14,10},{16,20},{18,... | collective-permute-start | bytes 442376 | tf_op jit(solution)/shard_map/ppermute | solution.py:24
  9.2 1.5 %collective-permute-start.7 = (f32[4,72,128]{2,1,0:T(8,128)S(1)}, f32[4,72,128]{2,1,0:T(8,128)S(1)}, u32[]{:S(2)}, u32[]{:S(2)}) collective-permute-start(f32[4,72,128]{2,1,0:T(8,128)S(1)} %get-tuple-element.299), channel_id=1, source_target_pairs={{0,2},{2,0},{4,6},{6,4},{8,10},{10,8},{12,14},{14,12},{16,18},{18,... | collective-permute-start | bytes 442376 | tf_op jit(solution)/shard_map/ppermute | solution.py:24
  10.7 0.6 %restrict.1 = (s32[16,128]{1,0:T(8,128)S(1)}, f32[1,128]{1,0:T(1,128)S(1)}) custom-call(f32[1,16,96]{2,1,0:T(8,128)S(1)} %copy-done.5, f32[1,6,16,96]{3,2,1,0:T(8,128)S(1)} %bitcast.144, s32[1,16]{1,0:T(1,128)S(1)} %copy-done.10), custom_call_target="tpu_custom_call" | custom-call | bytes 100000 | tf_op jit(solution)/shard_map/restrict/pallas_call | solution.py:28
  11.4 0.1 collective-permute-start.8
  11.4 0.3 local_rows.1.row_ref
  11.7 0.0 copy-start.8
  11.8 0.0 copy-start.6
  11.8 1.0 %load_blocks.1.refs_7_.refs_4_.blocks_ref = f32[1,16,6,96,96]{4,3,2,1,0:T(8,128)S(1)} custom-call(f32[1,16,6,96,96]{4,3,2,1,0:T(8,128)S(1)} %copy-done.2), custom_call_target="tpu_custom_call" | custom-call | bytes 8000000 | tf_op jit(solution)/shard_map/load_blocks/pallas_call | solution.py:28
  12.8 0.8 %tables.1 = (bf16[96,96]{1,0:T(8,128)(2,1)S(1)}, bf16[16,48]{1,0:T(8,128)(2,1)S(1)}, bf16[16,48]{1,0:T(8,128)(2,1)S(1)}, s32[2,128]{1,0:T(2,128)S(1)}) custom-call(s32[6,1,16]{2,1,0:T(1,128)S(1)} %bitcast.163, s32[1,4,4]{2,1,0:T(4,128)S(1)} %copy-done.8), custom_call_target="tpu_custom_call" | custom-call | bytes 100000 | tf_op jit(solution)/shard_map/tables/pallas_call | solution.py:28
  13.6 0.2 first_base.1
  13.8 0.5 collective-permute-done.7.refs_3_.refs_0_
  14.4 1.0 %first_spread.1 = (f32[16,96]{1,0:T(8,128)S(1)}, f32[16,96]{1,0:T(8,128)S(1)}, f32[8,96]{1,0:T(8,128)S(1)}, f32[8,96]{1,0:T(8,128)S(1)}, f32[8,96]{1,0:T(8,128)S(1)}, /*index=5*/f32[8,96]{1,0:T(8,128)S(1)}) custom-call(f32[4,72,128]{2,1,0:T(8,128)S(1)} %collective-permute-done.4.refs_0_.refs_3_, f32[4,72,128]{2,1,0:T(8,128)S(1)} %collective-permute-done.5.refs_1_.refs_2_, ...), custom_call_target="tpu_custom_call" | custom-call | bytes 100000 | tf_op jit(solution)/shard_map/first_spread/pallas_call | solution.py:28
  15.4 0.5 collective-permute-start.9
  15.9 2.4 %collective-permute-start.10 = (f32[8,96]{1,0:T(8,128)S(1)}, f32[8,96]{1,0:T(8,128)S(1)}, u32[]{:S(2)}, u32[]{:S(2)}) collective-permute-start(f32[8,96]{1,0:T(8,128)S(1)} %get-tuple-element.310), channel_id=1, source_target_pairs={{0,8},{2,10},{4,12},{6,14},{8,0},{10,2},{12,4},{14,6},{16,24},{18,... | collective-permute-start | bytes 9224 | tf_op jit(solution)/shard_map/ppermute | solution.py:24
  18.3 1.5 %collective-permute-start.11 = (f32[8,96]{1,0:T(8,128)S(1)}, f32[8,96]{1,0:T(8,128)S(1)}, u32[]{:S(2)}, u32[]{:S(2)}) collective-permute-start(f32[8,96]{1,0:T(8,128)S(1)} %get-tuple-element.311), channel_id=1, source_target_pairs={{0,4},{2,6},{4,0},{6,2},{8,12},{10,14},{12,8},{14,10},{16,20},{18,... | collective-permute-start | bytes 9224 | tf_op jit(solution)/shard_map/ppermute | solution.py:24
  19.8 1.5 %collective-permute-start.12 = (f32[8,96]{1,0:T(8,128)S(1)}, f32[8,96]{1,0:T(8,128)S(1)}, u32[]{:S(2)}, u32[]{:S(2)}) collective-permute-start(f32[8,96]{1,0:T(8,128)S(1)} %get-tuple-element.312), channel_id=1, source_target_pairs={{0,2},{2,0},{4,6},{6,4},{8,10},{10,8},{12,14},{14,12},{16,18},{18,... | collective-permute-start | bytes 9224 | tf_op jit(solution)/shard_map/ppermute | solution.py:24
  21.3 1.0 %combine.1.inverse_ref = f32[16,96,96]{2,1,0:T(8,128)S(1)} custom-call(f32[1,16,96,96]{3,2,1,0:T(8,128)S(1)} %copy-done.1, s32[1,4,4]{2,1,0:T(4,128)S(1)} %copy-done.8, f32[4,72,128]{2,1,0:T(8,128)S(1)} %collective-permute-done.7.refs_3_.refs_0_, f32[4,72,128]{2,1,0:T(8,128)S(1)} %collective-permute-done.6.refs_2_.refs_1_, ...), custom_call_target="tpu_custom_call" | custom-call | bytes 100000 | tf_op jit(solution)/shard_map/combine/pallas_call | solution.py:28
  22.3 1.1 %collective-permute-done.12.refs_3_ = f32[8,96]{1,0:T(8,128)S(1)} collective-permute-done((f32[8,96]{1,0:T(8,128)S(1)}, f32[8,96]{1,0:T(8,128)S(1)}, u32[]{:S(2)}, u32[]{:S(2)}) %collective-permute-start.12) | collective-permute-done | bytes 3104 | tf_op jit(solution)/shard_map/ppermute | solution.py:24
  23.4 0.7 %apply.2 = (f32[16,96]{1,0:T(8,128)S(1)}, f32[1,128]{1,0:T(1,128)S(1)}) custom-call(f32[1,16,96]{2,1,0:T(8,128)S(1)} %copy-done.5, f32[16,96]{1,0:T(8,128)S(1)} %get-tuple-element.307.z_ref.refs_3_, f32[16,96]{1,0:T(8,128)S(1)} %get-tuple-element.308.own_ref, f32[8,96]{1,0:T(8,128)S(1)} %collective-permute-done.9.refs_0_, ...), custom_call_target="tpu_custom_call" | custom-call | bytes 100000 | tf_op jit(solution)/shard_map/apply/pallas_call | solution.py:28
  24.1 0.1 collective-permute-start.13
  24.2 0.3 local_inverse.2
  24.5 0.8 %collective-permute-done.13.refs_3_ = f32[1,128]{1,0:T(1,128)S(1)} collective-permute-done((f32[1,128]{1,0:T(1,128)S(1)}, f32[1,128]{1,0:T(1,128)S(1)}, u32[]{:S(2)}, u32[]{:S(2)}) %collective-permute-start.13) | collective-permute-done | bytes 544 | tf_op jit(solution)/shard_map/ppermute | solution.py:670
  25.3 0.8 %spread.1 = (f32[16,96]{1,0:T(8,128)S(1)}, f32[16,96]{1,0:T(8,128)S(1)}, f32[8,96]{1,0:T(8,128)S(1)}, f32[8,96]{1,0:T(8,128)S(1)}, f32[8,96]{1,0:T(8,128)S(1)}, /*index=5*/f32[8,96]{1,0:T(8,128)S(1)}) custom-call(f32[16,96,128]{2,1,0:T(8,128)S(1)} %get-tuple-element.320.refs_0_, f32[16,96]{1,0:T(8,128)S(1)} %get-tuple-element.321.refs_1_, ...), custom_call_target="tpu_custom_call" | custom-call | bytes 100000 | tf_op jit(solution)/shard_map/spread/pallas_call | solution.py:28
  26.1 0.7 %collective-permute-start.14 = (f32[8,96]{1,0:T(8,128)S(1)}, f32[8,96]{1,0:T(8,128)S(1)}, u32[]{:S(2)}, u32[]{:S(2)}) collective-permute-start(f32[8,96]{1,0:T(8,128)S(1)} %get-tuple-element.325), channel_id=1, source_target_pairs={{0,16},{2,18},{4,20},{6,22},{8,24},{10,26},{12,28},{14,30},{16,0},... | collective-permute-start | bytes 9224 | tf_op jit(solution)/shard_map/ppermute | solution.py:24
  26.8 0.6 %collective-permute-start.15 = (f32[8,96]{1,0:T(8,128)S(1)}, f32[8,96]{1,0:T(8,128)S(1)}, u32[]{:S(2)}, u32[]{:S(2)}) collective-permute-start(f32[8,96]{1,0:T(8,128)S(1)} %get-tuple-element.326), channel_id=1, source_target_pairs={{0,8},{2,10},{4,12},{6,14},{8,0},{10,2},{12,4},{14,6},{16,24},{18,... | collective-permute-start | bytes 9224 | tf_op jit(solution)/shard_map/ppermute | solution.py:24
  27.4 1.4 %collective-permute-start.16 = (f32[8,96]{1,0:T(8,128)S(1)}, f32[8,96]{1,0:T(8,128)S(1)}, u32[]{:S(2)}, u32[]{:S(2)}) collective-permute-start(f32[8,96]{1,0:T(8,128)S(1)} %get-tuple-element.327), channel_id=1, source_target_pairs={{0,4},{2,6},{4,0},{6,2},{8,12},{10,14},{12,8},{14,10},{16,20},{18,... | collective-permute-start | bytes 9224 | tf_op jit(solution)/shard_map/ppermute | solution.py:24
  28.8 1.5 %collective-permute-start.17 = (f32[8,96]{1,0:T(8,128)S(1)}, f32[8,96]{1,0:T(8,128)S(1)}, u32[]{:S(2)}, u32[]{:S(2)}) collective-permute-start(f32[8,96]{1,0:T(8,128)S(1)} %get-tuple-element.328), channel_id=1, source_target_pairs={{0,2},{2,0},{4,6},{6,4},{8,10},{10,8},{12,14},{14,12},{16,18},{18,... | collective-permute-start | bytes 9224 | tf_op jit(solution)/shard_map/ppermute | solution.py:24
  30.3 0.4 collective-permute-done.14.refs_0_
  30.7 0.3 collective-permute-done.16.refs_2_
  31.0 1.4 %collective-permute-done.17.refs_3_ = f32[8,96]{1,0:T(8,128)S(1)} collective-permute-done((f32[8,96]{1,0:T(8,128)S(1)}, f32[8,96]{1,0:T(8,128)S(1)}, u32[]{:S(2)}, u32[]{:S(2)}) %collective-permute-start.17) | collective-permute-done | bytes 3104 | tf_op jit(solution)/shard_map/ppermute | solution.py:24
  32.4 0.7 %apply.3 = (f32[16,96]{1,0:T(8,128)S(1)}, f32[1,128]{1,0:T(1,128)S(1)}) custom-call(f32[16,96]{1,0:T(8,128)S(1)} %get-tuple-element.318.field_ref.refs_1_.refs_11_, f32[16,96]{1,0:T(8,128)S(1)} %get-tuple-element.323.z_ref.refs_4_, f32[16,96]{1,0:T(8,128)S(1)} %get-tuple-element.324.own_ref, f32[8,96]{1,0:T(8,128)S(1)} %collective-permute-done.14.refs_0_, ...), custom_call_target="tpu_custom_call" | custom-call | bytes 100000 | tf_op jit(solution)/shard_map/apply/pallas_call | solution.py:28
  33.1 0.1 collective-permute-start.18
  33.1 0.1 early_dots.1.refs_9_
  33.2 0.3 local_inverse.3
  33.5 0.7 %collective-permute-done.18.refs_3_ = f32[1,128]{1,0:T(1,128)S(1)} collective-permute-done((f32[1,128]{1,0:T(1,128)S(1)}, f32[1,128]{1,0:T(1,128)S(1)}, u32[]{:S(2)}, u32[]{:S(2)}) %collective-permute-start.18) | collective-permute-done | bytes 544 | tf_op jit(solution)/shard_map/ppermute | solution.py:670
  34.2 1.3 %last_spread.1 = (f32[16,96]{1,0:T(8,128)S(1)}, f32[16,96]{1,0:T(8,128)S(1)}, f32[16,32,128]{2,1,0:T(8,128)S(1)}) custom-call(f32[16,96,128]{2,1,0:T(8,128)S(1)} %get-tuple-element.330.refs_0_, f32[16,96]{1,0:T(8,128)S(1)} %get-tuple-element.331.refs_1_, f32[1,128]{1,0:T(1,128)S(1)} %get-tuple-element.332.refs_2_, ...), custom_call_target="tpu_custom_call" | custom-call | bytes 100000 | tf_op jit(solution)/shard_map/last_spread/pallas_call | solution.py:28
  35.5 15.6 %all_to_all.5.lines_ref = f32[16,32,128]{2,1,0:T(8,128)S(1)} all-to-all(f32[16,32,128]{2,1,0:T(8,128)S(1)} %get-tuple-element.333), channel_id=1, replica_groups=mesh['sub'=16,'coarse'=2] {'sub'}, dimensions={0} | all-to-all | bytes 524288 | tf_op jit(solution)/shard_map/all_to_all | solution.py:793
  51.1 0.2 totals.1.mine_ref
  51.3 0.6 %last_apply.1 = f32[16,96]{1,0:T(8,128)S(1)} custom-call(f32[16,96]{1,0:T(8,128)S(1)} %get-tuple-element.329.field_ref.refs_2_.refs_12_, f32[16,96]{1,0:T(8,128)S(1)} %get-tuple-element.334.z_ref, f32[16,96]{1,0:T(8,128)S(1)} %get-tuple-element.335.own_ref, f32[16,32,128]{2,1,0:T(8,128)S(1)} %all_to_all.5.lines_ref, ...), custom_call_target="tpu_custom_call" | custom-call | bytes 100000 | tf_op jit(solution)/shard_map/last_apply/pallas_call | solution.py:28
  51.9 0.5 collective-permute-done.19.theirs_ref
  52.4 0.1 decide.1
  52.6 1.0 %conditional.1 = ((f32[1,16,96]{2,1,0:T(8,128)}, f32[1,16,96]{2,1,0:T(8,128)})) conditional(s32[]{:T(128)} %bitcast.10, (f32[1,128]{1,0:T(1,128)S(1)}, f32[1,16,96]{2,1,0:T(8,128)S(1)}, f32[1,16,6,96]{3,1,2,0:T(8,128)S(1)}, s32[1,16]{1,0:T(1,128)S(1)}, f32[1,48,48]{2,1,0:T(8,128)S(1)}, /*index=5*/f32[16,96,96]{2,1,0:T(8,128)S(1)}, ...), branch_computations={%region_0.8_spmd, %region_8.9_spmd} | conditional | flops 32029620 | bytes 16889252 | solution.py:845
  52.8 0.8 %finish.1 = (f32[1,16,96]{2,1,0:T(8,128)}, f32[1,16,96]{2,1,0:T(8,128)}) custom-call(f32[1,128]{1,0:T(1,128)S(1)} %get-tuple-element.245.mine_ref, f32[1,128]{1,0:T(1,128)S(1)} %get-tuple-element.246.theirs_ref, f32[1,16,96]{2,1,0:T(8,128)S(1)} %get-tuple-element.247.refs_0_, f32[16,96]{1,0:T(8,128)S(1)} %get-tuple-element.248.refs_1_, ...), custom_call_target="tpu_custom_call" | custom-call | bytes 100000 | tf_op jit(solution)/shard_map/cond/branch_1_fun/finish/pallas_call | solution.py:28
  (23 shorter events, 0.1 us)
Async XLA Ops:
  0.6 1.1 %copy-start = (f32[1,16,96,96]{3,2,1,0:T(8,128)S(1)}, f32[1,16,96,96]{3,2,1,0:T(8,128)}, u32[]{:S(2)}) copy-start(f32[1,16,96,96]{3,2,1,0:T(8,128)} %refs_15_.1) | copy-start | bytes 1769476
  1.8 8.9 %copy-start.4 = (f32[1,16,6,96]{3,1,2,0:T(8,128)S(1)}, f32[1,16,6,96]{3,1,2,0:T(8,128)}, u32[]{:S(2)}) copy-start(f32[1,16,6,96]{3,1,2,0:T(8,128)} %param.19) | copy-start | bytes 110596
  1.8 8.9 %copy-start.5 = (f32[1,16,96]{2,1,0:T(8,128)S(1)}, f32[1,16,96]{2,1,0:T(8,128)}, u32[]{:S(2)}) copy-start(f32[1,16,96]{2,1,0:T(8,128)} %refs_10_.3) | copy-start | bytes 18436
  1.8 8.9 %copy-start.10 = (s32[1,16]{1,0:T(1,128)S(1)}, s32[1,16]{1,0:T(1,128)}, u32[]{:S(2)}) copy-start(s32[1,16]{1,0:T(1,128)} %aggregate_ref.1) | copy-start | bytes 196
  1.8 9.7 %copy-start.1 = (f32[1,16,96,96]{3,2,1,0:T(8,128)S(1)}, f32[1,16,96,96]{3,2,1,0:T(8,128)}, u32[]{:S(2)}) copy-start(f32[1,16,96,96]{3,2,1,0:T(8,128)} %inverse_ref.3) | copy-start | bytes 1769476
  1.8 10.0 %copy-start.2 = (f32[1,16,6,96,96]{4,3,2,1,0:T(8,128)S(1)}, f32[1,16,6,96,96]{4,3,2,1,0:T(8,128)}, u32[]{:S(2)}) copy-start(f32[1,16,6,96,96]{4,3,2,1,0:T(8,128)} %source_ref.1) | copy-start | bytes 10616836
  2.0 11.8 %collective-permute-start.4 = (f32[4,72,128]{2,1,0:T(8,128)S(1)}, f32[4,72,128]{2,1,0:T(8,128)S(1)}, u32[]{:S(2)}, u32[]{:S(2)}) collective-permute-start(f32[4,72,128]{2,1,0:T(8,128)S(1)} %get-tuple-element.296), channel_id=1, source_target_pairs={{0,16},{2,18},{4,20},{6,22},{8,24},{10,26},{12,28},{14,30},{16,0},... | collective-permute-start | bytes 442376 | tf_op jit(solution)/shard_map/ppermute | solution.py:24
  6.1 7.7 %collective-permute-start.5 = (f32[4,72,128]{2,1,0:T(8,128)S(1)}, f32[4,72,128]{2,1,0:T(8,128)S(1)}, u32[]{:S(2)}, u32[]{:S(2)}) collective-permute-start(f32[4,72,128]{2,1,0:T(8,128)S(1)} %get-tuple-element.297), channel_id=1, source_target_pairs={{0,8},{2,10},{4,12},{6,14},{8,0},{10,2},{12,4},{14,6},{16,24},{18,... | collective-permute-start | bytes 442376 | tf_op jit(solution)/shard_map/ppermute | solution.py:24
  7.7 6.1 %collective-permute-start.6 = (f32[4,72,128]{2,1,0:T(8,128)S(1)}, f32[4,72,128]{2,1,0:T(8,128)S(1)}, u32[]{:S(2)}, u32[]{:S(2)}) collective-permute-start(f32[4,72,128]{2,1,0:T(8,128)S(1)} %get-tuple-element.298), channel_id=1, source_target_pairs={{0,4},{2,6},{4,0},{6,2},{8,12},{10,14},{12,8},{14,10},{16,20},{18,... | collective-permute-start | bytes 442376 | tf_op jit(solution)/shard_map/ppermute | solution.py:24
  9.2 5.1 %collective-permute-start.7 = (f32[4,72,128]{2,1,0:T(8,128)S(1)}, f32[4,72,128]{2,1,0:T(8,128)S(1)}, u32[]{:S(2)}, u32[]{:S(2)}) collective-permute-start(f32[4,72,128]{2,1,0:T(8,128)S(1)} %get-tuple-element.299), channel_id=1, source_target_pairs={{0,2},{2,0},{4,6},{6,4},{8,10},{10,8},{12,14},{14,12},{16,18},{18,... | collective-permute-start | bytes 442376 | tf_op jit(solution)/shard_map/ppermute | solution.py:24
  11.4 2.2 %collective-permute-start.8 = (f32[1,128]{1,0:T(1,128)S(1)}, f32[1,128]{1,0:T(1,128)S(1)}, u32[]{:S(2)}, u32[]{:S(2)}) collective-permute-start(f32[1,128]{1,0:T(1,128)S(1)} %get-tuple-element.301.mine_ref), channel_id=1, source_target_pairs={{0,1},{1,0},{2,3},{3,2},{4,5},{5,4},{6,7},{7,6},{8,9},{9,8},{10,11... | collective-permute-start | bytes 1544 | tf_op jit(solution)/shard_map/ppermute | solution.py:670
  11.7 1.1 %copy-start.8 = (s32[1,4,4]{2,1,0:T(4,128)S(1)}, s32[1,4,4]{2,1,0:T(4,128)}, u32[]{:S(2)}) copy-start(s32[1,4,4]{2,1,0:T(4,128)} %senders_ref.3) | copy-start | bytes 196
  11.8 1.0 %copy-start.9 = (s32[1,16,6]{1,0,2:T(1,128)S(1)}, s32[1,16,6]{1,0,2:T(1,128)}, u32[]{:S(2)}) copy-start(s32[1,16,6]{1,0,2:T(1,128)} %param.15) | copy-start | bytes 1156
  11.8 1.8 %copy-start.6 = (f32[1,48,48]{2,1,0:T(8,128)S(1)}, f32[1,48,48]{2,1,0:T(8,128)}, u32[]{:S(2)}) copy-start(f32[1,48,48]{2,1,0:T(8,128)} %refs_4_.5) | copy-start | bytes 27652
  15.4 6.9 %collective-permute-start.9 = (f32[8,96]{1,0:T(8,128)S(1)}, f32[8,96]{1,0:T(8,128)S(1)}, u32[]{:S(2)}, u32[]{:S(2)}) collective-permute-start(f32[8,96]{1,0:T(8,128)S(1)} %get-tuple-element.309), channel_id=1, source_target_pairs={{0,16},{2,18},{4,20},{6,22},{8,24},{10,26},{12,28},{14,30},{16,0},... | collective-permute-start | bytes 9224 | tf_op jit(solution)/shard_map/ppermute | solution.py:24
  15.9 6.4 %collective-permute-start.10 = (f32[8,96]{1,0:T(8,128)S(1)}, f32[8,96]{1,0:T(8,128)S(1)}, u32[]{:S(2)}, u32[]{:S(2)}) collective-permute-start(f32[8,96]{1,0:T(8,128)S(1)} %get-tuple-element.310), channel_id=1, source_target_pairs={{0,8},{2,10},{4,12},{6,14},{8,0},{10,2},{12,4},{14,6},{16,24},{18,... | collective-permute-start | bytes 9224 | tf_op jit(solution)/shard_map/ppermute | solution.py:24
  18.3 4.0 %collective-permute-start.11 = (f32[8,96]{1,0:T(8,128)S(1)}, f32[8,96]{1,0:T(8,128)S(1)}, u32[]{:S(2)}, u32[]{:S(2)}) collective-permute-start(f32[8,96]{1,0:T(8,128)S(1)} %get-tuple-element.311), channel_id=1, source_target_pairs={{0,4},{2,6},{4,0},{6,2},{8,12},{10,14},{12,8},{14,10},{16,20},{18,... | collective-permute-start | bytes 9224 | tf_op jit(solution)/shard_map/ppermute | solution.py:24
  19.8 3.6 %collective-permute-start.12 = (f32[8,96]{1,0:T(8,128)S(1)}, f32[8,96]{1,0:T(8,128)S(1)}, u32[]{:S(2)}, u32[]{:S(2)}) collective-permute-start(f32[8,96]{1,0:T(8,128)S(1)} %get-tuple-element.312), channel_id=1, source_target_pairs={{0,2},{2,0},{4,6},{6,4},{8,10},{10,8},{12,14},{14,12},{16,18},{18,... | collective-permute-start | bytes 9224 | tf_op jit(solution)/shard_map/ppermute | solution.py:24
  24.1 1.2 %collective-permute-start.13 = (f32[1,128]{1,0:T(1,128)S(1)}, f32[1,128]{1,0:T(1,128)S(1)}, u32[]{:S(2)}, u32[]{:S(2)}) collective-permute-start(f32[1,128]{1,0:T(1,128)S(1)} %get-tuple-element.322.refs_2_), channel_id=1, source_target_pairs={{0,1},{1,0},{2,3},{3,2},{4,5},{5,4},{6,7},{7,6},{8,9},{9,8},{10,11... | collective-permute-start | bytes 1544 | tf_op jit(solution)/shard_map/ppermute | solution.py:670
  26.1 4.6 %collective-permute-start.14 = (f32[8,96]{1,0:T(8,128)S(1)}, f32[8,96]{1,0:T(8,128)S(1)}, u32[]{:S(2)}, u32[]{:S(2)}) collective-permute-start(f32[8,96]{1,0:T(8,128)S(1)} %get-tuple-element.325), channel_id=1, source_target_pairs={{0,16},{2,18},{4,20},{6,22},{8,24},{10,26},{12,28},{14,30},{16,0},... | collective-permute-start | bytes 9224 | tf_op jit(solution)/shard_map/ppermute | solution.py:24
  26.8 3.9 %collective-permute-start.15 = (f32[8,96]{1,0:T(8,128)S(1)}, f32[8,96]{1,0:T(8,128)S(1)}, u32[]{:S(2)}, u32[]{:S(2)}) collective-permute-start(f32[8,96]{1,0:T(8,128)S(1)} %get-tuple-element.326), channel_id=1, source_target_pairs={{0,8},{2,10},{4,12},{6,14},{8,0},{10,2},{12,4},{14,6},{16,24},{18,... | collective-permute-start | bytes 9224 | tf_op jit(solution)/shard_map/ppermute | solution.py:24
  27.4 3.6 %collective-permute-start.16 = (f32[8,96]{1,0:T(8,128)S(1)}, f32[8,96]{1,0:T(8,128)S(1)}, u32[]{:S(2)}, u32[]{:S(2)}) collective-permute-start(f32[8,96]{1,0:T(8,128)S(1)} %get-tuple-element.327), channel_id=1, source_target_pairs={{0,4},{2,6},{4,0},{6,2},{8,12},{10,14},{12,8},{14,10},{16,20},{18,... | collective-permute-start | bytes 9224 | tf_op jit(solution)/shard_map/ppermute | solution.py:24
  28.8 3.6 %collective-permute-start.17 = (f32[8,96]{1,0:T(8,128)S(1)}, f32[8,96]{1,0:T(8,128)S(1)}, u32[]{:S(2)}, u32[]{:S(2)}) collective-permute-start(f32[8,96]{1,0:T(8,128)S(1)} %get-tuple-element.328), channel_id=1, source_target_pairs={{0,2},{2,0},{4,6},{6,4},{8,10},{10,8},{12,14},{14,12},{16,18},{18,... | collective-permute-start | bytes 9224 | tf_op jit(solution)/shard_map/ppermute | solution.py:24
  33.1 1.2 %collective-permute-start.18 = (f32[1,128]{1,0:T(1,128)S(1)}, f32[1,128]{1,0:T(1,128)S(1)}, u32[]{:S(2)}, u32[]{:S(2)}) collective-permute-start(f32[1,128]{1,0:T(1,128)S(1)} %get-tuple-element.332.refs_2_), channel_id=1, source_target_pairs={{0,1},{1,0},{2,3},{3,2},{4,5},{5,4},{6,7},{7,6},{8,9},{9,8},{10,11... | collective-permute-start | bytes 1544 | tf_op jit(solution)/shard_map/ppermute | solution.py:670
  51.3 1.1 %collective-permute-start.19 = (f32[1,128]{1,0:T(1,128)S(1)}, f32[1,128]{1,0:T(1,128)S(1)}, u32[]{:S(2)}, u32[]{:S(2)}) collective-permute-start(f32[1,128]{1,0:T(1,128)S(1)} %totals.1.mine_ref), channel_id=1, source_target_pairs={{0,1},{1,0},{2,3},{3,2},{4,5},{5,4},{6,7},{7,6},{8,9},{9,8},{10,11... | collective-permute-start | bytes 1544 | tf_op jit(solution)/shard_map/ppermute | solution.py:670

commit v6 on v5

--- a/solution.py
+++ b/solution.py
@@ -62,18 +62,26 @@
     return jnp.sum(total, axis=0, keepdims=True)
 
 
-def coarse_field(mine_ref, theirs_ref, solver_ref, null_ref, offset_ref):
+def coarse_solve(mine_ref, theirs_ref, solver_ref):
     size = solver_ref.shape[1]
     total = mine_ref[...] + theirs_ref[...]
     solved = jnp.sum(solver_ref[0] * total[:, :size], axis=1, keepdims=True)
-    flat = to_row(solved, eye_mask(size))
-    offset = offset_ref[:, :size]
+    return to_row(solved, eye_mask(size))
+
+
+def coarse_combine(flat, offset, terms):
+    offset = offset[:, : flat.shape[1]]
     field = None
-    for mode in range(null_ref.shape[1]):
+    for mode, term in enumerate(terms):
         weight = jnp.sum(jnp.where(offset == mode, flat, 0.0), axis=1, keepdims=True)
-        term = null_ref[0, mode] * weight
-        field = term if field is None else field + term
+        field = term * weight if field is None else field + term * weight
     return field
+
+
+def coarse_field(mine_ref, theirs_ref, solver_ref, null_ref, offset_ref):
+    flat = coarse_solve(mine_ref, theirs_ref, solver_ref)
+    terms = [null_ref[0, mode] for mode in range(null_ref.shape[1])]
+    return coarse_combine(flat, offset_ref[...], terms)
 
 
 def thirds(value):
@@ -110,11 +118,14 @@
                 ]
 
 
-def restrict_kernel(field_ref, null_ref, aggregate_ref, offset_ref, mine_ref):
+def restrict_kernel(field_ref, null_ref, aggregate_ref, offset_ref, wide_offset_ref, mine_ref):
     modes = null_ref.shape[1]
     lane = lax.broadcasted_iota(jnp.int32, (1, 128), 1)
     for i in range(offset_ref.shape[0]):
-        offset_ref[i : i + 1, :] = lane - aggregate_ref[0, i] * modes
+        offset = lane - aggregate_ref[0, i] * modes
+        offset_ref[i : i + 1, :] = offset
+        each = wide_offset_ref.shape[0] // offset_ref.shape[0]
+        wide_offset_ref[i * each : (i + 1) * each, :] = jnp.broadcast_to(offset, (each, 128))
     mine_ref[...] = restrict(null_ref, offset_ref, field_ref[0])
 
 
@@ -170,13 +181,39 @@
         row_ref[i : i + 1, :] = to_row(column, eye)
 
 
-def local_kernel(field_ref, inverse_ref, column_ref, row_ref):
+def local_kernel(field_ref, inverse_ref, blocks_ref, row_ref, parts_ref):
     rows, width = row_ref.shape
     eye = eye_mask(width)
     for i in range(rows):
         column = jnp.sum(inverse_ref[i] * field_ref[i : i + 1, :], axis=1, keepdims=True)
-        column_ref[i] = jnp.broadcast_to(column, (width, 128))
         row_ref[i : i + 1, :] = to_row(column, eye)
+        spread_block_row(blocks_ref, parts_ref, i, column)
+
+
+def modes_kernel(first, blocks_ref, null_ref, out_ref):
+    rows, width = null_ref.shape[2:]
+    modes = out_ref.shape[0]
+    slots = blocks_ref.shape[2]
+    eye = eye_mask(width)
+
+    def body(i, carry):
+        columns = [
+            to_column(null_ref[0, first + mode, pl.ds(i, 1), :], eye) for mode in range(modes)
+        ]
+        for j in range(slots):
+            sums = [None] * modes
+            for start in range(0, width, 8):
+                tile = blocks_ref[0, i, j, start : start + 8, :]
+                for mode in range(modes):
+                    term = tile * columns[mode][start : start + 8]
+                    sums[mode] = term if start == 0 else sums[mode] + term
+            for mode in range(modes):
+                out_ref[mode, pl.ds(i * slots + j, 1), :] = jnp.sum(
+                    sums[mode], axis=0, keepdims=True
+                )
+        return carry
+
+    lax.fori_loop(0, rows, body, 0, unroll=2)
 
 
 def spread_block_row(blocks_ref, parts_ref, i, column):
@@ -308,34 +345,36 @@
 
 
 def spread_rows(
-    column_ref,
+    local_ref,
     row_ref,
     mine_ref,
     theirs_ref,
     solver_ref,
     null_ref,
     offset_ref,
-    blocks_ref,
+    wide_offset_ref,
+    early_modes_ref,
+    late_modes_ref,
     z_ref,
     parts_ref,
 ):
-    rows, width = z_ref.shape
-    eye = eye_mask(width)
-    coarse = coarse_field(mine_ref, theirs_ref, solver_ref, null_ref, offset_ref)
+    flat = coarse_solve(mine_ref, theirs_ref, solver_ref)
+    modes = null_ref.shape[1]
+    terms = [ref[mode] for ref in (early_modes_ref, late_modes_ref) for mode in range(ref.shape[0])]
+    added = coarse_combine(flat, wide_offset_ref[...], terms)
+    parts_ref[...] = local_ref[...] + added
+    coarse = coarse_combine(flat, offset_ref[...], [null_ref[0, mode] for mode in range(modes)])
     z_ref[...] = row_ref[...] + coarse
-    for i in range(rows):
-        column = column_ref[i][:, :width] + to_column(coarse[i : i + 1], eye)
-        spread_block_row(blocks_ref, parts_ref, i, column)
 
 
 def spread_kernel(turns, *refs):
-    index_ref, z_ref, own_ref = refs[8:11]
-    packets = refs[11 : 11 + turns]
-    parts_ref, slots_ref, indices_ref, sem = refs[11 + turns :]
+    index_ref, z_ref, own_ref = refs[10:13]
+    packets = refs[13 : 13 + turns]
+    parts_ref, slots_ref, indices_ref, sem = refs[13 + turns :]
     fetch = pltpu.make_async_copy(index_ref, indices_ref, sem)
     fetch.start()
     slots_ref[...] = jnp.zeros(slots_ref.shape, f32)
-    spread_rows(*refs[:8], z_ref, parts_ref)
+    spread_rows(*refs[:10], z_ref, parts_ref)
     fetch.wait()
     finish_spread(parts_ref, slots_ref, indices_ref, z_ref, own_ref, packets)
 
@@ -359,14 +398,14 @@
 
 
 def last_spread_kernel(fields, *refs):
-    index_ref, early_ref = refs[8:10]
-    value_refs = refs[10 : 10 + fields]
-    z_ref, own_ref, payload_ref, parts_ref, slots_ref, line_ref, indices_ref, sem = refs[10 + fields :]
+    index_ref, early_ref = refs[10:12]
+    value_refs = refs[12 : 12 + fields]
+    z_ref, own_ref, payload_ref, parts_ref, slots_ref, line_ref, indices_ref, sem = refs[12 + fields :]
     fetch = pltpu.make_async_copy(index_ref, indices_ref, sem)
     fetch.start()
     slots_ref[...] = jnp.zeros(slots_ref.shape, f32)
     line_ref[...] = jnp.zeros(line_ref.shape, f32)
-    spread_rows(*refs[:8], z_ref, parts_ref)
+    spread_rows(*refs[:10], z_ref, parts_ref)
     rows, width = z_ref.shape
     ghosts = line_ref.shape[0] // 2
     z = z_ref[...]
@@ -677,9 +716,9 @@
         name="pack_margin",
     )
     gathered = [partner(packs[turn], "sub", bits[turn]) for turn in range(turns)]
-    offset, mine = call(
+    offset, wide_offset, mine = call(
         restrict_kernel,
-        [((rows, 128), jnp.int32), (1, 128)],
+        [((rows, 128), jnp.int32), ((parts, 128), jnp.int32), (1, 128)],
         [VMEM, VMEM, SMEM],
         [right_side, null_view, aggregate],
         name="restrict",
@@ -722,6 +761,18 @@
         [source, send, row, mine, theirs, solver, null_modes, offset],
         name="first_base",
     )
+    half = modes // 2
+    early_modes, late_modes = (
+        call(
+            functools.partial(modes_kernel, first),
+            [(count, parts, width)],
+            [VMEM, VMEM],
+            [held, null_modes],
+            name="spread_modes",
+        )[0]
+        for first, count in ((0, half), (half, modes - half))
+    )
+    base, early_modes = lax.optimization_barrier([base, early_modes])
     z, own, *packets = call(
         functools.partial(first_kernel, turns),
         [row_shape, row_shape] + [packet] * turns,
@@ -742,7 +793,9 @@
     for step in range(ITERS - 1):
         arrived = [partner(packets[turn], "sub", bits[turn]) for turn in range(turns)]
         if step == 0:
-            combined, *arrived = lax.optimization_barrier([combined, *arrived[::-1]])
+            combined, late_modes, *arrived = lax.optimization_barrier(
+                [combined, late_modes, *arrived[::-1]]
+            )
             arrived = arrived[::-1]
         following, mine = call(
             functools.partial(apply_kernel, turns),
@@ -754,19 +807,20 @@
         )
         values.append(following)
         theirs = swap(mine)
-        column, row = call(
+        row, local = call(
             local_kernel,
-            [(rows, width, 128), row_shape],
-            [VMEM, VMEM],
-            [following, combined],
+            [row_shape, (parts, width)],
+            [VMEM, VMEM, VMEM],
+            [following, combined, held],
             name="local_inverse",
         )
-        inputs = [column, row, mine, theirs, solver, null_modes, offset, held, index]
+        inputs = [local, row, mine, theirs, solver, null_modes, offset, wide_offset]
+        inputs += [early_modes, late_modes, index]
         if step + 2 < ITERS:
             z, own, *packets = call(
                 functools.partial(spread_kernel, turns),
                 [row_shape, row_shape] + [packet] * turns,
-                [VMEM] * 9,
+                [VMEM] * 11,
                 inputs,
                 scratch=spread_scratch,
                 name="spread",
@@ -782,7 +836,7 @@
             z, own, payload = call(
                 functools.partial(last_spread_kernel, ITERS),
                 [row_shape, row_shape, (lax.axis_size("sub"), 2 * ghost_total, 128)],
-                [VMEM] * (10 + ITERS),
+                [VMEM] * (12 + ITERS),
                 [*inputs, early, *values],
                 scratch=spread_scratch[:2]
                 + [pltpu.VMEM((2 * ghost_total, 128), f32)]

time: 53.8 us -> 53.2 us (0.989)
  Pallas kernels: 10.8 us -> 14.5 us
  waiting for transfers between devices: 5.83 us -> 3.85 us
  blocking collectives: 15.6 us -> 14.3 us
  starting transfers between devices: 19 us -> 18 us
    pallas_call x19 -> x21, Pallas kernels: 10.8 us -> 14.5 us  [call(): pl.pallas_call(kernel, out_shape=[jax.ShapeDtypeStruct(*(out if isinstanc...]
    ppermute x12, waiting for transfers between devices: 3.79 us -> 2.39 us  [partner(): lax.ppermute(array, axis, [(i, i ^ 1 << bit) for i in range(lax.axis_size...]
    all_to_all x1, blocking collectives: 15.6 us -> 14.3 us  [on_device(): lines = lax.all_to_all(payload, 'sub', 0, 0)]
    ppermute x12, starting transfers between devices: 18.8 us -> 17.8 us  [partner(): lax.ppermute(array, axis, [(i, i ^ 1 << bit) for i in range(lax.axis_size...]
    ppermute x4, waiting for transfers between devices: 2.04 us -> 1.46 us  [swap(): return lax.ppermute(array, 'coarse', flip)]
  transfers between devices with their start and end apart: 16 -> 16, of which waited for: 8 -> 6; matrix products, arithmetic and copies ran while one was open for 0% -> 0% of each run, Pallas kernels for 10% -> 18%
where the time goes in v6:
time: 53.2 us; the launch traced here: 53 us
  starting transfers between devices  18 us (34%)
  Pallas kernels  14.5 us (27%)
  blocking collectives  14.3 us (27%)
  waiting for transfers between devices  3.85 us (7%)
  local copies, waits for them, and re-layouts  1.17 us (2%)
  between operations  0.95 us (2%)
    ppermute x12, starting transfers between devices, partner(): lax.ppermute(array, axis, [(i, i ^ 1 << bit) for i in range(lax.axis_size...  17.8 us
    pallas_call x21, Pallas kernels, call(): pl.pallas_call(kernel, out_shape=[jax.ShapeDtypeStruct(*(out if isinstanc...  14.5 us
    all_to_all x1, blocking collectives, on_device(): lines = lax.all_to_all(payload, 'sub', 0, 0)  14.3 us
    ppermute x12, waiting for transfers between devices, partner(): lax.ppermute(array, axis, [(i, i ^ 1 << bit) for i in range(lax.axis_size...  2.39 us
    ppermute x4, waiting for transfers between devices, swap(): return lax.ppermute(array, 'coarse', flip)  1.46 us
    unnamed x18, local copies, waits for them, and re-layouts  1.17 us
  transfers between devices with their start and end apart: 16, of which 6 were waited for; matrix products, arithmetic and copies ran while one was open for 0% of the time, Pallas kernels for 18%

profile of v6, /device:TPU:0, one launch (start us, length us, event | category | flops | bytes accessed | tf_op | source)
XLA Modules:
  0.0 53.0 jit_solution(6110305551606162806)
XLA Ops:
  0.6 1.1 %copy-done = f32[1,16,96,96]{3,2,1,0:T(8,128)S(1)} copy-done((f32[1,16,96,96]{3,2,1,0:T(8,128)S(1)}, f32[1,16,96,96]{3,2,1,0:T(8,128)}, u32[]{:S(2)}) %copy-start) | copy-done | bytes 589848
  1.8 0.0 copy-start.2
  1.8 0.2 pack_margin.1
  2.0 4.1 %collective-permute-start.4 = (f32[4,72,128]{2,1,0:T(8,128)S(1)}, f32[4,72,128]{2,1,0:T(8,128)S(1)}, u32[]{:S(2)}, u32[]{:S(2)}) collective-permute-start(f32[4,72,128]{2,1,0:T(8,128)S(1)} %get-tuple-element.300), channel_id=1, source_target_pairs={{0,16},{2,18},{4,20},{6,22},{8,24},{10,26},{12,28},{14,30},{16,0},... | collective-permute-start | bytes 442376 | tf_op jit(solution)/shard_map/ppermute | solution.py:24
  6.1 1.6 %collective-permute-start.5 = (f32[4,72,128]{2,1,0:T(8,128)S(1)}, f32[4,72,128]{2,1,0:T(8,128)S(1)}, u32[]{:S(2)}, u32[]{:S(2)}) collective-permute-start(f32[4,72,128]{2,1,0:T(8,128)S(1)} %get-tuple-element.301), channel_id=1, source_target_pairs={{0,8},{2,10},{4,12},{6,14},{8,0},{10,2},{12,4},{14,6},{16,24},{18,... | collective-permute-start | bytes 442376 | tf_op jit(solution)/shard_map/ppermute | solution.py:24
  7.7 1.5 %collective-permute-start.6 = (f32[4,72,128]{2,1,0:T(8,128)S(1)}, f32[4,72,128]{2,1,0:T(8,128)S(1)}, u32[]{:S(2)}, u32[]{:S(2)}) collective-permute-start(f32[4,72,128]{2,1,0:T(8,128)S(1)} %get-tuple-element.302), channel_id=1, source_target_pairs={{0,4},{2,6},{4,0},{6,2},{8,12},{10,14},{12,8},{14,10},{16,20},{18,... | collective-permute-start | bytes 442376 | tf_op jit(solution)/shard_map/ppermute | solution.py:24
  9.2 1.5 %collective-permute-start.7 = (f32[4,72,128]{2,1,0:T(8,128)S(1)}, f32[4,72,128]{2,1,0:T(8,128)S(1)}, u32[]{:S(2)}, u32[]{:S(2)}) collective-permute-start(f32[4,72,128]{2,1,0:T(8,128)S(1)} %get-tuple-element.303), channel_id=1, source_target_pairs={{0,2},{2,0},{4,6},{6,4},{8,10},{10,8},{12,14},{14,12},{16,18},{18,... | collective-permute-start | bytes 442376 | tf_op jit(solution)/shard_map/ppermute | solution.py:24
  10.7 0.6 %restrict.1 = (s32[16,128]{1,0:T(8,128)S(1)}, s32[96,128]{1,0:T(8,128)S(1)}, f32[1,128]{1,0:T(1,128)S(1)}) custom-call(f32[1,16,96]{2,1,0:T(8,128)S(1)} %copy-done.5, f32[1,6,16,96]{3,2,1,0:T(8,128)S(1)} %bitcast.141, s32[1,16]{1,0:T(1,128)S(1)} %copy-done.10), custom_call_target="tpu_custom_call" | custom-call | bytes 100000 | tf_op jit(solution)/shard_map/restrict/pallas_call | solution.py:28
  11.4 0.1 collective-permute-start.8
  11.4 0.3 local_rows.1.row_ref
  11.7 1.0 %load_blocks.1.blocks_ref.refs_7_.refs_4_ = f32[1,16,6,96,96]{4,3,2,1,0:T(8,128)S(1)} custom-call(f32[1,16,6,96,96]{4,3,2,1,0:T(8,128)S(1)} %copy-done.2), custom_call_target="tpu_custom_call" | custom-call | bytes 8000000 | tf_op jit(solution)/shard_map/load_blocks/pallas_call | solution.py:28
  12.8 0.0 copy-start.8
  12.8 0.0 copy-start.9
  12.8 1.8 %spread_modes.2.refs_8_ = f32[3,96,96]{2,1,0:T(8,128)S(1)} custom-call(f32[1,16,6,96,96]{4,3,2,1,0:T(8,128)S(1)} %load_blocks.1.blocks_ref.refs_7_.refs_4_, f32[1,6,16,96]{3,2,1,0:T(8,128)S(1)} %bitcast.142), custom_call_target="tpu_custom_call" | custom-call | bytes 100000 | tf_op jit(solution)/shard_map/spread_modes/pallas_call | solution.py:28
  14.6 0.8 %tables.1 = (bf16[96,96]{1,0:T(8,128)(2,1)S(1)}, bf16[16,48]{1,0:T(8,128)(2,1)S(1)}, bf16[16,48]{1,0:T(8,128)(2,1)S(1)}, s32[2,128]{1,0:T(2,128)S(1)}) custom-call(s32[6,1,16]{2,1,0:T(1,128)S(1)} %bitcast.165, s32[1,4,4]{2,1,0:T(4,128)S(1)} %copy-done.8), custom_call_target="tpu_custom_call" | custom-call | bytes 100000 | tf_op jit(solution)/shard_map/tables/pallas_call | solution.py:28
  15.4 0.2 first_base.1
  15.6 1.0 %first_spread.1 = (f32[16,96]{1,0:T(8,128)S(1)}, f32[16,96]{1,0:T(8,128)S(1)}, f32[8,96]{1,0:T(8,128)S(1)}, f32[8,96]{1,0:T(8,128)S(1)}, f32[8,96]{1,0:T(8,128)S(1)}, /*index=5*/f32[8,96]{1,0:T(8,128)S(1)}) custom-call(f32[4,72,128]{2,1,0:T(8,128)S(1)} %collective-permute-done.4.refs_0_.refs_3_, f32[4,72,128]{2,1,0:T(8,128)S(1)} %collective-permute-done.5.refs_1_.refs_2_, ...), custom_call_target="tpu_custom_call" | custom-call | bytes 100000 | tf_op jit(solution)/shard_map/first_spread/pallas_call | solution.py:28
  16.7 0.4 collective-permute-start.9
  17.1 1.3 %collective-permute-start.10 = (f32[8,96]{1,0:T(8,128)S(1)}, f32[8,96]{1,0:T(8,128)S(1)}, u32[]{:S(2)}, u32[]{:S(2)}) collective-permute-start(f32[8,96]{1,0:T(8,128)S(1)} %get-tuple-element.315), channel_id=1, source_target_pairs={{0,8},{2,10},{4,12},{6,14},{8,0},{10,2},{12,4},{14,6},{16,24},{18,... | collective-permute-start | bytes 9224 | tf_op jit(solution)/shard_map/ppermute | solution.py:24
  18.3 1.5 %collective-permute-start.11 = (f32[8,96]{1,0:T(8,128)S(1)}, f32[8,96]{1,0:T(8,128)S(1)}, u32[]{:S(2)}, u32[]{:S(2)}) collective-permute-start(f32[8,96]{1,0:T(8,128)S(1)} %get-tuple-element.316), channel_id=1, source_target_pairs={{0,4},{2,6},{4,0},{6,2},{8,12},{10,14},{12,8},{14,10},{16,20},{18,... | collective-permute-start | bytes 9224 | tf_op jit(solution)/shard_map/ppermute | solution.py:24
  19.8 1.5 %collective-permute-start.12 = (f32[8,96]{1,0:T(8,128)S(1)}, f32[8,96]{1,0:T(8,128)S(1)}, u32[]{:S(2)}, u32[]{:S(2)}) collective-permute-start(f32[8,96]{1,0:T(8,128)S(1)} %get-tuple-element.317), channel_id=1, source_target_pairs={{0,2},{2,0},{4,6},{6,4},{8,10},{10,8},{12,14},{14,12},{16,18},{18,... | collective-permute-start | bytes 9224 | tf_op jit(solution)/shard_map/ppermute | solution.py:24
  21.3 1.8 %spread_modes.3.refs_9_ = f32[3,96,96]{2,1,0:T(8,128)S(1)} custom-call(f32[1,16,6,96,96]{4,3,2,1,0:T(8,128)S(1)} %load_blocks.1.blocks_ref.refs_7_.refs_4_, f32[1,6,16,96]{3,2,1,0:T(8,128)S(1)} %bitcast.144), custom_call_target="tpu_custom_call" | custom-call | bytes 100000 | tf_op jit(solution)/shard_map/spread_modes/pallas_call | solution.py:28
  23.1 1.0 %combine.1.inverse_ref = f32[16,96,96]{2,1,0:T(8,128)S(1)} custom-call(f32[1,16,96,96]{3,2,1,0:T(8,128)S(1)} %copy-done.1, s32[1,4,4]{2,1,0:T(4,128)S(1)} %copy-done.8, f32[4,72,128]{2,1,0:T(8,128)S(1)} %collective-permute-done.7.refs_3_.refs_0_, f32[4,72,128]{2,1,0:T(8,128)S(1)} %collective-permute-done.6.refs_2_.refs_1_, ...), custom_call_target="tpu_custom_call" | custom-call | bytes 100000 | tf_op jit(solution)/shard_map/combine/pallas_call | solution.py:28
  24.1 0.7 %apply.2 = (f32[16,96]{1,0:T(8,128)S(1)}, f32[1,128]{1,0:T(1,128)S(1)}) custom-call(f32[1,16,96]{2,1,0:T(8,128)S(1)} %copy-done.5, f32[16,96]{1,0:T(8,128)S(1)} %get-tuple-element.312.z_ref.refs_3_, f32[16,96]{1,0:T(8,128)S(1)} %get-tuple-element.313.own_ref, f32[8,96]{1,0:T(8,128)S(1)} %collective-permute-done.9.refs_0_, ...), custom_call_target="tpu_custom_call" | custom-call | bytes 100000 | tf_op jit(solution)/shard_map/apply/pallas_call | solution.py:28
  24.8 0.1 collective-permute-start.13
  24.9 0.6 %local_inverse.2 = (f32[16,96]{1,0:T(8,128)S(1)}, f32[96,96]{1,0:T(8,128)S(1)}) custom-call(f32[16,96]{1,0:T(8,128)S(1)} %get-tuple-element.323.field_ref.refs_1_.refs_13_, f32[16,96,96]{2,1,0:T(8,128)S(1)} %combine.1.inverse_ref, f32[1,16,6,96,96]{4,3,2,1,0:T(8,128)S(1)} %load_blocks.1.blocks_ref.refs_7_.refs_4_), custom_call_target="tpu_custom_call" | custom-call | bytes 100000 | tf_op jit(solution)/shard_map/local_inverse/pallas_call | solution.py:28
  25.5 0.5 collective-permute-done.13.refs_3_
  26.0 0.6 %spread.1 = (f32[16,96]{1,0:T(8,128)S(1)}, f32[16,96]{1,0:T(8,128)S(1)}, f32[8,96]{1,0:T(8,128)S(1)}, f32[8,96]{1,0:T(8,128)S(1)}, f32[8,96]{1,0:T(8,128)S(1)}, /*index=5*/f32[8,96]{1,0:T(8,128)S(1)}) custom-call(f32[96,96]{1,0:T(8,128)S(1)} %get-tuple-element.325.refs_0_, f32[16,96]{1,0:T(8,128)S(1)} %get-tuple-element.326.refs_1_, ...), custom_call_target="tpu_custom_call" | custom-call | bytes 100000 | tf_op jit(solution)/shard_map/spread/pallas_call | solution.py:28
  26.6 0.7 %collective-permute-start.14 = (f32[8,96]{1,0:T(8,128)S(1)}, f32[8,96]{1,0:T(8,128)S(1)}, u32[]{:S(2)}, u32[]{:S(2)}) collective-permute-start(f32[8,96]{1,0:T(8,128)S(1)} %get-tuple-element.333), channel_id=1, source_target_pairs={{0,16},{2,18},{4,20},{6,22},{8,24},{10,26},{12,28},{14,30},{16,0},... | collective-permute-start | bytes 9224 | tf_op jit(solution)/shard_map/ppermute | solution.py:24
  27.3 1.0 %collective-permute-start.15 = (f32[8,96]{1,0:T(8,128)S(1)}, f32[8,96]{1,0:T(8,128)S(1)}, u32[]{:S(2)}, u32[]{:S(2)}) collective-permute-start(f32[8,96]{1,0:T(8,128)S(1)} %get-tuple-element.334), channel_id=1, source_target_pairs={{0,8},{2,10},{4,12},{6,14},{8,0},{10,2},{12,4},{14,6},{16,24},{18,... | collective-permute-start | bytes 9224 | tf_op jit(solution)/shard_map/ppermute | solution.py:24
  28.4 1.5 %collective-permute-start.16 = (f32[8,96]{1,0:T(8,128)S(1)}, f32[8,96]{1,0:T(8,128)S(1)}, u32[]{:S(2)}, u32[]{:S(2)}) collective-permute-start(f32[8,96]{1,0:T(8,128)S(1)} %get-tuple-element.335), channel_id=1, source_target_pairs={{0,4},{2,6},{4,0},{6,2},{8,12},{10,14},{12,8},{14,10},{16,20},{18,... | collective-permute-start | bytes 9224 | tf_op jit(solution)/shard_map/ppermute | solution.py:24
  29.9 1.2 %collective-permute-start.17 = (f32[8,96]{1,0:T(8,128)S(1)}, f32[8,96]{1,0:T(8,128)S(1)}, u32[]{:S(2)}, u32[]{:S(2)}) collective-permute-start(f32[8,96]{1,0:T(8,128)S(1)} %get-tuple-element.336), channel_id=1, source_target_pairs={{0,2},{2,0},{4,6},{6,4},{8,10},{10,8},{12,14},{14,12},{16,18},{18,... | collective-permute-start | bytes 9224 | tf_op jit(solution)/shard_map/ppermute | solution.py:24
  31.1 0.1 collective-permute-done.14.refs_0_
  31.2 0.7 %collective-permute-done.16.refs_2_ = f32[8,96]{1,0:T(8,128)S(1)} collective-permute-done((f32[8,96]{1,0:T(8,128)S(1)}, f32[8,96]{1,0:T(8,128)S(1)}, u32[]{:S(2)}, u32[]{:S(2)}) %collective-permute-start.16) | collective-permute-done | bytes 3104 | tf_op jit(solution)/shard_map/ppermute | solution.py:24
  32.0 1.5 %collective-permute-done.17.refs_3_ = f32[8,96]{1,0:T(8,128)S(1)} collective-permute-done((f32[8,96]{1,0:T(8,128)S(1)}, f32[8,96]{1,0:T(8,128)S(1)}, u32[]{:S(2)}, u32[]{:S(2)}) %collective-permute-start.17) | collective-permute-done | bytes 3104 | tf_op jit(solution)/shard_map/ppermute | solution.py:24
  33.5 0.7 %apply.3 = (f32[16,96]{1,0:T(8,128)S(1)}, f32[1,128]{1,0:T(1,128)S(1)}) custom-call(f32[16,96]{1,0:T(8,128)S(1)} %get-tuple-element.323.field_ref.refs_1_.refs_13_, f32[16,96]{1,0:T(8,128)S(1)} %get-tuple-element.331.z_ref.refs_4_, f32[16,96]{1,0:T(8,128)S(1)} %get-tuple-element.332.own_ref, f32[8,96]{1,0:T(8,128)S(1)} %collective-permute-done.14.refs_0_, ...), custom_call_target="tpu_custom_call" | custom-call | bytes 100000 | tf_op jit(solution)/shard_map/apply/pallas_call | solution.py:28
  34.2 0.1 collective-permute-start.18
  34.3 0.1 early_dots.1.refs_11_
  34.3 0.6 %local_inverse.3 = (f32[16,96]{1,0:T(8,128)S(1)}, f32[96,96]{1,0:T(8,128)S(1)}) custom-call(f32[16,96]{1,0:T(8,128)S(1)} %get-tuple-element.337.field_ref.refs_2_.refs_14_, f32[16,96,96]{2,1,0:T(8,128)S(1)} %combine.1.inverse_ref, f32[1,16,6,96,96]{4,3,2,1,0:T(8,128)S(1)} %load_blocks.1.blocks_ref.refs_7_.refs_4_), custom_call_target="tpu_custom_call" | custom-call | bytes 100000 | tf_op jit(solution)/shard_map/local_inverse/pallas_call | solution.py:28
  34.9 0.4 collective-permute-done.18.refs_3_
  35.4 0.9 %last_spread.1 = (f32[16,96]{1,0:T(8,128)S(1)}, f32[16,96]{1,0:T(8,128)S(1)}, f32[16,32,128]{2,1,0:T(8,128)S(1)}) custom-call(f32[96,96]{1,0:T(8,128)S(1)} %get-tuple-element.338.refs_0_, f32[16,96]{1,0:T(8,128)S(1)} %get-tuple-element.339.refs_1_, f32[1,128]{1,0:T(1,128)S(1)} %get-tuple-element.340.refs_2_, f32[1,128]{1,0:T(1,128)S(1)} %collective-permute-done.18.refs_3_, ...), custom_call_target="tpu_custom_call" | custom-call | bytes 100000 | tf_op jit(solution)/shard_map/last_spread/pallas_call | solution.py:28
  36.3 14.3 %all_to_all.5.lines_ref = f32[16,32,128]{2,1,0:T(8,128)S(1)} all-to-all(f32[16,32,128]{2,1,0:T(8,128)S(1)} %get-tuple-element.341), channel_id=1, replica_groups=mesh['sub'=16,'coarse'=2] {'sub'}, dimensions={0} | all-to-all | bytes 524288 | tf_op jit(solution)/shard_map/all_to_all | solution.py:847
  50.6 0.2 totals.1.mine_ref
  50.8 0.6 %last_apply.1 = f32[16,96]{1,0:T(8,128)S(1)} custom-call(f32[16,96]{1,0:T(8,128)S(1)} %get-tuple-element.337.field_ref.refs_2_.refs_14_, f32[16,96]{1,0:T(8,128)S(1)} %get-tuple-element.342.z_ref, f32[16,96]{1,0:T(8,128)S(1)} %get-tuple-element.343.own_ref, f32[16,32,128]{2,1,0:T(8,128)S(1)} %all_to_all.5.lines_ref, ...), custom_call_target="tpu_custom_call" | custom-call | bytes 100000 | tf_op jit(solution)/shard_map/last_apply/pallas_call | solution.py:28
  51.4 0.5 collective-permute-done.19.theirs_ref
  51.9 0.1 decide.1
  52.1 1.0 %conditional.1 = ((f32[1,16,96]{2,1,0:T(8,128)}, f32[1,16,96]{2,1,0:T(8,128)})) conditional(s32[]{:T(128)} %bitcast.10, (f32[1,128]{1,0:T(1,128)S(1)}, f32[1,16,96]{2,1,0:T(8,128)S(1)}, f32[1,16,6,96]{3,1,2,0:T(8,128)S(1)}, s32[1,16]{1,0:T(1,128)S(1)}, f32[1,48,48]{2,1,0:T(8,128)S(1)}, /*index=5*/f32[16,96,96]{2,1,0:T(8,128)S(1)}, ...), branch_computations={%region_0.8_spmd, %region_8.9_spmd} | conditional | flops 32029620 | bytes 16889252 | solution.py:899
  52.3 0.8 %finish.1 = (f32[1,16,96]{2,1,0:T(8,128)}, f32[1,16,96]{2,1,0:T(8,128)}) custom-call(f32[1,128]{1,0:T(1,128)S(1)} %get-tuple-element.245.mine_ref, f32[1,128]{1,0:T(1,128)S(1)} %get-tuple-element.246.theirs_ref, f32[1,16,96]{2,1,0:T(8,128)S(1)} %get-tuple-element.247.refs_0_, f32[16,96]{1,0:T(8,128)S(1)} %get-tuple-element.248.refs_1_, ...), custom_call_target="tpu_custom_call" | custom-call | bytes 100000 | tf_op jit(solution)/shard_map/cond/branch_1_fun/finish/pallas_call | solution.py:28
  (25 shorter events, 0.1 us)
Async XLA Ops:
  0.6 1.1 %copy-start = (f32[1,16,96,96]{3,2,1,0:T(8,128)S(1)}, f32[1,16,96,96]{3,2,1,0:T(8,128)}, u32[]{:S(2)}) copy-start(f32[1,16,96,96]{3,2,1,0:T(8,128)} %refs_15_.1) | copy-start | bytes 1769476
  1.8 8.9 %copy-start.3 = (f32[1,16,6,96]{3,1,2,0:T(8,128)S(1)}, f32[1,16,6,96]{3,1,2,0:T(8,128)}, u32[]{:S(2)}) copy-start(f32[1,16,6,96]{3,1,2,0:T(8,128)} %param.19) | copy-start | bytes 110596
  1.8 8.9 %copy-start.5 = (f32[1,16,96]{2,1,0:T(8,128)S(1)}, f32[1,16,96]{2,1,0:T(8,128)}, u32[]{:S(2)}) copy-start(f32[1,16,96]{2,1,0:T(8,128)} %refs_12_.3) | copy-start | bytes 18436
  1.8 8.9 %copy-start.10 = (s32[1,16]{1,0:T(1,128)S(1)}, s32[1,16]{1,0:T(1,128)}, u32[]{:S(2)}) copy-start(s32[1,16]{1,0:T(1,128)} %aggregate_ref.1) | copy-start | bytes 196
  1.8 9.7 %copy-start.1 = (f32[1,16,96,96]{3,2,1,0:T(8,128)S(1)}, f32[1,16,96,96]{3,2,1,0:T(8,128)}, u32[]{:S(2)}) copy-start(f32[1,16,96,96]{3,2,1,0:T(8,128)} %inverse_ref.3) | copy-start | bytes 1769476
  1.8 10.0 %copy-start.2 = (f32[1,16,6,96,96]{4,3,2,1,0:T(8,128)S(1)}, f32[1,16,6,96,96]{4,3,2,1,0:T(8,128)}, u32[]{:S(2)}) copy-start(f32[1,16,6,96,96]{4,3,2,1,0:T(8,128)} %source_ref.1) | copy-start | bytes 10616836
  2.0 13.6 %collective-permute-start.4 = (f32[4,72,128]{2,1,0:T(8,128)S(1)}, f32[4,72,128]{2,1,0:T(8,128)S(1)}, u32[]{:S(2)}, u32[]{:S(2)}) collective-permute-start(f32[4,72,128]{2,1,0:T(8,128)S(1)} %get-tuple-element.300), channel_id=1, source_target_pairs={{0,16},{2,18},{4,20},{6,22},{8,24},{10,26},{12,28},{14,30},{16,0},... | collective-permute-start | bytes 442376 | tf_op jit(solution)/shard_map/ppermute | solution.py:24
  6.1 9.5 %collective-permute-start.5 = (f32[4,72,128]{2,1,0:T(8,128)S(1)}, f32[4,72,128]{2,1,0:T(8,128)S(1)}, u32[]{:S(2)}, u32[]{:S(2)}) collective-permute-start(f32[4,72,128]{2,1,0:T(8,128)S(1)} %get-tuple-element.301), channel_id=1, source_target_pairs={{0,8},{2,10},{4,12},{6,14},{8,0},{10,2},{12,4},{14,6},{16,24},{18,... | collective-permute-start | bytes 442376 | tf_op jit(solution)/shard_map/ppermute | solution.py:24
  7.7 7.9 %collective-permute-start.6 = (f32[4,72,128]{2,1,0:T(8,128)S(1)}, f32[4,72,128]{2,1,0:T(8,128)S(1)}, u32[]{:S(2)}, u32[]{:S(2)}) collective-permute-start(f32[4,72,128]{2,1,0:T(8,128)S(1)} %get-tuple-element.302), channel_id=1, source_target_pairs={{0,4},{2,6},{4,0},{6,2},{8,12},{10,14},{12,8},{14,10},{16,20},{18,... | collective-permute-start | bytes 442376 | tf_op jit(solution)/shard_map/ppermute | solution.py:24
  9.2 6.4 %collective-permute-start.7 = (f32[4,72,128]{2,1,0:T(8,128)S(1)}, f32[4,72,128]{2,1,0:T(8,128)S(1)}, u32[]{:S(2)}, u32[]{:S(2)}) collective-permute-start(f32[4,72,128]{2,1,0:T(8,128)S(1)} %get-tuple-element.303), channel_id=1, source_target_pairs={{0,2},{2,0},{4,6},{6,4},{8,10},{10,8},{12,14},{14,12},{16,18},{18,... | collective-permute-start | bytes 442376 | tf_op jit(solution)/shard_map/ppermute | solution.py:24
  11.4 4.0 %collective-permute-start.8 = (f32[1,128]{1,0:T(1,128)S(1)}, f32[1,128]{1,0:T(1,128)S(1)}, u32[]{:S(2)}, u32[]{:S(2)}) collective-permute-start(f32[1,128]{1,0:T(1,128)S(1)} %get-tuple-element.305.mine_ref), channel_id=1, source_target_pairs={{0,1},{1,0},{2,3},{3,2},{4,5},{5,4},{6,7},{7,6},{8,9},{9,8},{10,11... | collective-permute-start | bytes 1544 | tf_op jit(solution)/shard_map/ppermute | solution.py:709
  12.8 1.8 %copy-start.8 = (s32[1,4,4]{2,1,0:T(4,128)S(1)}, s32[1,4,4]{2,1,0:T(4,128)}, u32[]{:S(2)}) copy-start(s32[1,4,4]{2,1,0:T(4,128)} %senders_ref.3) | copy-start | bytes 196
  12.8 1.8 %copy-start.9 = (s32[1,16,6]{1,0,2:T(1,128)S(1)}, s32[1,16,6]{1,0,2:T(1,128)}, u32[]{:S(2)}) copy-start(s32[1,16,6]{1,0,2:T(1,128)} %param.15) | copy-start | bytes 1156
  12.8 2.6 %copy-start.6 = (f32[1,48,48]{2,1,0:T(8,128)S(1)}, f32[1,48,48]{2,1,0:T(8,128)}, u32[]{:S(2)}) copy-start(f32[1,48,48]{2,1,0:T(8,128)} %refs_4_.5) | copy-start | bytes 27652
  16.7 7.4 %collective-permute-start.9 = (f32[8,96]{1,0:T(8,128)S(1)}, f32[8,96]{1,0:T(8,128)S(1)}, u32[]{:S(2)}, u32[]{:S(2)}) collective-permute-start(f32[8,96]{1,0:T(8,128)S(1)} %get-tuple-element.314), channel_id=1, source_target_pairs={{0,16},{2,18},{4,20},{6,22},{8,24},{10,26},{12,28},{14,30},{16,0},... | collective-permute-start | bytes 9224 | tf_op jit(solution)/shard_map/ppermute | solution.py:24
  17.1 7.1 %collective-permute-start.10 = (f32[8,96]{1,0:T(8,128)S(1)}, f32[8,96]{1,0:T(8,128)S(1)}, u32[]{:S(2)}, u32[]{:S(2)}) collective-permute-start(f32[8,96]{1,0:T(8,128)S(1)} %get-tuple-element.315), channel_id=1, source_target_pairs={{0,8},{2,10},{4,12},{6,14},{8,0},{10,2},{12,4},{14,6},{16,24},{18,... | collective-permute-start | bytes 9224 | tf_op jit(solution)/shard_map/ppermute | solution.py:24
  18.3 5.8 %collective-permute-start.11 = (f32[8,96]{1,0:T(8,128)S(1)}, f32[8,96]{1,0:T(8,128)S(1)}, u32[]{:S(2)}, u32[]{:S(2)}) collective-permute-start(f32[8,96]{1,0:T(8,128)S(1)} %get-tuple-element.316), channel_id=1, source_target_pairs={{0,4},{2,6},{4,0},{6,2},{8,12},{10,14},{12,8},{14,10},{16,20},{18,... | collective-permute-start | bytes 9224 | tf_op jit(solution)/shard_map/ppermute | solution.py:24
  19.8 4.3 %collective-permute-start.12 = (f32[8,96]{1,0:T(8,128)S(1)}, f32[8,96]{1,0:T(8,128)S(1)}, u32[]{:S(2)}, u32[]{:S(2)}) collective-permute-start(f32[8,96]{1,0:T(8,128)S(1)} %get-tuple-element.317), channel_id=1, source_target_pairs={{0,2},{2,0},{4,6},{6,4},{8,10},{10,8},{12,14},{14,12},{16,18},{18,... | collective-permute-start | bytes 9224 | tf_op jit(solution)/shard_map/ppermute | solution.py:24
  24.8 1.2 %collective-permute-start.13 = (f32[1,128]{1,0:T(1,128)S(1)}, f32[1,128]{1,0:T(1,128)S(1)}, u32[]{:S(2)}, u32[]{:S(2)}) collective-permute-start(f32[1,128]{1,0:T(1,128)S(1)} %get-tuple-element.327.refs_2_), channel_id=1, source_target_pairs={{0,1},{1,0},{2,3},{3,2},{4,5},{5,4},{6,7},{7,6},{8,9},{9,8},{10,11... | collective-permute-start | bytes 1544 | tf_op jit(solution)/shard_map/ppermute | solution.py:709
  26.6 4.6 %collective-permute-start.14 = (f32[8,96]{1,0:T(8,128)S(1)}, f32[8,96]{1,0:T(8,128)S(1)}, u32[]{:S(2)}, u32[]{:S(2)}) collective-permute-start(f32[8,96]{1,0:T(8,128)S(1)} %get-tuple-element.333), channel_id=1, source_target_pairs={{0,16},{2,18},{4,20},{6,22},{8,24},{10,26},{12,28},{14,30},{16,0},... | collective-permute-start | bytes 9224 | tf_op jit(solution)/shard_map/ppermute | solution.py:24
  27.3 3.9 %collective-permute-start.15 = (f32[8,96]{1,0:T(8,128)S(1)}, f32[8,96]{1,0:T(8,128)S(1)}, u32[]{:S(2)}, u32[]{:S(2)}) collective-permute-start(f32[8,96]{1,0:T(8,128)S(1)} %get-tuple-element.334), channel_id=1, source_target_pairs={{0,8},{2,10},{4,12},{6,14},{8,0},{10,2},{12,4},{14,6},{16,24},{18,... | collective-permute-start | bytes 9224 | tf_op jit(solution)/shard_map/ppermute | solution.py:24
  28.4 3.6 %collective-permute-start.16 = (f32[8,96]{1,0:T(8,128)S(1)}, f32[8,96]{1,0:T(8,128)S(1)}, u32[]{:S(2)}, u32[]{:S(2)}) collective-permute-start(f32[8,96]{1,0:T(8,128)S(1)} %get-tuple-element.335), channel_id=1, source_target_pairs={{0,4},{2,6},{4,0},{6,2},{8,12},{10,14},{12,8},{14,10},{16,20},{18,... | collective-permute-start | bytes 9224 | tf_op jit(solution)/shard_map/ppermute | solution.py:24
  29.9 3.6 %collective-permute-start.17 = (f32[8,96]{1,0:T(8,128)S(1)}, f32[8,96]{1,0:T(8,128)S(1)}, u32[]{:S(2)}, u32[]{:S(2)}) collective-permute-start(f32[8,96]{1,0:T(8,128)S(1)} %get-tuple-element.336), channel_id=1, source_target_pairs={{0,2},{2,0},{4,6},{6,4},{8,10},{10,8},{12,14},{14,12},{16,18},{18,... | collective-permute-start | bytes 9224 | tf_op jit(solution)/shard_map/ppermute | solution.py:24
  34.2 1.2 %collective-permute-start.18 = (f32[1,128]{1,0:T(1,128)S(1)}, f32[1,128]{1,0:T(1,128)S(1)}, u32[]{:S(2)}, u32[]{:S(2)}) collective-permute-start(f32[1,128]{1,0:T(1,128)S(1)} %get-tuple-element.340.refs_2_), channel_id=1, source_target_pairs={{0,1},{1,0},{2,3},{3,2},{4,5},{5,4},{6,7},{7,6},{8,9},{9,8},{10,11... | collective-permute-start | bytes 1544 | tf_op jit(solution)/shard_map/ppermute | solution.py:709
  50.8 1.1 %collective-permute-start.19 = (f32[1,128]{1,0:T(1,128)S(1)}, f32[1,128]{1,0:T(1,128)S(1)}, u32[]{:S(2)}, u32[]{:S(2)}) collective-permute-start(f32[1,128]{1,0:T(1,128)S(1)} %totals.1.mine_ref), channel_id=1, source_target_pairs={{0,1},{1,0},{2,3},{3,2},{4,5},{5,4},{6,7},{7,6},{8,9},{9,8},{10,11... | collective-permute-start | bytes 1544 | tf_op jit(solution)/shard_map/ppermute | solution.py:709

commit v7 on v6

--- a/solution.py
+++ b/solution.py
@@ -213,7 +213,7 @@
                 )
         return carry
 
-    lax.fori_loop(0, rows, body, 0, unroll=2)
+    lax.fori_loop(0, rows, body, 0, unroll=True)
 
 
 def spread_block_row(blocks_ref, parts_ref, i, column):

time: 53.2 us -> 53.2 us (level)
  Pallas kernels: 14.5 us -> 13.6 us
    pallas_call x21, Pallas kernels: 14.5 us -> 13.6 us  [call(): pl.pallas_call(kernel, out_shape=[jax.ShapeDtypeStruct(*(out if isinstanc...]
  transfers between devices with their start and end apart: 16 -> 16, of which waited for: 6 -> 6; matrix products, arithmetic and copies ran while one was open for 0% -> 0% of each run, Pallas kernels for 18% -> 16%
where the time goes in v7:
time: 53.2 us; the launch traced here: 53 us
  starting transfers between devices  18 us (34%)
  blocking collectives  14.8 us (28%)
  Pallas kernels  13.6 us (26%)
  waiting for transfers between devices  4.29 us (8%)
  local copies, waits for them, and re-layouts  1.17 us (2%)
  between operations  0.95 us (2%)
    ppermute x12, starting transfers between devices, partner(): lax.ppermute(array, axis, [(i, i ^ 1 << bit) for i in range(lax.axis_size...  17.8 us
    all_to_all x1, blocking collectives, on_device(): lines = lax.all_to_all(payload, 'sub', 0, 0)  14.8 us
    pallas_call x21, Pallas kernels, call(): pl.pallas_call(kernel, out_shape=[jax.ShapeDtypeStruct(*(out if isinstanc...  13.6 us
    ppermute x12, waiting for transfers between devices, partner(): lax.ppermute(array, axis, [(i, i ^ 1 << bit) for i in range(lax.axis_size...  2.83 us
    ppermute x4, waiting for transfers between devices, swap(): return lax.ppermute(array, 'coarse', flip)  1.46 us
    unnamed x18, local copies, waits for them, and re-layouts  1.17 us
  transfers between devices with their start and end apart: 16, of which 6 were waited for; matrix products, arithmetic and copies ran while one was open for 0% of the time, Pallas kernels for 16%

profile of v7, /device:TPU:0, one launch (start us, length us, event | category | flops | bytes accessed | tf_op | source)
XLA Modules:
  0.0 53.0 jit_solution(17820849199179978285)
XLA Ops:
  0.6 1.1 %copy-done = f32[1,16,96,96]{3,2,1,0:T(8,128)S(1)} copy-done((f32[1,16,96,96]{3,2,1,0:T(8,128)S(1)}, f32[1,16,96,96]{3,2,1,0:T(8,128)}, u32[]{:S(2)}) %copy-start) | copy-done | bytes 589848
  1.8 0.0 copy-start.2
  1.8 0.2 pack_margin.1
  2.0 4.1 %collective-permute-start.4 = (f32[4,72,128]{2,1,0:T(8,128)S(1)}, f32[4,72,128]{2,1,0:T(8,128)S(1)}, u32[]{:S(2)}, u32[]{:S(2)}) collective-permute-start(f32[4,72,128]{2,1,0:T(8,128)S(1)} %get-tuple-element.300), channel_id=1, source_target_pairs={{0,16},{2,18},{4,20},{6,22},{8,24},{10,26},{12,28},{14,30},{16,0},... | collective-permute-start | bytes 442376 | tf_op jit(solution)/shard_map/ppermute | solution.py:24
  6.1 1.6 %collective-permute-start.5 = (f32[4,72,128]{2,1,0:T(8,128)S(1)}, f32[4,72,128]{2,1,0:T(8,128)S(1)}, u32[]{:S(2)}, u32[]{:S(2)}) collective-permute-start(f32[4,72,128]{2,1,0:T(8,128)S(1)} %get-tuple-element.301), channel_id=1, source_target_pairs={{0,8},{2,10},{4,12},{6,14},{8,0},{10,2},{12,4},{14,6},{16,24},{18,... | collective-permute-start | bytes 442376 | tf_op jit(solution)/shard_map/ppermute | solution.py:24
  7.7 1.5 %collective-permute-start.6 = (f32[4,72,128]{2,1,0:T(8,128)S(1)}, f32[4,72,128]{2,1,0:T(8,128)S(1)}, u32[]{:S(2)}, u32[]{:S(2)}) collective-permute-start(f32[4,72,128]{2,1,0:T(8,128)S(1)} %get-tuple-element.302), channel_id=1, source_target_pairs={{0,4},{2,6},{4,0},{6,2},{8,12},{10,14},{12,8},{14,10},{16,20},{18,... | collective-permute-start | bytes 442376 | tf_op jit(solution)/shard_map/ppermute | solution.py:24
  9.2 1.5 %collective-permute-start.7 = (f32[4,72,128]{2,1,0:T(8,128)S(1)}, f32[4,72,128]{2,1,0:T(8,128)S(1)}, u32[]{:S(2)}, u32[]{:S(2)}) collective-permute-start(f32[4,72,128]{2,1,0:T(8,128)S(1)} %get-tuple-element.303), channel_id=1, source_target_pairs={{0,2},{2,0},{4,6},{6,4},{8,10},{10,8},{12,14},{14,12},{16,18},{18,... | collective-permute-start | bytes 442376 | tf_op jit(solution)/shard_map/ppermute | solution.py:24
  10.7 0.6 %restrict.1 = (s32[16,128]{1,0:T(8,128)S(1)}, s32[96,128]{1,0:T(8,128)S(1)}, f32[1,128]{1,0:T(1,128)S(1)}) custom-call(f32[1,16,96]{2,1,0:T(8,128)S(1)} %copy-done.5, f32[1,6,16,96]{3,2,1,0:T(8,128)S(1)} %bitcast.141, s32[1,16]{1,0:T(1,128)S(1)} %copy-done.10), custom_call_target="tpu_custom_call" | custom-call | bytes 100000 | tf_op jit(solution)/shard_map/restrict/pallas_call | solution.py:28
  11.4 0.1 collective-permute-start.8
  11.4 0.3 local_rows.1.row_ref
  11.7 1.0 %load_blocks.1.blocks_ref.refs_7_.refs_4_ = f32[1,16,6,96,96]{4,3,2,1,0:T(8,128)S(1)} custom-call(f32[1,16,6,96,96]{4,3,2,1,0:T(8,128)S(1)} %copy-done.2), custom_call_target="tpu_custom_call" | custom-call | bytes 8000000 | tf_op jit(solution)/shard_map/load_blocks/pallas_call | solution.py:28
  12.8 0.0 copy-start.8
  12.8 0.0 copy-start.9
  12.8 1.4 %spread_modes.2.refs_8_ = f32[3,96,96]{2,1,0:T(8,128)S(1)} custom-call(f32[1,16,6,96,96]{4,3,2,1,0:T(8,128)S(1)} %load_blocks.1.blocks_ref.refs_7_.refs_4_, f32[1,6,16,96]{3,2,1,0:T(8,128)S(1)} %bitcast.142), custom_call_target="tpu_custom_call" | custom-call | bytes 100000 | tf_op jit(solution)/shard_map/spread_modes/pallas_call | solution.py:28
  14.2 0.8 %tables.1 = (bf16[96,96]{1,0:T(8,128)(2,1)S(1)}, bf16[16,48]{1,0:T(8,128)(2,1)S(1)}, bf16[16,48]{1,0:T(8,128)(2,1)S(1)}, s32[2,128]{1,0:T(2,128)S(1)}) custom-call(s32[6,1,16]{2,1,0:T(1,128)S(1)} %bitcast.165, s32[1,4,4]{2,1,0:T(4,128)S(1)} %copy-done.8), custom_call_target="tpu_custom_call" | custom-call | bytes 100000 | tf_op jit(solution)/shard_map/tables/pallas_call | solution.py:28
  15.0 0.2 first_base.1
  15.2 1.0 %first_spread.1 = (f32[16,96]{1,0:T(8,128)S(1)}, f32[16,96]{1,0:T(8,128)S(1)}, f32[8,96]{1,0:T(8,128)S(1)}, f32[8,96]{1,0:T(8,128)S(1)}, f32[8,96]{1,0:T(8,128)S(1)}, /*index=5*/f32[8,96]{1,0:T(8,128)S(1)}) custom-call(f32[4,72,128]{2,1,0:T(8,128)S(1)} %collective-permute-done.4.refs_0_.refs_3_, f32[4,72,128]{2,1,0:T(8,128)S(1)} %collective-permute-done.5.refs_1_.refs_2_, ...), custom_call_target="tpu_custom_call" | custom-call | bytes 100000 | tf_op jit(solution)/shard_map/first_spread/pallas_call | solution.py:28
  16.2 0.4 collective-permute-start.9
  16.6 1.7 %collective-permute-start.10 = (f32[8,96]{1,0:T(8,128)S(1)}, f32[8,96]{1,0:T(8,128)S(1)}, u32[]{:S(2)}, u32[]{:S(2)}) collective-permute-start(f32[8,96]{1,0:T(8,128)S(1)} %get-tuple-element.315), channel_id=1, source_target_pairs={{0,8},{2,10},{4,12},{6,14},{8,0},{10,2},{12,4},{14,6},{16,24},{18,... | collective-permute-start | bytes 9224 | tf_op jit(solution)/shard_map/ppermute | solution.py:24
  18.3 1.5 %collective-permute-start.11 = (f32[8,96]{1,0:T(8,128)S(1)}, f32[8,96]{1,0:T(8,128)S(1)}, u32[]{:S(2)}, u32[]{:S(2)}) collective-permute-start(f32[8,96]{1,0:T(8,128)S(1)} %get-tuple-element.316), channel_id=1, source_target_pairs={{0,4},{2,6},{4,0},{6,2},{8,12},{10,14},{12,8},{14,10},{16,20},{18,... | collective-permute-start | bytes 9224 | tf_op jit(solution)/shard_map/ppermute | solution.py:24
  19.8 1.5 %collective-permute-start.12 = (f32[8,96]{1,0:T(8,128)S(1)}, f32[8,96]{1,0:T(8,128)S(1)}, u32[]{:S(2)}, u32[]{:S(2)}) collective-permute-start(f32[8,96]{1,0:T(8,128)S(1)} %get-tuple-element.317), channel_id=1, source_target_pairs={{0,2},{2,0},{4,6},{6,4},{8,10},{10,8},{12,14},{14,12},{16,18},{18,... | collective-permute-start | bytes 9224 | tf_op jit(solution)/shard_map/ppermute | solution.py:24
  21.3 1.4 %spread_modes.3.refs_9_ = f32[3,96,96]{2,1,0:T(8,128)S(1)} custom-call(f32[1,16,6,96,96]{4,3,2,1,0:T(8,128)S(1)} %load_blocks.1.blocks_ref.refs_7_.refs_4_, f32[1,6,16,96]{3,2,1,0:T(8,128)S(1)} %bitcast.144), custom_call_target="tpu_custom_call" | custom-call | bytes 100000 | tf_op jit(solution)/shard_map/spread_modes/pallas_call | solution.py:28
  22.7 1.0 %combine.1.inverse_ref = f32[16,96,96]{2,1,0:T(8,128)S(1)} custom-call(f32[1,16,96,96]{3,2,1,0:T(8,128)S(1)} %copy-done.1, s32[1,4,4]{2,1,0:T(4,128)S(1)} %copy-done.8, f32[4,72,128]{2,1,0:T(8,128)S(1)} %collective-permute-done.7.refs_3_.refs_0_, f32[4,72,128]{2,1,0:T(8,128)S(1)} %collective-permute-done.6.refs_2_.refs_1_, ...), custom_call_target="tpu_custom_call" | custom-call | bytes 100000 | tf_op jit(solution)/shard_map/combine/pallas_call | solution.py:28
  23.7 0.7 %apply.2 = (f32[16,96]{1,0:T(8,128)S(1)}, f32[1,128]{1,0:T(1,128)S(1)}) custom-call(f32[1,16,96]{2,1,0:T(8,128)S(1)} %copy-done.5, f32[16,96]{1,0:T(8,128)S(1)} %get-tuple-element.312.z_ref.refs_3_, f32[16,96]{1,0:T(8,128)S(1)} %get-tuple-element.313.own_ref, f32[8,96]{1,0:T(8,128)S(1)} %collective-permute-done.9.refs_0_, ...), custom_call_target="tpu_custom_call" | custom-call | bytes 100000 | tf_op jit(solution)/shard_map/apply/pallas_call | solution.py:28
  24.4 0.1 collective-permute-start.13
  24.5 0.6 %local_inverse.2 = (f32[16,96]{1,0:T(8,128)S(1)}, f32[96,96]{1,0:T(8,128)S(1)}) custom-call(f32[16,96]{1,0:T(8,128)S(1)} %get-tuple-element.323.field_ref.refs_1_.refs_13_, f32[16,96,96]{2,1,0:T(8,128)S(1)} %combine.1.inverse_ref, f32[1,16,6,96,96]{4,3,2,1,0:T(8,128)S(1)} %load_blocks.1.blocks_ref.refs_7_.refs_4_), custom_call_target="tpu_custom_call" | custom-call | bytes 100000 | tf_op jit(solution)/shard_map/local_inverse/pallas_call | solution.py:28
  25.1 0.5 collective-permute-done.13.refs_3_
  25.6 0.6 %spread.1 = (f32[16,96]{1,0:T(8,128)S(1)}, f32[16,96]{1,0:T(8,128)S(1)}, f32[8,96]{1,0:T(8,128)S(1)}, f32[8,96]{1,0:T(8,128)S(1)}, f32[8,96]{1,0:T(8,128)S(1)}, /*index=5*/f32[8,96]{1,0:T(8,128)S(1)}) custom-call(f32[96,96]{1,0:T(8,128)S(1)} %get-tuple-element.325.refs_0_, f32[16,96]{1,0:T(8,128)S(1)} %get-tuple-element.326.refs_1_, ...), custom_call_target="tpu_custom_call" | custom-call | bytes 100000 | tf_op jit(solution)/shard_map/spread/pallas_call | solution.py:28
  26.2 0.7 %collective-permute-start.14 = (f32[8,96]{1,0:T(8,128)S(1)}, f32[8,96]{1,0:T(8,128)S(1)}, u32[]{:S(2)}, u32[]{:S(2)}) collective-permute-start(f32[8,96]{1,0:T(8,128)S(1)} %get-tuple-element.333), channel_id=1, source_target_pairs={{0,16},{2,18},{4,20},{6,22},{8,24},{10,26},{12,28},{14,30},{16,0},... | collective-permute-start | bytes 9224 | tf_op jit(solution)/shard_map/ppermute | solution.py:24
  26.9 1.0 %collective-permute-start.15 = (f32[8,96]{1,0:T(8,128)S(1)}, f32[8,96]{1,0:T(8,128)S(1)}, u32[]{:S(2)}, u32[]{:S(2)}) collective-permute-start(f32[8,96]{1,0:T(8,128)S(1)} %get-tuple-element.334), channel_id=1, source_target_pairs={{0,8},{2,10},{4,12},{6,14},{8,0},{10,2},{12,4},{14,6},{16,24},{18,... | collective-permute-start | bytes 9224 | tf_op jit(solution)/shard_map/ppermute | solution.py:24
  27.9 1.5 %collective-permute-start.16 = (f32[8,96]{1,0:T(8,128)S(1)}, f32[8,96]{1,0:T(8,128)S(1)}, u32[]{:S(2)}, u32[]{:S(2)}) collective-permute-start(f32[8,96]{1,0:T(8,128)S(1)} %get-tuple-element.335), channel_id=1, source_target_pairs={{0,4},{2,6},{4,0},{6,2},{8,12},{10,14},{12,8},{14,10},{16,20},{18,... | collective-permute-start | bytes 9224 | tf_op jit(solution)/shard_map/ppermute | solution.py:24
  29.4 0.8 %collective-permute-start.17 = (f32[8,96]{1,0:T(8,128)S(1)}, f32[8,96]{1,0:T(8,128)S(1)}, u32[]{:S(2)}, u32[]{:S(2)}) collective-permute-start(f32[8,96]{1,0:T(8,128)S(1)} %get-tuple-element.336), channel_id=1, source_target_pairs={{0,2},{2,0},{4,6},{6,4},{8,10},{10,8},{12,14},{14,12},{16,18},{18,... | collective-permute-start | bytes 9224 | tf_op jit(solution)/shard_map/ppermute | solution.py:24
  30.2 0.5 %collective-permute-done.14.refs_0_ = f32[8,96]{1,0:T(8,128)S(1)} collective-permute-done((f32[8,96]{1,0:T(8,128)S(1)}, f32[8,96]{1,0:T(8,128)S(1)}, u32[]{:S(2)}, u32[]{:S(2)}) %collective-permute-start.14) | collective-permute-done | bytes 3104 | tf_op jit(solution)/shard_map/ppermute | solution.py:24
  30.8 0.7 %collective-permute-done.16.refs_2_ = f32[8,96]{1,0:T(8,128)S(1)} collective-permute-done((f32[8,96]{1,0:T(8,128)S(1)}, f32[8,96]{1,0:T(8,128)S(1)}, u32[]{:S(2)}, u32[]{:S(2)}) %collective-permute-start.16) | collective-permute-done | bytes 3104 | tf_op jit(solution)/shard_map/ppermute | solution.py:24
  31.5 1.5 %collective-permute-done.17.refs_3_ = f32[8,96]{1,0:T(8,128)S(1)} collective-permute-done((f32[8,96]{1,0:T(8,128)S(1)}, f32[8,96]{1,0:T(8,128)S(1)}, u32[]{:S(2)}, u32[]{:S(2)}) %collective-permute-start.17) | collective-permute-done | bytes 3104 | tf_op jit(solution)/shard_map/ppermute | solution.py:24
  33.0 0.7 %apply.3 = (f32[16,96]{1,0:T(8,128)S(1)}, f32[1,128]{1,0:T(1,128)S(1)}) custom-call(f32[16,96]{1,0:T(8,128)S(1)} %get-tuple-element.323.field_ref.refs_1_.refs_13_, f32[16,96]{1,0:T(8,128)S(1)} %get-tuple-element.331.z_ref.refs_4_, f32[16,96]{1,0:T(8,128)S(1)} %get-tuple-element.332.own_ref, f32[8,96]{1,0:T(8,128)S(1)} %collective-permute-done.14.refs_0_, ...), custom_call_target="tpu_custom_call" | custom-call | bytes 100000 | tf_op jit(solution)/shard_map/apply/pallas_call | solution.py:28
  33.7 0.1 collective-permute-start.18
  33.8 0.1 early_dots.1.refs_11_
  33.9 0.6 %local_inverse.3 = (f32[16,96]{1,0:T(8,128)S(1)}, f32[96,96]{1,0:T(8,128)S(1)}) custom-call(f32[16,96]{1,0:T(8,128)S(1)} %get-tuple-element.337.field_ref.refs_2_.refs_14_, f32[16,96,96]{2,1,0:T(8,128)S(1)} %combine.1.inverse_ref, f32[1,16,6,96,96]{4,3,2,1,0:T(8,128)S(1)} %load_blocks.1.blocks_ref.refs_7_.refs_4_), custom_call_target="tpu_custom_call" | custom-call | bytes 100000 | tf_op jit(solution)/shard_map/local_inverse/pallas_call | solution.py:28
  34.5 0.4 collective-permute-done.18.refs_3_
  34.9 0.9 %last_spread.1 = (f32[16,96]{1,0:T(8,128)S(1)}, f32[16,96]{1,0:T(8,128)S(1)}, f32[16,32,128]{2,1,0:T(8,128)S(1)}) custom-call(f32[96,96]{1,0:T(8,128)S(1)} %get-tuple-element.338.refs_0_, f32[16,96]{1,0:T(8,128)S(1)} %get-tuple-element.339.refs_1_, f32[1,128]{1,0:T(1,128)S(1)} %get-tuple-element.340.refs_2_, f32[1,128]{1,0:T(1,128)S(1)} %collective-permute-done.18.refs_3_, ...), custom_call_target="tpu_custom_call" | custom-call | bytes 100000 | tf_op jit(solution)/shard_map/last_spread/pallas_call | solution.py:28
  35.8 14.8 %all_to_all.5.lines_ref = f32[16,32,128]{2,1,0:T(8,128)S(1)} all-to-all(f32[16,32,128]{2,1,0:T(8,128)S(1)} %get-tuple-element.341), channel_id=1, replica_groups=mesh['sub'=16,'coarse'=2] {'sub'}, dimensions={0} | all-to-all | bytes 524288 | tf_op jit(solution)/shard_map/all_to_all | solution.py:847
  50.6 0.2 totals.1.mine_ref
  50.8 0.6 %last_apply.1 = f32[16,96]{1,0:T(8,128)S(1)} custom-call(f32[16,96]{1,0:T(8,128)S(1)} %get-tuple-element.337.field_ref.refs_2_.refs_14_, f32[16,96]{1,0:T(8,128)S(1)} %get-tuple-element.342.z_ref, f32[16,96]{1,0:T(8,128)S(1)} %get-tuple-element.343.own_ref, f32[16,32,128]{2,1,0:T(8,128)S(1)} %all_to_all.5.lines_ref, ...), custom_call_target="tpu_custom_call" | custom-call | bytes 100000 | tf_op jit(solution)/shard_map/last_apply/pallas_call | solution.py:28
  51.4 0.5 collective-permute-done.19.theirs_ref
  51.9 0.1 decide.1
  52.1 1.0 %conditional.1 = ((f32[1,16,96]{2,1,0:T(8,128)}, f32[1,16,96]{2,1,0:T(8,128)})) conditional(s32[]{:T(128)} %bitcast.10, (f32[1,128]{1,0:T(1,128)S(1)}, f32[1,16,96]{2,1,0:T(8,128)S(1)}, f32[1,16,6,96]{3,1,2,0:T(8,128)S(1)}, s32[1,16]{1,0:T(1,128)S(1)}, f32[1,48,48]{2,1,0:T(8,128)S(1)}, /*index=5*/f32[16,96,96]{2,1,0:T(8,128)S(1)}, ...), branch_computations={%region_0.8_spmd, %region_8.9_spmd} | conditional | flops 32029620 | bytes 16889252 | solution.py:899
  52.3 0.8 %finish.1 = (f32[1,16,96]{2,1,0:T(8,128)}, f32[1,16,96]{2,1,0:T(8,128)}) custom-call(f32[1,128]{1,0:T(1,128)S(1)} %get-tuple-element.245.mine_ref, f32[1,128]{1,0:T(1,128)S(1)} %get-tuple-element.246.theirs_ref, f32[1,16,96]{2,1,0:T(8,128)S(1)} %get-tuple-element.247.refs_0_, f32[16,96]{1,0:T(8,128)S(1)} %get-tuple-element.248.refs_1_, ...), custom_call_target="tpu_custom_call" | custom-call | bytes 100000 | tf_op jit(solution)/shard_map/cond/branch_1_fun/finish/pallas_call | solution.py:28
  (25 shorter events, 0.1 us)
Async XLA Ops:
  0.6 1.1 %copy-start = (f32[1,16,96,96]{3,2,1,0:T(8,128)S(1)}, f32[1,16,96,96]{3,2,1,0:T(8,128)}, u32[]{:S(2)}) copy-start(f32[1,16,96,96]{3,2,1,0:T(8,128)} %refs_15_.1) | copy-start | bytes 1769476
  1.8 8.9 %copy-start.3 = (f32[1,16,6,96]{3,1,2,0:T(8,128)S(1)}, f32[1,16,6,96]{3,1,2,0:T(8,128)}, u32[]{:S(2)}) copy-start(f32[1,16,6,96]{3,1,2,0:T(8,128)} %param.19) | copy-start | bytes 110596
  1.8 8.9 %copy-start.5 = (f32[1,16,96]{2,1,0:T(8,128)S(1)}, f32[1,16,96]{2,1,0:T(8,128)}, u32[]{:S(2)}) copy-start(f32[1,16,96]{2,1,0:T(8,128)} %refs_12_.3) | copy-start | bytes 18436
  1.8 8.9 %copy-start.10 = (s32[1,16]{1,0:T(1,128)S(1)}, s32[1,16]{1,0:T(1,128)}, u32[]{:S(2)}) copy-start(s32[1,16]{1,0:T(1,128)} %aggregate_ref.1) | copy-start | bytes 196
  1.8 9.7 %copy-start.1 = (f32[1,16,96,96]{3,2,1,0:T(8,128)S(1)}, f32[1,16,96,96]{3,2,1,0:T(8,128)}, u32[]{:S(2)}) copy-start(f32[1,16,96,96]{3,2,1,0:T(8,128)} %inverse_ref.3) | copy-start | bytes 1769476
  1.8 10.0 %copy-start.2 = (f32[1,16,6,96,96]{4,3,2,1,0:T(8,128)S(1)}, f32[1,16,6,96,96]{4,3,2,1,0:T(8,128)}, u32[]{:S(2)}) copy-start(f32[1,16,6,96,96]{4,3,2,1,0:T(8,128)} %source_ref.1) | copy-start | bytes 10616836
  2.0 13.1 %collective-permute-start.4 = (f32[4,72,128]{2,1,0:T(8,128)S(1)}, f32[4,72,128]{2,1,0:T(8,128)S(1)}, u32[]{:S(2)}, u32[]{:S(2)}) collective-permute-start(f32[4,72,128]{2,1,0:T(8,128)S(1)} %get-tuple-element.300), channel_id=1, source_target_pairs={{0,16},{2,18},{4,20},{6,22},{8,24},{10,26},{12,28},{14,30},{16,0},... | collective-permute-start | bytes 442376 | tf_op jit(solution)/shard_map/ppermute | solution.py:24
  6.1 9.1 %collective-permute-start.5 = (f32[4,72,128]{2,1,0:T(8,128)S(1)}, f32[4,72,128]{2,1,0:T(8,128)S(1)}, u32[]{:S(2)}, u32[]{:S(2)}) collective-permute-start(f32[4,72,128]{2,1,0:T(8,128)S(1)} %get-tuple-element.301), channel_id=1, source_target_pairs={{0,8},{2,10},{4,12},{6,14},{8,0},{10,2},{12,4},{14,6},{16,24},{18,... | collective-permute-start | bytes 442376 | tf_op jit(solution)/shard_map/ppermute | solution.py:24
  7.7 7.5 %collective-permute-start.6 = (f32[4,72,128]{2,1,0:T(8,128)S(1)}, f32[4,72,128]{2,1,0:T(8,128)S(1)}, u32[]{:S(2)}, u32[]{:S(2)}) collective-permute-start(f32[4,72,128]{2,1,0:T(8,128)S(1)} %get-tuple-element.302), channel_id=1, source_target_pairs={{0,4},{2,6},{4,0},{6,2},{8,12},{10,14},{12,8},{14,10},{16,20},{18,... | collective-permute-start | bytes 442376 | tf_op jit(solution)/shard_map/ppermute | solution.py:24
  9.2 6.0 %collective-permute-start.7 = (f32[4,72,128]{2,1,0:T(8,128)S(1)}, f32[4,72,128]{2,1,0:T(8,128)S(1)}, u32[]{:S(2)}, u32[]{:S(2)}) collective-permute-start(f32[4,72,128]{2,1,0:T(8,128)S(1)} %get-tuple-element.303), channel_id=1, source_target_pairs={{0,2},{2,0},{4,6},{6,4},{8,10},{10,8},{12,14},{14,12},{16,18},{18,... | collective-permute-start | bytes 442376 | tf_op jit(solution)/shard_map/ppermute | solution.py:24
  11.4 3.6 %collective-permute-start.8 = (f32[1,128]{1,0:T(1,128)S(1)}, f32[1,128]{1,0:T(1,128)S(1)}, u32[]{:S(2)}, u32[]{:S(2)}) collective-permute-start(f32[1,128]{1,0:T(1,128)S(1)} %get-tuple-element.305.mine_ref), channel_id=1, source_target_pairs={{0,1},{1,0},{2,3},{3,2},{4,5},{5,4},{6,7},{7,6},{8,9},{9,8},{10,11... | collective-permute-start | bytes 1544 | tf_op jit(solution)/shard_map/ppermute | solution.py:709
  12.8 1.4 %copy-start.8 = (s32[1,4,4]{2,1,0:T(4,128)S(1)}, s32[1,4,4]{2,1,0:T(4,128)}, u32[]{:S(2)}) copy-start(s32[1,4,4]{2,1,0:T(4,128)} %senders_ref.3) | copy-start | bytes 196
  12.8 1.4 %copy-start.9 = (s32[1,16,6]{1,0,2:T(1,128)S(1)}, s32[1,16,6]{1,0,2:T(1,128)}, u32[]{:S(2)}) copy-start(s32[1,16,6]{1,0,2:T(1,128)} %param.15) | copy-start | bytes 1156
  12.8 2.2 %copy-start.6 = (f32[1,48,48]{2,1,0:T(8,128)S(1)}, f32[1,48,48]{2,1,0:T(8,128)}, u32[]{:S(2)}) copy-start(f32[1,48,48]{2,1,0:T(8,128)} %refs_4_.5) | copy-start | bytes 27652
  16.2 7.4 %collective-permute-start.9 = (f32[8,96]{1,0:T(8,128)S(1)}, f32[8,96]{1,0:T(8,128)S(1)}, u32[]{:S(2)}, u32[]{:S(2)}) collective-permute-start(f32[8,96]{1,0:T(8,128)S(1)} %get-tuple-element.314), channel_id=1, source_target_pairs={{0,16},{2,18},{4,20},{6,22},{8,24},{10,26},{12,28},{14,30},{16,0},... | collective-permute-start | bytes 9224 | tf_op jit(solution)/shard_map/ppermute | solution.py:24
  16.6 7.1 %collective-permute-start.10 = (f32[8,96]{1,0:T(8,128)S(1)}, f32[8,96]{1,0:T(8,128)S(1)}, u32[]{:S(2)}, u32[]{:S(2)}) collective-permute-start(f32[8,96]{1,0:T(8,128)S(1)} %get-tuple-element.315), channel_id=1, source_target_pairs={{0,8},{2,10},{4,12},{6,14},{8,0},{10,2},{12,4},{14,6},{16,24},{18,... | collective-permute-start | bytes 9224 | tf_op jit(solution)/shard_map/ppermute | solution.py:24
  18.3 5.4 %collective-permute-start.11 = (f32[8,96]{1,0:T(8,128)S(1)}, f32[8,96]{1,0:T(8,128)S(1)}, u32[]{:S(2)}, u32[]{:S(2)}) collective-permute-start(f32[8,96]{1,0:T(8,128)S(1)} %get-tuple-element.316), channel_id=1, source_target_pairs={{0,4},{2,6},{4,0},{6,2},{8,12},{10,14},{12,8},{14,10},{16,20},{18,... | collective-permute-start | bytes 9224 | tf_op jit(solution)/shard_map/ppermute | solution.py:24
  19.8 3.9 %collective-permute-start.12 = (f32[8,96]{1,0:T(8,128)S(1)}, f32[8,96]{1,0:T(8,128)S(1)}, u32[]{:S(2)}, u32[]{:S(2)}) collective-permute-start(f32[8,96]{1,0:T(8,128)S(1)} %get-tuple-element.317), channel_id=1, source_target_pairs={{0,2},{2,0},{4,6},{6,4},{8,10},{10,8},{12,14},{14,12},{16,18},{18,... | collective-permute-start | bytes 9224 | tf_op jit(solution)/shard_map/ppermute | solution.py:24
  24.4 1.2 %collective-permute-start.13 = (f32[1,128]{1,0:T(1,128)S(1)}, f32[1,128]{1,0:T(1,128)S(1)}, u32[]{:S(2)}, u32[]{:S(2)}) collective-permute-start(f32[1,128]{1,0:T(1,128)S(1)} %get-tuple-element.327.refs_2_), channel_id=1, source_target_pairs={{0,1},{1,0},{2,3},{3,2},{4,5},{5,4},{6,7},{7,6},{8,9},{9,8},{10,11... | collective-permute-start | bytes 1544 | tf_op jit(solution)/shard_map/ppermute | solution.py:709
  26.2 4.6 %collective-permute-start.14 = (f32[8,96]{1,0:T(8,128)S(1)}, f32[8,96]{1,0:T(8,128)S(1)}, u32[]{:S(2)}, u32[]{:S(2)}) collective-permute-start(f32[8,96]{1,0:T(8,128)S(1)} %get-tuple-element.333), channel_id=1, source_target_pairs={{0,16},{2,18},{4,20},{6,22},{8,24},{10,26},{12,28},{14,30},{16,0},... | collective-permute-start | bytes 9224 | tf_op jit(solution)/shard_map/ppermute | solution.py:24
  26.9 3.9 %collective-permute-start.15 = (f32[8,96]{1,0:T(8,128)S(1)}, f32[8,96]{1,0:T(8,128)S(1)}, u32[]{:S(2)}, u32[]{:S(2)}) collective-permute-start(f32[8,96]{1,0:T(8,128)S(1)} %get-tuple-element.334), channel_id=1, source_target_pairs={{0,8},{2,10},{4,12},{6,14},{8,0},{10,2},{12,4},{14,6},{16,24},{18,... | collective-permute-start | bytes 9224 | tf_op jit(solution)/shard_map/ppermute | solution.py:24
  27.9 3.6 %collective-permute-start.16 = (f32[8,96]{1,0:T(8,128)S(1)}, f32[8,96]{1,0:T(8,128)S(1)}, u32[]{:S(2)}, u32[]{:S(2)}) collective-permute-start(f32[8,96]{1,0:T(8,128)S(1)} %get-tuple-element.335), channel_id=1, source_target_pairs={{0,4},{2,6},{4,0},{6,2},{8,12},{10,14},{12,8},{14,10},{16,20},{18,... | collective-permute-start | bytes 9224 | tf_op jit(solution)/shard_map/ppermute | solution.py:24
  29.4 3.6 %collective-permute-start.17 = (f32[8,96]{1,0:T(8,128)S(1)}, f32[8,96]{1,0:T(8,128)S(1)}, u32[]{:S(2)}, u32[]{:S(2)}) collective-permute-start(f32[8,96]{1,0:T(8,128)S(1)} %get-tuple-element.336), channel_id=1, source_target_pairs={{0,2},{2,0},{4,6},{6,4},{8,10},{10,8},{12,14},{14,12},{16,18},{18,... | collective-permute-start | bytes 9224 | tf_op jit(solution)/shard_map/ppermute | solution.py:24
  33.7 1.2 %collective-permute-start.18 = (f32[1,128]{1,0:T(1,128)S(1)}, f32[1,128]{1,0:T(1,128)S(1)}, u32[]{:S(2)}, u32[]{:S(2)}) collective-permute-start(f32[1,128]{1,0:T(1,128)S(1)} %get-tuple-element.340.refs_2_), channel_id=1, source_target_pairs={{0,1},{1,0},{2,3},{3,2},{4,5},{5,4},{6,7},{7,6},{8,9},{9,8},{10,11... | collective-permute-start | bytes 1544 | tf_op jit(solution)/shard_map/ppermute | solution.py:709
  50.8 1.1 %collective-permute-start.19 = (f32[1,128]{1,0:T(1,128)S(1)}, f32[1,128]{1,0:T(1,128)S(1)}, u32[]{:S(2)}, u32[]{:S(2)}) collective-permute-start(f32[1,128]{1,0:T(1,128)S(1)} %totals.1.mine_ref), channel_id=1, source_target_pairs={{0,1},{1,0},{2,3},{3,2},{4,5},{5,4},{6,7},{7,6},{8,9},{9,8},{10,11... | collective-permute-start | bytes 1544 | tf_op jit(solution)/shard_map/ppermute | solution.py:709
